TPU v7x, 128 devices: a whole 4x4x4 slice. The times are simulated.
128 devices in a mesh: ctx: 32 (over y, x, core), head: 4 (over z).
Axes of the slice: x: 4, y: 4, z: 4, core: 2. Of those that a mesh axis runs over, the one named last changes fastest.
Arguments:
- attn_query: bfloat16 [16384, 32, 128], P('ctx', 'head'), may hold values from -6 to 6
- attn_key: bfloat16 [16384, 8, 128], P('ctx', 'head'), may hold values from -6 to 6
- attention_value: bfloat16 [16384, 8, 128], P('ctx', 'head'), may hold values from -6 to 6
- delta_query: bfloat16 [16384, 32, 128], P('ctx', 'head'), may hold values from -6 to 6
- delta_key: bfloat16 [16384, 32, 128], P('ctx', 'head'), may hold values from -6 to 6
- delta_value: bfloat16 [16384, 32, 128], P('ctx', 'head'), may hold values from -6 to 6
- log_decay: float32 [32, 16384], P('head', 'ctx'), may hold values from -0.8 to 0, as said below
- beta_gate: float32 [32, 16384], P('head', 'ctx'), may hold values from 0.1 to 0.9
Outputs:
- attn_out: bfloat16 [16384, 4096], P(('ctx', 'head'))
- delta_out: bfloat16 [16384, 4096], P(('ctx', 'head'))
Inputs may be any that keep to these rules, and one draw needn't show every extreme that they name: `log_decay`: each entry is the natural logarithm of a decay factor of one head at one token.
All inputs are finite; a program needn't handle non-finite values.
Results may differ from a plain program's by a relative error of at most 0.0045.
Values may be sent and summed in bfloat16 or wider, within the bound.
No kernel may reach another device: no remote copies, remote signals or barrier semaphores. Data moves between devices by JAX's collectives and lax.ppermute only.
A program may use at most 128 MiB of HBM per device.

v0:
```python
import math

import jax
import jax.numpy as jnp
from jax import lax
from jax.sharding import PartitionSpec as P

WINDOW = 1024
SPAN = 64


norm_epsilon = 1e-06


def shifted(block, axis, distance):
    devices = range(lax.axis_size(axis))
    route = [(i - distance, i) for i in devices if i - distance in devices]
    return lax.ppermute(block, axis, route)


def product(form, left, right):
    return jnp.einsum(form, left, right, precision=lax.Precision.HIGHEST)


def normalize(tensor, scale_factor):
    widened = tensor.astype(jnp.float32)
    return (
        widened
        / jnp.sqrt(jnp.sum(widened * widened, axis=-1, keepdims=True) + norm_epsilon)
        * scale_factor
    )


def invert_unit(strict):
    span_len = strict.shape[-1]
    identity = jnp.eye(span_len, dtype=strict.dtype)
    inverse = identity - strict
    power_term = strict
    for level in range(1, max(1, (span_len - 1).bit_length())):
        power_term = product("hij,hjk->hik", power_term, power_term)
        inverse = inverse + product("hij,hjk->hik", inverse, power_term)
    return inverse


def prepare(query_unit, key_unit, beta_rows, log_rows):
    span_len = log_rows.shape[1]
    cumulative = jnp.cumsum(log_rows, axis=1)
    row_index = jnp.arange(span_len, dtype=jnp.int32)[:, None]
    col_index = jnp.arange(span_len, dtype=jnp.int32)[None, :]
    log_gap = cumulative[:, :, None] - cumulative[:, None, :]
    decay_ratio = jnp.exp(jnp.where(row_index >= col_index, log_gap, -jnp.inf))
    key_inner = product("hcd,hed->hce", key_unit, key_unit)
    strict = jnp.where(row_index > col_index, beta_rows[:, :, None] * decay_ratio * key_inner, 0.0)
    causal = product("hcd,hed->hce", query_unit, key_unit) * decay_ratio
    return (cumulative, invert_unit(strict), causal)


def advance(carried, query_unit, key_unit, value_rows, beta_rows, prepared):
    cumulative, inverse, causal = prepared
    leading = jnp.exp(cumulative)
    projected = product("hcd,hvd->hcv", key_unit, carried)
    right_side = beta_rows[:, :, None] * (value_rows - leading[:, :, None] * projected)
    weighted = product("hce,hev->hcv", inverse, right_side)
    result = leading[:, :, None] * product("hcd,hvd->hcv", query_unit, carried) + product(
        "hts,hsv->htv", causal, weighted
    )
    trailing = jnp.exp(cumulative[:, -1:] - cumulative)
    updated = jnp.exp(cumulative[:, -1])[:, None, None] * carried + product(
        "hsv,hsd->hvd", trailing[:, :, None] * weighted, key_unit
    )
    return (updated, result)


def to_spans(tensor, span_len):
    return tensor.reshape(
        tensor.shape[0] // span_len, span_len, tensor.shape[1], tensor.shape[2]
    ).transpose(0, 2, 1, 3)


def gate_spans(tensor, span_len):
    return tensor.reshape(tensor.shape[0], tensor.shape[1] // span_len, span_len).transpose(1, 0, 2)


def from_spans(tensor):
    return tensor.transpose(0, 2, 1, 3).reshape(
        tensor.shape[0] * tensor.shape[2], tensor.shape[1] * tensor.shape[3]
    )


def attend(query_tile_block, key_block, value_block, block_start, group_count):
    rows = query_tile_block.shape[0]
    head_dim = query_tile_block.shape[2]
    grouped = query_tile_block.reshape(rows, key_block.shape[1], group_count, head_dim)
    scores = jnp.einsum(
        "qgrd,kgd->grqk", grouped, key_block, preferred_element_type=jnp.float32
    ) * (1.0 / math.sqrt(head_dim))
    query_pos = block_start + jnp.arange(rows, dtype=jnp.int32)
    key_pos = block_start - WINDOW + jnp.arange(key_block.shape[0], dtype=jnp.int32)
    allowed = (
        (key_pos[None, :] <= query_pos[:, None])
        & (key_pos[None, :] > query_pos[:, None] - WINDOW)
        & (key_pos[None, :] >= 0)
    )
    scores = jnp.where(allowed, scores, -jnp.inf)
    row_max = jnp.max(scores, axis=-1, keepdims=True)
    unnormed = jnp.exp(scores - row_max)
    row_total = jnp.sum(unnormed, axis=-1)
    weights = unnormed.astype(jnp.bfloat16)
    mixed_out = jnp.einsum(
        "grqk,kgd->qgrd", weights, value_block, preferred_element_type=jnp.float32
    )
    mixed_out = mixed_out / jnp.transpose(row_total, (2, 0, 1))[..., None]
    return mixed_out.reshape(rows, -1).astype(jnp.bfloat16)


def local(
    attn_query, attn_key, attention_value, delta_query, delta_key, delta_value, log_decay, beta_gate
):
    tokens = attn_query.shape[0]
    head_dim = attn_query.shape[2]
    group_count = attn_query.shape[1] // attn_key.shape[1]
    reach_hops = -(-WINDOW // tokens)
    key_value = jnp.stack((attn_key, attention_value))
    pieces = []
    for distance in range(reach_hops, 0, -1):
        pieces.append(shifted(key_value, "ctx", distance))
    pieces.append(key_value)
    extended = jnp.concatenate(pieces, axis=1)
    anchor = lax.axis_index("ctx") * tokens
    blocks_out = attend(attn_query, extended[0], extended[1], anchor + 0, group_count)
    attn_out = lax.all_to_all(blocks_out, "head", split_axis=0, concat_axis=1, tiled=True)
    heads_dev = delta_query.shape[1]
    query_unit = normalize(delta_query, 1.0 / math.sqrt(head_dim))
    key_unit = normalize(delta_key, 1.0)
    inputs = (
        to_spans(query_unit, SPAN),
        to_spans(key_unit, SPAN),
        to_spans(delta_value.astype(jnp.float32), SPAN),
        gate_spans(beta_gate, SPAN),
        gate_spans(log_decay, SPAN),
    )
    zero_state = jnp.zeros((heads_dev, head_dim, head_dim), jnp.float32)
    identity = jnp.broadcast_to(
        jnp.eye(head_dim, dtype=jnp.float32), (heads_dev, head_dim, head_dim)
    )

    def paired_step(carried, span_inputs):
        source_state, transit = carried
        query_part, key_part, value_part, beta_part, log_part = span_inputs
        prepared = prepare(query_part, key_part, beta_part, log_part)
        source_next, local_result = advance(
            source_state, query_part, key_part, value_part, beta_part, prepared
        )
        transit_next, moved_query = advance(transit, query_part, key_part, 0.0, beta_part, prepared)
        return ((source_next, transit_next), (local_result, moved_query))

    def states_step(carried, span_inputs):
        following, outputs_unused = paired_step(carried, span_inputs)
        return (following, None)

    (source_state, transit), unused = lax.scan(states_step, (zero_state, identity), inputs)

    def relay_step(turn, inbound):
        leaving = product("hij,hjk->hik", inbound, transit) + source_state
        return shifted(leaving, "ctx", 1)

    incoming = lax.fori_loop(0, lax.axis_size("ctx") - 1, relay_step, zero_state)

    def output_step(carried, span_inputs):
        query_part, key_part, value_part, beta_part, log_part = span_inputs
        prepared = prepare(query_part, key_part, beta_part, log_part)
        return advance(carried, query_part, key_part, value_part, beta_part, prepared)

    final_state, result_spans = lax.scan(output_step, incoming, inputs)
    delta_local = from_spans(result_spans).astype(jnp.bfloat16)
    delta_out = lax.all_to_all(delta_local, "head", split_axis=0, concat_axis=1, tiled=True)
    return (attn_out, delta_out)


def solution(mesh):
    placed = (
        P("ctx", "head", None),
        P("ctx", "head", None),
        P("ctx", "head", None),
        P("ctx", "head", None),
        P("ctx", "head", None),
        P("ctx", "head", None),
        P("head", "ctx"),
        P("head", "ctx"),
    )
    return jax.shard_map(
        local,
        mesh=mesh,
        in_specs=placed,
        out_specs=(P(("ctx", "head"), None), P(("ctx", "head"), None)),
        check_vma=False,
    )
```

profile of v0, /device:TPU:16, one launch (start us, length us, event | category | flops | bytes accessed | tf_op | source)
XLA Modules:
  0.0 738.2 jit_solution(12141526163066707337)
XLA Ops:
  2.8 3.4 collective-permute-start.1
  13.5 122.5 %while.37 = (s32[]{:T(128)}, f32[8,128,128]{2,1,0:T(8,128)S(1)}, f32[8,128,128]{2,1,0:T(8,128)S(1)}, f32[8,8,64]{2,1,0:T(8,128)S(1)}, f32[8,8,64]{2,1,0:T(8,128)...) while((s32[]{:T(128)}, f32[8,128,128]{2,1,0:T(8,128)S(1)}, ...), condition=%wide.region_5.6_spmd.clone, body=%wide.region_3.0_spmd.clone.sunk | while | flops 807026688 | bytes 10589528 | solution.py:161
  24.2 2.2 fusion.298
  39.5 2.2 fusion.298
  54.8 2.2 fusion.298
  70.1 2.2 fusion.298
  85.4 2.2 fusion.298
  100.7 2.2 fusion.298
  116.1 2.2 fusion.298
  131.4 2.2 fusion.298
  138.5 411.2 %while.35 = (s32[]{:T(128)}, f32[8,128,128]{2,1,0:T(8,128)S(1)}, f32[8,128,128]{2,1,0:T(8,128)S(1)}, f32[8,128,128]{2,1,0:T(8,128)S(1)}, s32[]{:T(128)}) while((s32[]{:T(128)}, f32[8,128,128]{2,1,0:T(8,128)S(1)}, f32[8,128,128]{2,1,0:T(8,128)S(1)}, f32[8,128,128]{2,1,0:T(8,128)S(1)}, s32[]{:T(128)}) %tuple.84), condition=%wide.region_7.8_spmd, body=%wide.region_6.7_spmd.sunk | while | flops 201457664 | bytes 4194405 | solution.py:167
  139.1 3.5 collective-permute-start
  142.7 9.1 %collective-permute-done = f32[8,128,128]{2,1,0:T(8,128)S(1)} collective-permute-done((f32[8,128,128]{2,1,0:T(8,128)S(1)}, f32[8,128,128]{2,1,0:T(8,128)S(1)}, u32[]{:S(2)}, u32[]{:S(2)}) %collective-permute-start) | collective-permute-done | bytes 524320 | tf_op jit(solution)/shard_map/while/body/eval_jaxpr/ppermute | solution.py:18
  154.3 10.7 %collective-permute-done = f32[8,128,128]{2,1,0:T(8,128)S(1)} collective-permute-done((f32[8,128,128]{2,1,0:T(8,128)S(1)}, f32[8,128,128]{2,1,0:T(8,128)S(1)}, u32[]{:S(2)}, u32[]{:S(2)}) %collective-permute-start) | collective-permute-done | bytes 524320 | tf_op jit(solution)/shard_map/while/body/eval_jaxpr/ppermute | solution.py:18
  167.6 10.7 %collective-permute-done = f32[8,128,128]{2,1,0:T(8,128)S(1)} collective-permute-done((f32[8,128,128]{2,1,0:T(8,128)S(1)}, f32[8,128,128]{2,1,0:T(8,128)S(1)}, u32[]{:S(2)}, u32[]{:S(2)}) %collective-permute-start) | collective-permute-done | bytes 524320 | tf_op jit(solution)/shard_map/while/body/eval_jaxpr/ppermute | solution.py:18
  180.9 10.7 %collective-permute-done = f32[8,128,128]{2,1,0:T(8,128)S(1)} collective-permute-done((f32[8,128,128]{2,1,0:T(8,128)S(1)}, f32[8,128,128]{2,1,0:T(8,128)S(1)}, u32[]{:S(2)}, u32[]{:S(2)}) %collective-permute-start) | collective-permute-done | bytes 524320 | tf_op jit(solution)/shard_map/while/body/eval_jaxpr/ppermute | solution.py:18
  194.1 10.7 %collective-permute-done = f32[8,128,128]{2,1,0:T(8,128)S(1)} collective-permute-done((f32[8,128,128]{2,1,0:T(8,128)S(1)}, f32[8,128,128]{2,1,0:T(8,128)S(1)}, u32[]{:S(2)}, u32[]{:S(2)}) %collective-permute-start) | collective-permute-done | bytes 524320 | tf_op jit(solution)/shard_map/while/body/eval_jaxpr/ppermute | solution.py:18
  207.4 10.7 %collective-permute-done = f32[8,128,128]{2,1,0:T(8,128)S(1)} collective-permute-done((f32[8,128,128]{2,1,0:T(8,128)S(1)}, f32[8,128,128]{2,1,0:T(8,128)S(1)}, u32[]{:S(2)}, u32[]{:S(2)}) %collective-permute-start) | collective-permute-done | bytes 524320 | tf_op jit(solution)/shard_map/while/body/eval_jaxpr/ppermute | solution.py:18
  220.7 10.7 %collective-permute-done = f32[8,128,128]{2,1,0:T(8,128)S(1)} collective-permute-done((f32[8,128,128]{2,1,0:T(8,128)S(1)}, f32[8,128,128]{2,1,0:T(8,128)S(1)}, u32[]{:S(2)}, u32[]{:S(2)}) %collective-permute-start) | collective-permute-done | bytes 524320 | tf_op jit(solution)/shard_map/while/body/eval_jaxpr/ppermute | solution.py:18
  233.9 10.7 %collective-permute-done = f32[8,128,128]{2,1,0:T(8,128)S(1)} collective-permute-done((f32[8,128,128]{2,1,0:T(8,128)S(1)}, f32[8,128,128]{2,1,0:T(8,128)S(1)}, u32[]{:S(2)}, u32[]{:S(2)}) %collective-permute-start) | collective-permute-done | bytes 524320 | tf_op jit(solution)/shard_map/while/body/eval_jaxpr/ppermute | solution.py:18
  247.2 10.7 %collective-permute-done = f32[8,128,128]{2,1,0:T(8,128)S(1)} collective-permute-done((f32[8,128,128]{2,1,0:T(8,128)S(1)}, f32[8,128,128]{2,1,0:T(8,128)S(1)}, u32[]{:S(2)}, u32[]{:S(2)}) %collective-permute-start) | collective-permute-done | bytes 524320 | tf_op jit(solution)/shard_map/while/body/eval_jaxpr/ppermute | solution.py:18
  260.4 10.7 %collective-permute-done = f32[8,128,128]{2,1,0:T(8,128)S(1)} collective-permute-done((f32[8,128,128]{2,1,0:T(8,128)S(1)}, f32[8,128,128]{2,1,0:T(8,128)S(1)}, u32[]{:S(2)}, u32[]{:S(2)}) %collective-permute-start) | collective-permute-done | bytes 524320 | tf_op jit(solution)/shard_map/while/body/eval_jaxpr/ppermute | solution.py:18
  273.7 10.7 %collective-permute-done = f32[8,128,128]{2,1,0:T(8,128)S(1)} collective-permute-done((f32[8,128,128]{2,1,0:T(8,128)S(1)}, f32[8,128,128]{2,1,0:T(8,128)S(1)}, u32[]{:S(2)}, u32[]{:S(2)}) %collective-permute-start) | collective-permute-done | bytes 524320 | tf_op jit(solution)/shard_map/while/body/eval_jaxpr/ppermute | solution.py:18
  287.0 10.7 %collective-permute-done = f32[8,128,128]{2,1,0:T(8,128)S(1)} collective-permute-done((f32[8,128,128]{2,1,0:T(8,128)S(1)}, f32[8,128,128]{2,1,0:T(8,128)S(1)}, u32[]{:S(2)}, u32[]{:S(2)}) %collective-permute-start) | collective-permute-done | bytes 524320 | tf_op jit(solution)/shard_map/while/body/eval_jaxpr/ppermute | solution.py:18
  300.2 10.7 %collective-permute-done = f32[8,128,128]{2,1,0:T(8,128)S(1)} collective-permute-done((f32[8,128,128]{2,1,0:T(8,128)S(1)}, f32[8,128,128]{2,1,0:T(8,128)S(1)}, u32[]{:S(2)}, u32[]{:S(2)}) %collective-permute-start) | collective-permute-done | bytes 524320 | tf_op jit(solution)/shard_map/while/body/eval_jaxpr/ppermute | solution.py:18
  313.5 10.7 %collective-permute-done = f32[8,128,128]{2,1,0:T(8,128)S(1)} collective-permute-done((f32[8,128,128]{2,1,0:T(8,128)S(1)}, f32[8,128,128]{2,1,0:T(8,128)S(1)}, u32[]{:S(2)}, u32[]{:S(2)}) %collective-permute-start) | collective-permute-done | bytes 524320 | tf_op jit(solution)/shard_map/while/body/eval_jaxpr/ppermute | solution.py:18
  326.8 10.7 %collective-permute-done = f32[8,128,128]{2,1,0:T(8,128)S(1)} collective-permute-done((f32[8,128,128]{2,1,0:T(8,128)S(1)}, f32[8,128,128]{2,1,0:T(8,128)S(1)}, u32[]{:S(2)}, u32[]{:S(2)}) %collective-permute-start) | collective-permute-done | bytes 524320 | tf_op jit(solution)/shard_map/while/body/eval_jaxpr/ppermute | solution.py:18
  340.0 10.7 %collective-permute-done = f32[8,128,128]{2,1,0:T(8,128)S(1)} collective-permute-done((f32[8,128,128]{2,1,0:T(8,128)S(1)}, f32[8,128,128]{2,1,0:T(8,128)S(1)}, u32[]{:S(2)}, u32[]{:S(2)}) %collective-permute-start) | collective-permute-done | bytes 524320 | tf_op jit(solution)/shard_map/while/body/eval_jaxpr/ppermute | solution.py:18
  353.3 10.7 %collective-permute-done = f32[8,128,128]{2,1,0:T(8,128)S(1)} collective-permute-done((f32[8,128,128]{2,1,0:T(8,128)S(1)}, f32[8,128,128]{2,1,0:T(8,128)S(1)}, u32[]{:S(2)}, u32[]{:S(2)}) %collective-permute-start) | collective-permute-done | bytes 524320 | tf_op jit(solution)/shard_map/while/body/eval_jaxpr/ppermute | solution.py:18
  366.6 10.7 %collective-permute-done = f32[8,128,128]{2,1,0:T(8,128)S(1)} collective-permute-done((f32[8,128,128]{2,1,0:T(8,128)S(1)}, f32[8,128,128]{2,1,0:T(8,128)S(1)}, u32[]{:S(2)}, u32[]{:S(2)}) %collective-permute-start) | collective-permute-done | bytes 524320 | tf_op jit(solution)/shard_map/while/body/eval_jaxpr/ppermute | solution.py:18
  379.8 10.7 %collective-permute-done = f32[8,128,128]{2,1,0:T(8,128)S(1)} collective-permute-done((f32[8,128,128]{2,1,0:T(8,128)S(1)}, f32[8,128,128]{2,1,0:T(8,128)S(1)}, u32[]{:S(2)}, u32[]{:S(2)}) %collective-permute-start) | collective-permute-done | bytes 524320 | tf_op jit(solution)/shard_map/while/body/eval_jaxpr/ppermute | solution.py:18
  393.1 10.7 %collective-permute-done = f32[8,128,128]{2,1,0:T(8,128)S(1)} collective-permute-done((f32[8,128,128]{2,1,0:T(8,128)S(1)}, f32[8,128,128]{2,1,0:T(8,128)S(1)}, u32[]{:S(2)}, u32[]{:S(2)}) %collective-permute-start) | collective-permute-done | bytes 524320 | tf_op jit(solution)/shard_map/while/body/eval_jaxpr/ppermute | solution.py:18
  406.3 10.7 %collective-permute-done = f32[8,128,128]{2,1,0:T(8,128)S(1)} collective-permute-done((f32[8,128,128]{2,1,0:T(8,128)S(1)}, f32[8,128,128]{2,1,0:T(8,128)S(1)}, u32[]{:S(2)}, u32[]{:S(2)}) %collective-permute-start) | collective-permute-done | bytes 524320 | tf_op jit(solution)/shard_map/while/body/eval_jaxpr/ppermute | solution.py:18
  419.6 10.7 %collective-permute-done = f32[8,128,128]{2,1,0:T(8,128)S(1)} collective-permute-done((f32[8,128,128]{2,1,0:T(8,128)S(1)}, f32[8,128,128]{2,1,0:T(8,128)S(1)}, u32[]{:S(2)}, u32[]{:S(2)}) %collective-permute-start) | collective-permute-done | bytes 524320 | tf_op jit(solution)/shard_map/while/body/eval_jaxpr/ppermute | solution.py:18
  432.9 10.7 %collective-permute-done = f32[8,128,128]{2,1,0:T(8,128)S(1)} collective-permute-done((f32[8,128,128]{2,1,0:T(8,128)S(1)}, f32[8,128,128]{2,1,0:T(8,128)S(1)}, u32[]{:S(2)}, u32[]{:S(2)}) %collective-permute-start) | collective-permute-done | bytes 524320 | tf_op jit(solution)/shard_map/while/body/eval_jaxpr/ppermute | solution.py:18
  446.1 10.7 %collective-permute-done = f32[8,128,128]{2,1,0:T(8,128)S(1)} collective-permute-done((f32[8,128,128]{2,1,0:T(8,128)S(1)}, f32[8,128,128]{2,1,0:T(8,128)S(1)}, u32[]{:S(2)}, u32[]{:S(2)}) %collective-permute-start) | collective-permute-done | bytes 524320 | tf_op jit(solution)/shard_map/while/body/eval_jaxpr/ppermute | solution.py:18
  459.4 10.7 %collective-permute-done = f32[8,128,128]{2,1,0:T(8,128)S(1)} collective-permute-done((f32[8,128,128]{2,1,0:T(8,128)S(1)}, f32[8,128,128]{2,1,0:T(8,128)S(1)}, u32[]{:S(2)}, u32[]{:S(2)}) %collective-permute-start) | collective-permute-done | bytes 524320 | tf_op jit(solution)/shard_map/while/body/eval_jaxpr/ppermute | solution.py:18
  472.7 10.7 %collective-permute-done = f32[8,128,128]{2,1,0:T(8,128)S(1)} collective-permute-done((f32[8,128,128]{2,1,0:T(8,128)S(1)}, f32[8,128,128]{2,1,0:T(8,128)S(1)}, u32[]{:S(2)}, u32[]{:S(2)}) %collective-permute-start) | collective-permute-done | bytes 524320 | tf_op jit(solution)/shard_map/while/body/eval_jaxpr/ppermute | solution.py:18
  485.9 10.7 %collective-permute-done = f32[8,128,128]{2,1,0:T(8,128)S(1)} collective-permute-done((f32[8,128,128]{2,1,0:T(8,128)S(1)}, f32[8,128,128]{2,1,0:T(8,128)S(1)}, u32[]{:S(2)}, u32[]{:S(2)}) %collective-permute-start) | collective-permute-done | bytes 524320 | tf_op jit(solution)/shard_map/while/body/eval_jaxpr/ppermute | solution.py:18
  499.2 10.7 %collective-permute-done = f32[8,128,128]{2,1,0:T(8,128)S(1)} collective-permute-done((f32[8,128,128]{2,1,0:T(8,128)S(1)}, f32[8,128,128]{2,1,0:T(8,128)S(1)}, u32[]{:S(2)}, u32[]{:S(2)}) %collective-permute-start) | collective-permute-done | bytes 524320 | tf_op jit(solution)/shard_map/while/body/eval_jaxpr/ppermute | solution.py:18
  512.4 10.7 %collective-permute-done = f32[8,128,128]{2,1,0:T(8,128)S(1)} collective-permute-done((f32[8,128,128]{2,1,0:T(8,128)S(1)}, f32[8,128,128]{2,1,0:T(8,128)S(1)}, u32[]{:S(2)}, u32[]{:S(2)}) %collective-permute-start) | collective-permute-done | bytes 524320 | tf_op jit(solution)/shard_map/while/body/eval_jaxpr/ppermute | solution.py:18
  525.7 10.7 %collective-permute-done = f32[8,128,128]{2,1,0:T(8,128)S(1)} collective-permute-done((f32[8,128,128]{2,1,0:T(8,128)S(1)}, f32[8,128,128]{2,1,0:T(8,128)S(1)}, u32[]{:S(2)}, u32[]{:S(2)}) %collective-permute-start) | collective-permute-done | bytes 524320 | tf_op jit(solution)/shard_map/while/body/eval_jaxpr/ppermute | solution.py:18
  539.0 10.7 %collective-permute-done = f32[8,128,128]{2,1,0:T(8,128)S(1)} collective-permute-done((f32[8,128,128]{2,1,0:T(8,128)S(1)}, f32[8,128,128]{2,1,0:T(8,128)S(1)}, u32[]{:S(2)}, u32[]{:S(2)}) %collective-permute-start) | collective-permute-done | bytes 524320 | tf_op jit(solution)/shard_map/while/body/eval_jaxpr/ppermute | solution.py:18
  549.7 123.9 %while.36 = (s32[]{:T(128)}, f32[8,128,128]{2,1,0:T(8,128)S(1)}, bf16[8,8,64,128]{3,2,1,0:T(8,128)(2,1)}, f32[8,8,64]{2,1,0:T(8,128)S(1)}, f32[8,8,64]{2,1,0:T(8...) while((s32[]{:T(128)}, f32[8,128,128]{2,1,0:T(8,128)S(1)}, ...), condition=%wide.region_11.12_spmd, body=%wide.region_9.11_spmd.sunk | while | flops 756137984 | bytes 10470705 | solution.py:174
  555.7 2.2 fusion.255
  563.0 2.2 convolution_add_fusion.35
  571.2 2.2 fusion.255
  578.4 2.2 convolution_add_fusion.35
  586.7 2.2 fusion.255
  593.9 2.2 convolution_add_fusion.35
  602.2 2.2 fusion.255
  617.7 2.2 fusion.255
  633.2 2.2 fusion.255
  640.4 2.2 convolution_add_fusion.35
  648.7 2.2 fusion.255
  655.9 2.2 convolution_add_fusion.35
  664.2 2.2 fusion.255
  676.8 5.3 all-to-all-start.1
  684.7 10.4 %fusion.51 = (f32[2,4,512]{2,1,0:T(4,128)S(1)}, f32[2,1536,512,4]{2,1,3,0:T(8,128)}) fusion(pred[512,1536]{0,1:T(8,128)(4,1)S(1)} %and_and_fusion, bf16[512,2,4,128]{3,2,1,0:T(4,128)(2,1)S(1)} %bitcast.293, bf16[2,1536,2,128]{3,1,2,0:T(8,128)(2,1)S(1)} %maximum_maximum_fusion), kind=kOutput, calls=%fused_computation.94 | convolution fusion | flops 1629483008 | bytes 27803648 | tf_op jit(solution)/shard_map/qgrd,kgd->grqk/dot_general | solution.py:94
  695.0 11.1 %fusion.49 = f32[2,4,512]{2,1,0:T(4,128)S(1)} fusion(f32[2,1536,512,4]{2,1,3,0:T(8,128)} %get-tuple-element.232, f32[2,4,512]{2,1,0:T(4,128)S(1)} %get-tuple-element.231, pred[512,1536]{0,1:T(8,128)(4,1)S(1)} %and_and_fusion), kind=kLoop, calls=%fused_computation.92 | loop fusion | flops 25161728 | bytes 25985024 | tf_op jit(solution)/shard_map/reduce_sum | solution.py:107
  706.1 12.6 %fusion.58 = bf16[512,2,4,128]{0,3,2,1:T(8,128)(2,1)} fusion(f32[2,1536,512,4]{2,1,3,0:T(8,128)} %get-tuple-element.232, f32[2,4,512]{2,1,0:T(4,128)S(1)} %get-tuple-element.231, pred[512,1536]{0,1:T(8,128)(4,1)S(1)} %and_and_fusion, f32[512,2,4]{0,2,1:T(4,128)S(1)} %bitcast.303, bf16[2,1536,2,128]{3,1,2,0:T(8,128)(2,1)S(1)} %maximum_maximum_fusion), kind=kOutput, calls=%fused_computation.107 | convolution fusion | flops 1636827136 | bytes 27820032 | tf_op jit(solution)/shard_map/grqk,kgd->qgrd/dot_general | solution.py:109
  721.2 4.8 all-to-all-start
  727.3 2.3 copy.68
  729.6 7.3 all-to-all-done
  (487 shorter events, 298.6 us)
Async XLA Ops:
  0.6 684.0 %copy-start = (bf16[512,8,128]{2,1,0:T(8,128)(2,1)S(1)}, bf16[512,8,128]{2,1,0:T(8,128)(2,1)}, u32[]{:S(2)}) copy-start(bf16[512,8,128]{2,1,0:T(8,128)(2,1)} %param.14) | copy-start | bytes 3145732
  0.6 7.6 %copy-start.1 = (bf16[512,8,128]{2,1,0:T(8,128)(2,1)S(1)}, bf16[512,8,128]{2,1,0:T(8,128)(2,1)}, u32[]{:S(2)}) copy-start(bf16[512,8,128]{2,1,0:T(8,128)(2,1)} %param.18) | copy-start | bytes 3145732
  1.9 6.3 copy-start.3
  1.9 6.3 copy-start.5
  2.8 680.5 %collective-permute-start.1 = (bf16[2,512,2,128]{3,1,2,0:T(8,128)(2,1)}, bf16[2,512,2,128]{3,1,2,0:T(8,128)(2,1)}, u32[]{:S(2)}, u32[]{:S(2)}) collective-permute-start(bf16[2,512,2,128]{3,1,2,0:T(8,128)(2,1)} %pad_maximum_fusion), channel_id=1, source_target_pairs={{0,8},{4,12},{8,16},{12,20},{16,24},{20,28},{24,32},{28,36},{32,40... | collective-permute-start | bytes 1572872 | tf_op jit(solution)/shard_map/ppermute | solution.py:18
  6.2 677.1 %collective-permute-start.2 = (bf16[2,512,2,128]{3,1,2,0:T(8,128)(2,1)}, bf16[2,512,2,128]{3,1,2,0:T(8,128)(2,1)}, u32[]{:S(2)}, u32[]{:S(2)}) collective-permute-start(bf16[2,512,2,128]{3,1,2,0:T(8,128)(2,1)} %pad_maximum_fusion), channel_id=1, source_target_pairs={{0,4},{4,8},{8,12},{12,16},{16,20},{20,24},{24,28},{28,32},{32,36}... | collective-permute-start | bytes 1572872 | tf_op jit(solution)/shard_map/ppermute | solution.py:18
  9.7 1.7 copy-start.7
  11.5 1.7 copy-start.8
  11.6 1.8 copy-start.9
  13.5 122.5 %copy-start.2 = (bf16[512,8,128]{2,1,0:T(8,128)(2,1)S(1)}, bf16[512,8,128]{2,1,0:T(8,128)(2,1)}, u32[]{:S(2)}) copy-start(bf16[512,8,128]{2,1,0:T(8,128)(2,1)} %param.17) | copy-start | bytes 3145732
  139.1 12.6 %collective-permute-start = (f32[8,128,128]{2,1,0:T(8,128)S(1)}, f32[8,128,128]{2,1,0:T(8,128)S(1)}, u32[]{:S(2)}, u32[]{:S(2)}) collective-permute-start(f32[8,128,128]{2,1,0:T(8,128)S(1)} %convolution_add_fusion.29), channel_id=1, source_target_pairs={{0,4},{4,8},{8,12},{12,16},{16,20},{20,24},{24,28},{28,32},{32,36}... | collective-permute-start | bytes 1572872 | tf_op jit(solution)/shard_map/while/body/eval_jaxpr/ppermute | solution.py:18
  152.4 12.6 %collective-permute-start = (f32[8,128,128]{2,1,0:T(8,128)S(1)}, f32[8,128,128]{2,1,0:T(8,128)S(1)}, u32[]{:S(2)}, u32[]{:S(2)}) collective-permute-start(f32[8,128,128]{2,1,0:T(8,128)S(1)} %convolution_add_fusion.29), channel_id=1, source_target_pairs={{0,4},{4,8},{8,12},{12,16},{16,20},{20,24},{24,28},{28,32},{32,36}... | collective-permute-start | bytes 1572872 | tf_op jit(solution)/shard_map/while/body/eval_jaxpr/ppermute | solution.py:18
  165.7 12.6 %collective-permute-start = (f32[8,128,128]{2,1,0:T(8,128)S(1)}, f32[8,128,128]{2,1,0:T(8,128)S(1)}, u32[]{:S(2)}, u32[]{:S(2)}) collective-permute-start(f32[8,128,128]{2,1,0:T(8,128)S(1)} %convolution_add_fusion.29), channel_id=1, source_target_pairs={{0,4},{4,8},{8,12},{12,16},{16,20},{20,24},{24,28},{28,32},{32,36}... | collective-permute-start | bytes 1572872 | tf_op jit(solution)/shard_map/while/body/eval_jaxpr/ppermute | solution.py:18
  178.9 12.6 %collective-permute-start = (f32[8,128,128]{2,1,0:T(8,128)S(1)}, f32[8,128,128]{2,1,0:T(8,128)S(1)}, u32[]{:S(2)}, u32[]{:S(2)}) collective-permute-start(f32[8,128,128]{2,1,0:T(8,128)S(1)} %convolution_add_fusion.29), channel_id=1, source_target_pairs={{0,4},{4,8},{8,12},{12,16},{16,20},{20,24},{24,28},{28,32},{32,36}... | collective-permute-start | bytes 1572872 | tf_op jit(solution)/shard_map/while/body/eval_jaxpr/ppermute | solution.py:18
  192.2 12.6 %collective-permute-start = (f32[8,128,128]{2,1,0:T(8,128)S(1)}, f32[8,128,128]{2,1,0:T(8,128)S(1)}, u32[]{:S(2)}, u32[]{:S(2)}) collective-permute-start(f32[8,128,128]{2,1,0:T(8,128)S(1)} %convolution_add_fusion.29), channel_id=1, source_target_pairs={{0,4},{4,8},{8,12},{12,16},{16,20},{20,24},{24,28},{28,32},{32,36}... | collective-permute-start | bytes 1572872 | tf_op jit(solution)/shard_map/while/body/eval_jaxpr/ppermute | solution.py:18
  205.5 12.6 %collective-permute-start = (f32[8,128,128]{2,1,0:T(8,128)S(1)}, f32[8,128,128]{2,1,0:T(8,128)S(1)}, u32[]{:S(2)}, u32[]{:S(2)}) collective-permute-start(f32[8,128,128]{2,1,0:T(8,128)S(1)} %convolution_add_fusion.29), channel_id=1, source_target_pairs={{0,4},{4,8},{8,12},{12,16},{16,20},{20,24},{24,28},{28,32},{32,36}... | collective-permute-start | bytes 1572872 | tf_op jit(solution)/shard_map/while/body/eval_jaxpr/ppermute | solution.py:18
  218.7 12.6 %collective-permute-start = (f32[8,128,128]{2,1,0:T(8,128)S(1)}, f32[8,128,128]{2,1,0:T(8,128)S(1)}, u32[]{:S(2)}, u32[]{:S(2)}) collective-permute-start(f32[8,128,128]{2,1,0:T(8,128)S(1)} %convolution_add_fusion.29), channel_id=1, source_target_pairs={{0,4},{4,8},{8,12},{12,16},{16,20},{20,24},{24,28},{28,32},{32,36}... | collective-permute-start | bytes 1572872 | tf_op jit(solution)/shard_map/while/body/eval_jaxpr/ppermute | solution.py:18
  232.0 12.6 %collective-permute-start = (f32[8,128,128]{2,1,0:T(8,128)S(1)}, f32[8,128,128]{2,1,0:T(8,128)S(1)}, u32[]{:S(2)}, u32[]{:S(2)}) collective-permute-start(f32[8,128,128]{2,1,0:T(8,128)S(1)} %convolution_add_fusion.29), channel_id=1, source_target_pairs={{0,4},{4,8},{8,12},{12,16},{16,20},{20,24},{24,28},{28,32},{32,36}... | collective-permute-start | bytes 1572872 | tf_op jit(solution)/shard_map/while/body/eval_jaxpr/ppermute | solution.py:18
  245.3 12.6 %collective-permute-start = (f32[8,128,128]{2,1,0:T(8,128)S(1)}, f32[8,128,128]{2,1,0:T(8,128)S(1)}, u32[]{:S(2)}, u32[]{:S(2)}) collective-permute-start(f32[8,128,128]{2,1,0:T(8,128)S(1)} %convolution_add_fusion.29), channel_id=1, source_target_pairs={{0,4},{4,8},{8,12},{12,16},{16,20},{20,24},{24,28},{28,32},{32,36}... | collective-permute-start | bytes 1572872 | tf_op jit(solution)/shard_map/while/body/eval_jaxpr/ppermute | solution.py:18
  258.5 12.6 %collective-permute-start = (f32[8,128,128]{2,1,0:T(8,128)S(1)}, f32[8,128,128]{2,1,0:T(8,128)S(1)}, u32[]{:S(2)}, u32[]{:S(2)}) collective-permute-start(f32[8,128,128]{2,1,0:T(8,128)S(1)} %convolution_add_fusion.29), channel_id=1, source_target_pairs={{0,4},{4,8},{8,12},{12,16},{16,20},{20,24},{24,28},{28,32},{32,36}... | collective-permute-start | bytes 1572872 | tf_op jit(solution)/shard_map/while/body/eval_jaxpr/ppermute | solution.py:18
  271.8 12.6 %collective-permute-start = (f32[8,128,128]{2,1,0:T(8,128)S(1)}, f32[8,128,128]{2,1,0:T(8,128)S(1)}, u32[]{:S(2)}, u32[]{:S(2)}) collective-permute-start(f32[8,128,128]{2,1,0:T(8,128)S(1)} %convolution_add_fusion.29), channel_id=1, source_target_pairs={{0,4},{4,8},{8,12},{12,16},{16,20},{20,24},{24,28},{28,32},{32,36}... | collective-permute-start | bytes 1572872 | tf_op jit(solution)/shard_map/while/body/eval_jaxpr/ppermute | solution.py:18
  285.0 12.6 %collective-permute-start = (f32[8,128,128]{2,1,0:T(8,128)S(1)}, f32[8,128,128]{2,1,0:T(8,128)S(1)}, u32[]{:S(2)}, u32[]{:S(2)}) collective-permute-start(f32[8,128,128]{2,1,0:T(8,128)S(1)} %convolution_add_fusion.29), channel_id=1, source_target_pairs={{0,4},{4,8},{8,12},{12,16},{16,20},{20,24},{24,28},{28,32},{32,36}... | collective-permute-start | bytes 1572872 | tf_op jit(solution)/shard_map/while/body/eval_jaxpr/ppermute | solution.py:18
  298.3 12.6 %collective-permute-start = (f32[8,128,128]{2,1,0:T(8,128)S(1)}, f32[8,128,128]{2,1,0:T(8,128)S(1)}, u32[]{:S(2)}, u32[]{:S(2)}) collective-permute-start(f32[8,128,128]{2,1,0:T(8,128)S(1)} %convolution_add_fusion.29), channel_id=1, source_target_pairs={{0,4},{4,8},{8,12},{12,16},{16,20},{20,24},{24,28},{28,32},{32,36}... | collective-permute-start | bytes 1572872 | tf_op jit(solution)/shard_map/while/body/eval_jaxpr/ppermute | solution.py:18
  311.6 12.6 %collective-permute-start = (f32[8,128,128]{2,1,0:T(8,128)S(1)}, f32[8,128,128]{2,1,0:T(8,128)S(1)}, u32[]{:S(2)}, u32[]{:S(2)}) collective-permute-start(f32[8,128,128]{2,1,0:T(8,128)S(1)} %convolution_add_fusion.29), channel_id=1, source_target_pairs={{0,4},{4,8},{8,12},{12,16},{16,20},{20,24},{24,28},{28,32},{32,36}... | collective-permute-start | bytes 1572872 | tf_op jit(solution)/shard_map/while/body/eval_jaxpr/ppermute | solution.py:18
  324.8 12.6 %collective-permute-start = (f32[8,128,128]{2,1,0:T(8,128)S(1)}, f32[8,128,128]{2,1,0:T(8,128)S(1)}, u32[]{:S(2)}, u32[]{:S(2)}) collective-permute-start(f32[8,128,128]{2,1,0:T(8,128)S(1)} %convolution_add_fusion.29), channel_id=1, source_target_pairs={{0,4},{4,8},{8,12},{12,16},{16,20},{20,24},{24,28},{28,32},{32,36}... | collective-permute-start | bytes 1572872 | tf_op jit(solution)/shard_map/while/body/eval_jaxpr/ppermute | solution.py:18
  338.1 12.6 %collective-permute-start = (f32[8,128,128]{2,1,0:T(8,128)S(1)}, f32[8,128,128]{2,1,0:T(8,128)S(1)}, u32[]{:S(2)}, u32[]{:S(2)}) collective-permute-start(f32[8,128,128]{2,1,0:T(8,128)S(1)} %convolution_add_fusion.29), channel_id=1, source_target_pairs={{0,4},{4,8},{8,12},{12,16},{16,20},{20,24},{24,28},{28,32},{32,36}... | collective-permute-start | bytes 1572872 | tf_op jit(solution)/shard_map/while/body/eval_jaxpr/ppermute | solution.py:18
  351.4 12.6 %collective-permute-start = (f32[8,128,128]{2,1,0:T(8,128)S(1)}, f32[8,128,128]{2,1,0:T(8,128)S(1)}, u32[]{:S(2)}, u32[]{:S(2)}) collective-permute-start(f32[8,128,128]{2,1,0:T(8,128)S(1)} %convolution_add_fusion.29), channel_id=1, source_target_pairs={{0,4},{4,8},{8,12},{12,16},{16,20},{20,24},{24,28},{28,32},{32,36}... | collective-permute-start | bytes 1572872 | tf_op jit(solution)/shard_map/while/body/eval_jaxpr/ppermute | solution.py:18
  364.6 12.6 %collective-permute-start = (f32[8,128,128]{2,1,0:T(8,128)S(1)}, f32[8,128,128]{2,1,0:T(8,128)S(1)}, u32[]{:S(2)}, u32[]{:S(2)}) collective-permute-start(f32[8,128,128]{2,1,0:T(8,128)S(1)} %convolution_add_fusion.29), channel_id=1, source_target_pairs={{0,4},{4,8},{8,12},{12,16},{16,20},{20,24},{24,28},{28,32},{32,36}... | collective-permute-start | bytes 1572872 | tf_op jit(solution)/shard_map/while/body/eval_jaxpr/ppermute | solution.py:18
  377.9 12.6 %collective-permute-start = (f32[8,128,128]{2,1,0:T(8,128)S(1)}, f32[8,128,128]{2,1,0:T(8,128)S(1)}, u32[]{:S(2)}, u32[]{:S(2)}) collective-permute-start(f32[8,128,128]{2,1,0:T(8,128)S(1)} %convolution_add_fusion.29), channel_id=1, source_target_pairs={{0,4},{4,8},{8,12},{12,16},{16,20},{20,24},{24,28},{28,32},{32,36}... | collective-permute-start | bytes 1572872 | tf_op jit(solution)/shard_map/while/body/eval_jaxpr/ppermute | solution.py:18
  391.1 12.6 %collective-permute-start = (f32[8,128,128]{2,1,0:T(8,128)S(1)}, f32[8,128,128]{2,1,0:T(8,128)S(1)}, u32[]{:S(2)}, u32[]{:S(2)}) collective-permute-start(f32[8,128,128]{2,1,0:T(8,128)S(1)} %convolution_add_fusion.29), channel_id=1, source_target_pairs={{0,4},{4,8},{8,12},{12,16},{16,20},{20,24},{24,28},{28,32},{32,36}... | collective-permute-start | bytes 1572872 | tf_op jit(solution)/shard_map/while/body/eval_jaxpr/ppermute | solution.py:18
  404.4 12.6 %collective-permute-start = (f32[8,128,128]{2,1,0:T(8,128)S(1)}, f32[8,128,128]{2,1,0:T(8,128)S(1)}, u32[]{:S(2)}, u32[]{:S(2)}) collective-permute-start(f32[8,128,128]{2,1,0:T(8,128)S(1)} %convolution_add_fusion.29), channel_id=1, source_target_pairs={{0,4},{4,8},{8,12},{12,16},{16,20},{20,24},{24,28},{28,32},{32,36}... | collective-permute-start | bytes 1572872 | tf_op jit(solution)/shard_map/while/body/eval_jaxpr/ppermute | solution.py:18
  417.7 12.6 %collective-permute-start = (f32[8,128,128]{2,1,0:T(8,128)S(1)}, f32[8,128,128]{2,1,0:T(8,128)S(1)}, u32[]{:S(2)}, u32[]{:S(2)}) collective-permute-start(f32[8,128,128]{2,1,0:T(8,128)S(1)} %convolution_add_fusion.29), channel_id=1, source_target_pairs={{0,4},{4,8},{8,12},{12,16},{16,20},{20,24},{24,28},{28,32},{32,36}... | collective-permute-start | bytes 1572872 | tf_op jit(solution)/shard_map/while/body/eval_jaxpr/ppermute | solution.py:18
  430.9 12.6 %collective-permute-start = (f32[8,128,128]{2,1,0:T(8,128)S(1)}, f32[8,128,128]{2,1,0:T(8,128)S(1)}, u32[]{:S(2)}, u32[]{:S(2)}) collective-permute-start(f32[8,128,128]{2,1,0:T(8,128)S(1)} %convolution_add_fusion.29), channel_id=1, source_target_pairs={{0,4},{4,8},{8,12},{12,16},{16,20},{20,24},{24,28},{28,32},{32,36}... | collective-permute-start | bytes 1572872 | tf_op jit(solution)/shard_map/while/body/eval_jaxpr/ppermute | solution.py:18
  444.2 12.6 %collective-permute-start = (f32[8,128,128]{2,1,0:T(8,128)S(1)}, f32[8,128,128]{2,1,0:T(8,128)S(1)}, u32[]{:S(2)}, u32[]{:S(2)}) collective-permute-start(f32[8,128,128]{2,1,0:T(8,128)S(1)} %convolution_add_fusion.29), channel_id=1, source_target_pairs={{0,4},{4,8},{8,12},{12,16},{16,20},{20,24},{24,28},{28,32},{32,36}... | collective-permute-start | bytes 1572872 | tf_op jit(solution)/shard_map/while/body/eval_jaxpr/ppermute | solution.py:18
  457.5 12.6 %collective-permute-start = (f32[8,128,128]{2,1,0:T(8,128)S(1)}, f32[8,128,128]{2,1,0:T(8,128)S(1)}, u32[]{:S(2)}, u32[]{:S(2)}) collective-permute-start(f32[8,128,128]{2,1,0:T(8,128)S(1)} %convolution_add_fusion.29), channel_id=1, source_target_pairs={{0,4},{4,8},{8,12},{12,16},{16,20},{20,24},{24,28},{28,32},{32,36}... | collective-permute-start | bytes 1572872 | tf_op jit(solution)/shard_map/while/body/eval_jaxpr/ppermute | solution.py:18
  470.7 12.6 %collective-permute-start = (f32[8,128,128]{2,1,0:T(8,128)S(1)}, f32[8,128,128]{2,1,0:T(8,128)S(1)}, u32[]{:S(2)}, u32[]{:S(2)}) collective-permute-start(f32[8,128,128]{2,1,0:T(8,128)S(1)} %convolution_add_fusion.29), channel_id=1, source_target_pairs={{0,4},{4,8},{8,12},{12,16},{16,20},{20,24},{24,28},{28,32},{32,36}... | collective-permute-start | bytes 1572872 | tf_op jit(solution)/shard_map/while/body/eval_jaxpr/ppermute | solution.py:18
  484.0 12.6 %collective-permute-start = (f32[8,128,128]{2,1,0:T(8,128)S(1)}, f32[8,128,128]{2,1,0:T(8,128)S(1)}, u32[]{:S(2)}, u32[]{:S(2)}) collective-permute-start(f32[8,128,128]{2,1,0:T(8,128)S(1)} %convolution_add_fusion.29), channel_id=1, source_target_pairs={{0,4},{4,8},{8,12},{12,16},{16,20},{20,24},{24,28},{28,32},{32,36}... | collective-permute-start | bytes 1572872 | tf_op jit(solution)/shard_map/while/body/eval_jaxpr/ppermute | solution.py:18
  497.3 12.6 %collective-permute-start = (f32[8,128,128]{2,1,0:T(8,128)S(1)}, f32[8,128,128]{2,1,0:T(8,128)S(1)}, u32[]{:S(2)}, u32[]{:S(2)}) collective-permute-start(f32[8,128,128]{2,1,0:T(8,128)S(1)} %convolution_add_fusion.29), channel_id=1, source_target_pairs={{0,4},{4,8},{8,12},{12,16},{16,20},{20,24},{24,28},{28,32},{32,36}... | collective-permute-start | bytes 1572872 | tf_op jit(solution)/shard_map/while/body/eval_jaxpr/ppermute | solution.py:18
  510.5 12.6 %collective-permute-start = (f32[8,128,128]{2,1,0:T(8,128)S(1)}, f32[8,128,128]{2,1,0:T(8,128)S(1)}, u32[]{:S(2)}, u32[]{:S(2)}) collective-permute-start(f32[8,128,128]{2,1,0:T(8,128)S(1)} %convolution_add_fusion.29), channel_id=1, source_target_pairs={{0,4},{4,8},{8,12},{12,16},{16,20},{20,24},{24,28},{28,32},{32,36}... | collective-permute-start | bytes 1572872 | tf_op jit(solution)/shard_map/while/body/eval_jaxpr/ppermute | solution.py:18
  523.8 12.6 %collective-permute-start = (f32[8,128,128]{2,1,0:T(8,128)S(1)}, f32[8,128,128]{2,1,0:T(8,128)S(1)}, u32[]{:S(2)}, u32[]{:S(2)}) collective-permute-start(f32[8,128,128]{2,1,0:T(8,128)S(1)} %convolution_add_fusion.29), channel_id=1, source_target_pairs={{0,4},{4,8},{8,12},{12,16},{16,20},{20,24},{24,28},{28,32},{32,36}... | collective-permute-start | bytes 1572872 | tf_op jit(solution)/shard_map/while/body/eval_jaxpr/ppermute | solution.py:18
  537.0 12.6 %collective-permute-start = (f32[8,128,128]{2,1,0:T(8,128)S(1)}, f32[8,128,128]{2,1,0:T(8,128)S(1)}, u32[]{:S(2)}, u32[]{:S(2)}) collective-permute-start(f32[8,128,128]{2,1,0:T(8,128)S(1)} %convolution_add_fusion.29), channel_id=1, source_target_pairs={{0,4},{4,8},{8,12},{12,16},{16,20},{20,24},{24,28},{28,32},{32,36}... | collective-permute-start | bytes 1572872 | tf_op jit(solution)/shard_map/while/body/eval_jaxpr/ppermute | solution.py:18
  675.5 7.8 %copy-start.4 = (bf16[1,512,2,128]{3,1,2,0:T(8,128)(2,1)S(1)}, bf16[1,512,2,128]{3,1,2,0:T(8,128)(2,1)}, u32[]{:S(2)}) copy-start(bf16[1,512,2,128]{3,1,2,0:T(8,128)(2,1)} %copy-done.3) | copy-start | bytes 786436
  675.5 7.8 %copy-start.6 = (bf16[1,512,2,128]{3,1,2,0:T(8,128)(2,1)S(1)}, bf16[1,512,2,128]{3,1,2,0:T(8,128)(2,1)}, u32[]{:S(2)}) copy-start(bf16[1,512,2,128]{3,1,2,0:T(8,128)(2,1)} %copy-done.5) | copy-start | bytes 786436
  676.8 44.4 %all-to-all-start.1 = ((bf16[4,128,1024]{2,1,0:T(8,128)(2,1)}), bf16[4,128,1024]{2,1,0:T(8,128)(2,1)S(1)}, u32[]{:S(2)}, u32[]{:S(2)}) async-start(bf16[4,128,1024]{2,1,0:T(8,128)(2,1)} %convert_element_type.52), calls=%async_computation.1 | async-start | bytes 2097152 | tf_op jit(solution)/shard_map/all_to_all | solution.py:176
  721.2 15.7 %all-to-all-start = ((bf16[4,128,1024]{1,2,0:T(8,128)(2,1)}), bf16[4,128,1024]{1,2,0:T(8,128)(2,1)S(1)}, u32[]{:S(2)}, u32[]{:S(2)}) async-start(bf16[4,128,1024]{1,2,0:T(8,128)(2,1)} %copy.55), calls=%async_computation | async-start | bytes 2097152 | tf_op jit(solution)/shard_map/all_to_all | solution.py:131
where the time goes:
time: 742 us; the launch traced here: 738 us
  waiting for transfers between devices  337 us (45%)
  matrix products  271 us (37%)
  starting transfers between devices  76.5 us (10%)
  local copies, waits for them, and re-layouts  26.4 us (4%)
  other arithmetic  23.4 us (3%)
    ppermute x33, waiting for transfers between devices, shifted(): return lax.ppermute(block, axis, route)  329 us
    dot_general x303, matrix products, product(): return jnp.einsum(form, left, right, precision=lax.Precision.HIGHEST)  248 us
    ppermute x33, starting transfers between devices, shifted(): return lax.ppermute(block, axis, route)  66.4 us
  transfers between devices with their start and end apart: 35, of which 32 were waited for; matrix products, arithmetic and copies ran while one was open for 43% of the time, Pallas kernels for 0%

commit v1 on v0

v1 whole, which is shorter than its diff:
```python
import math

import jax
import jax.numpy as jnp
from jax import lax
from jax.experimental import pallas as pl
from jax.experimental.pallas import tpu as pltpu
from jax.sharding import Mesh, PartitionSpec as P

WINDOW = 1024
CHUNK = 128
HEAD = 128
EPSILON = 1e-06
MASKED = -1e30

f32 = jnp.float32
bf16 = jnp.bfloat16


def dot(left, right):
    return lax.dot_general(left, right, (((1,), (0,)), ((), ())), preferred_element_type=f32)


def dot_t(left, right):
    return lax.dot_general(left, right, (((1,), (1,)), ((), ())), preferred_element_type=f32)


def split(value):
    high = value.astype(bf16)
    return high, (value - high.astype(f32)).astype(bf16)


def wide_left(value):
    return jnp.concatenate(split(value), axis=1)


def full_product(left, right):
    size = right.shape[1]
    pair = jnp.concatenate(split(right), axis=1)
    both = dot(wide_left(left), jnp.concatenate((pair, pair), axis=0))
    return both[:, :size] + both[:, size:]


def exact_right(left, right):
    return dot(wide_left(left), jnp.concatenate((right, right), axis=0))


def invert_unit(stricts, row, col):
    size = stricts[0].shape[0]
    eye = jnp.where(row == col, 1.0, 0.0).astype(f32)
    block = 8
    same = (row // block) == (col // block)
    power = [jnp.where(same, a, 0.0) for a in stricts]
    inverse = [eye - a for a in power]
    for _ in range(2):
        power = [full_product(a, a) for a in power]
        inverse = [x + full_product(x, a) for x, a in zip(inverse, power)]
    while block < size:
        below = ((row // block) % 2 == 1) & ((col // block) == (row // block) - 1)
        joint = [full_product(jnp.where(below, a, 0.0), x) for a, x in zip(stricts, inverse)]
        inverse = [x - full_product(x, j) for x, j in zip(inverse, joint)]
        block *= 2
    return inverse


def delta_body(q_ref, k_ref, v_ref, log_ref, beta_ref, local_ref, reach_ref, state_ref):
    tokens = q_ref.shape[0]
    heads = q_ref.shape[1] // HEAD
    chunks = tokens // CHUNK
    row = lax.broadcasted_iota(jnp.int32, (CHUNK, CHUNK), 0)
    col = lax.broadcasted_iota(jnp.int32, (CHUNK, CHUNK), 1)
    parts = []
    for h in range(heads):
        for c in range(chunks):
            span = slice(c * CHUNK, (c + 1) * CHUNK)
            lanes = slice(h * HEAD, (h + 1) * HEAD)
            key = k_ref[span, lanes]
            query = q_ref[span, lanes]
            log_row = log_ref[0, h : h + 1, span]
            beta_row = beta_ref[0, h : h + 1, span]
            cum_col = jnp.sum(jnp.where(col <= row, log_row, 0.0), axis=1, keepdims=True)
            log_col = jnp.sum(jnp.where(col == row, log_row, 0.0), axis=1, keepdims=True)
            beta_col = jnp.sum(jnp.where(col == row, beta_row, 0.0), axis=1, keepdims=True)
            cum_row = jnp.sum(jnp.where(row <= col, log_col, 0.0), axis=0, keepdims=True)
            inner = dot_t(key, key)
            cross = dot_t(query, key)
            diag = jnp.where(row == col, inner, 0.0)
            key_col = lax.rsqrt(jnp.sum(diag, axis=1, keepdims=True) + EPSILON)
            key_row = lax.rsqrt(jnp.sum(diag, axis=0, keepdims=True) + EPSILON)
            wide_query = query.astype(f32)
            query_col = lax.rsqrt(
                jnp.sum(wide_query * wide_query, axis=1, keepdims=True) + EPSILON
            ) * (1.0 / math.sqrt(HEAD))
            decay = jnp.exp(jnp.where(row >= col, cum_col - cum_row, MASKED)) * key_row
            strict = jnp.where(row > col, decay * inner * (beta_col * key_col), 0.0)
            causal = decay * cross * query_col
            lead_col = jnp.exp(cum_col)
            last = cum_col[CHUNK - 1 : CHUNK, :]
            parts.append(
                dict(
                    key=key,
                    query=query,
                    strict=strict,
                    causal=causal,
                    u_row=beta_row,
                    y_row=beta_row * jnp.exp(cum_row) * key_row,
                    out_col=lead_col * query_col,
                    trail_col=jnp.exp(last - cum_col) * key_col,
                    whole=jnp.exp(last),
                    value=v_ref[span, lanes],
                )
            )
    inverses = invert_unit([p["strict"] for p in parts], row, col)
    for p, inverse in zip(parts, inverses):
        p["u"] = exact_right(inverse * p["u_row"], p["value"])
        p["y"] = exact_right(inverse * p["y_row"], p["key"])
    eye = jnp.where(row == col, 1.0, 0.0).astype(f32)
    states = [jnp.concatenate((jnp.zeros((HEAD, HEAD), f32), eye), axis=1)] * heads
    zero = jnp.zeros((CHUNK, HEAD), f32)
    for c in range(chunks):
        for h in range(heads):
            p = parts[h * chunks + c]
            span = slice(c * CHUNK, (c + 1) * CHUNK)
            lanes = slice(h * HEAD, (h + 1) * HEAD)
            state = states[h]
            high, low = split(state)
            wide = jnp.concatenate((high, low), axis=0)
            y_wide = wide_left(p["y"])
            moved = dot(y_wide, jnp.concatenate((high, high), axis=0)) + dot(
                y_wide[:, :HEAD], low
            )
            weighted = jnp.concatenate((p["u"], zero), axis=1) - moved
            seen = dot(jnp.concatenate((p["query"], p["query"]), axis=1), wide)
            near = weighted.astype(bf16)
            result = p["out_col"] * seen + dot(
                wide_left(p["causal"]), jnp.concatenate((near, near), axis=0)
            )
            local_ref[span, lanes] = result[:, :HEAD]
            reach_ref[span, lanes] = result[:, HEAD:].astype(bf16)
            key_t = p["key"].T
            kept = jnp.concatenate(split(weighted * p["trail_col"]), axis=0)
            states[h] = p["whole"] * state + dot(jnp.concatenate((key_t, key_t), axis=1), kept)
    for h in range(heads):
        state_ref[h, :HEAD, :] = states[h][:, :HEAD].T
        state_ref[h, HEAD:, :] = states[h][:, HEAD:].T


def delta_local(query, key, value, log_decay, beta_gate, heads_step=2):
    tokens, width = query.shape
    heads = width // HEAD
    steps = heads // heads_step
    lanes = heads_step * HEAD
    gates = pl.BlockSpec((1, heads_step, tokens), lambda i: (i, 0, 0))
    rows = pl.BlockSpec((tokens, lanes), lambda i: (0, i))
    return pl.pallas_call(
        delta_body,
        grid=(steps,),
        in_specs=[rows, rows, rows, gates, gates],
        out_specs=[
            rows,
            rows,
            pl.BlockSpec((heads_step, 2 * HEAD, HEAD), lambda i: (i, 0, 0)),
        ],
        out_shape=[
            jax.ShapeDtypeStruct((tokens, width), f32),
            jax.ShapeDtypeStruct((tokens, width), bf16),
            jax.ShapeDtypeStruct((heads, 2 * HEAD, HEAD), f32),
        ],
        name="delta_local",
        compiler_params=pltpu.CompilerParams(dimension_semantics=("arbitrary",)),
    )(
        query,
        key,
        value,
        log_decay.reshape(steps, heads_step, tokens),
        beta_gate.reshape(steps, heads_step, tokens),
    )


def row_product(left, right):
    high, low = split(right)
    wide = wide_left(left)
    return dot(wide, jnp.concatenate((high, high), axis=0)) + dot(wide[:, :HEAD], low)


def pack_body(pair_ref, whole_ref, out_ref):
    heads = pair_ref.shape[1]
    quarter = HEAD // 4
    row = lax.broadcasted_iota(jnp.int32, (HEAD, HEAD), 0)
    col = lax.broadcasted_iota(jnp.int32, (HEAD, HEAD), 1)
    for h in range(heads):
        joined = row_product(pair_ref[0, h], pair_ref[1, h, HEAD:, :])
        source = joined[:HEAD] + pair_ref[1, h, :HEAD, :]
        scale = whole_ref[0, h : h + 1, :].astype(bf16)
        transit = joined[HEAD:] - jnp.where(row == col, scale.astype(f32), 0.0)
        transit = transit.astype(bf16)
        source = source.astype(bf16)
        for piece in range(4):
            index = h * 4 + piece
            out_ref[index, :HEAD, :] = transit
            out_ref[index, HEAD : HEAD + quarter, :] = source[
                piece * quarter : (piece + 1) * quarter
            ]
            out_ref[index, HEAD + quarter :, :] = jnp.broadcast_to(scale, (16, HEAD))


def relay_body(message_ref, out_ref):
    quarter = HEAD // 4
    carried = jnp.zeros((quarter, HEAD), f32)
    members = message_ref.shape[0]
    for m in range(members):
        out_ref[m] = carried.astype(bf16)
        if m + 1 < members:
            transit = message_ref[m, :HEAD, :]
            source = message_ref[m, HEAD : HEAD + quarter, :].astype(f32)
            scale = message_ref[m, HEAD + quarter : HEAD + quarter + 1, :].astype(f32)
            carried = exact_right(carried, transit) + carried * scale + source


def unpack_body(start_ref, pair_ref, out_ref):
    heads = start_ref.shape[0]
    for h in range(heads):
        first = start_ref[h].astype(f32)
        out_ref[0, h] = first
        out_ref[1, h] = row_product(first, pair_ref[0, h, HEAD:, :]) + pair_ref[0, h, :HEAD, :]


def finish_body(reach_ref, local_ref, state_ref, out_ref):
    heads = state_ref.shape[0]
    for h in range(heads):
        lanes = slice(h * HEAD, (h + 1) * HEAD)
        state = state_ref[h]
        out_ref[:, lanes] = (
            local_ref[:, lanes] + dot_t(reach_ref[:, lanes], state.astype(bf16))
        ).astype(bf16)


def attend_body(first_ref, query_ref, own_ref, near_ref, far_ref, out_ref, kv_ref):
    tokens = own_ref.shape[0]
    block = query_ref.shape[0]
    group = query_ref.shape[1] // HEAD
    reach = WINDOW + block
    step = pl.program_id(1)

    @pl.when(step == 0)
    def _():
        for kv in range(2):
            kv_ref[kv, :tokens, :] = far_ref[:, kv * HEAD : (kv + 1) * HEAD]
            kv_ref[kv, tokens : 2 * tokens, :] = near_ref[:, kv * HEAD : (kv + 1) * HEAD]
            kv_ref[kv, 2 * tokens :, :] = own_ref[:, kv * HEAD : (kv + 1) * HEAD]

    begin = pl.multiple_of(step * block, block)
    keys = kv_ref[0, pl.ds(begin, reach), :]
    values = kv_ref[1, pl.ds(begin, reach), :]
    row = lax.broadcasted_iota(jnp.int32, (block, block), 0)
    col = lax.broadcasted_iota(jnp.int32, (block, block), 1)
    position = lax.broadcasted_iota(jnp.int32, (1, reach), 1) + begin
    bias = jnp.where(position >= first_ref[0], 0.0, MASKED)
    head_bias = jnp.where(col > row, 0.0, MASKED)
    tail_bias = jnp.where(col <= row, 0.0, MASKED)
    scale = 1.0 / math.sqrt(HEAD)
    for r in range(group):
        lanes = slice(r * HEAD, (r + 1) * HEAD)
        scores = dot_t(query_ref[:, lanes], keys)
        scores = jnp.concatenate(
            (
                scores[:, :block] + head_bias,
                scores[:, block:WINDOW],
                scores[:, WINDOW:] + tail_bias,
            ),
            axis=1,
        )
        scores = scores + bias
        top = jnp.max(scores, axis=1, keepdims=True)
        unnormed = jnp.exp((scores - top) * scale)
        total = jnp.sum(unnormed, axis=1, keepdims=True)
        mixed = dot(unnormed.astype(bf16), values)
        out_ref[:, lanes] = (mixed / total).astype(bf16)


def attend(first, query, own, near, far, block=128):
    tokens, width = query.shape
    groups = own.shape[1] // (2 * HEAD)
    lanes = width // groups
    kv = pl.BlockSpec((tokens, 2 * HEAD), lambda g, i, _: (0, g))
    rows = pl.BlockSpec((block, lanes), lambda g, i, _: (i, g))
    return pl.pallas_call(
        attend_body,
        grid_spec=pltpu.PrefetchScalarGridSpec(
            num_scalar_prefetch=1,
            grid=(groups, tokens // block),
            in_specs=[rows, kv, kv, kv],
            out_specs=rows,
            scratch_shapes=[pltpu.VMEM((2, WINDOW + tokens, HEAD), bf16)],
        ),
        out_shape=jax.ShapeDtypeStruct((tokens, width), bf16),
        name="attend",
        compiler_params=pltpu.CompilerParams(dimension_semantics=("arbitrary", "arbitrary")),
    )(first, query, own, near, far)


def simple_call(body, shape, name, *operands):
    return pl.pallas_call(body, out_shape=shape, name=name)(*operands)


def ring(block, axes, distance, size):
    return lax.ppermute(block, axes, [(i, (i + distance) % size) for i in range(size)])


CTX = ("y", "x", "core")
CHIPS = ("y", "x")


def local(
    attn_query, attn_key, attention_value, delta_query, delta_key, delta_value, log_decay, beta_gate
):
    tokens = attn_query.shape[0]
    size = lax.axis_size(CTX)
    index = lax.axis_index(CTX)
    kv_heads = attn_key.shape[1]
    key_value = jnp.stack((attn_key, attention_value), axis=2).reshape(tokens, -1)
    far = ring(key_value, CTX, 2, size)
    near = ring(key_value, CTX, 1, size)

    def rows(tensor):
        return tensor.reshape(tokens, -1)

    local_out, reach, state = delta_local(
        rows(delta_query), rows(delta_key), rows(delta_value), log_decay, beta_gate
    )
    heads = state.shape[0]
    half = heads // 2
    core = lax.axis_index("core")
    pair = lax.all_to_all(
        state.reshape(2, half, 2 * HEAD, HEAD), "core", split_axis=0, concat_axis=0, tiled=True
    )
    total = jnp.exp(jnp.sum(log_decay, axis=1))
    total = lax.all_to_all(
        jnp.broadcast_to(total.reshape(2, half, 1), (2, half, HEAD)),
        "core",
        split_axis=0,
        concat_axis=0,
        tiled=True,
    )
    message = simple_call(
        pack_body,
        jax.ShapeDtypeStruct((half * 4, HEAD + HEAD // 4 + 16, HEAD), bf16),
        "pack",
        pair,
        (total[0] * total[1])[None],
    )
    gathered = lax.all_to_all(message, CHIPS, split_axis=0, concat_axis=0, tiled=True)
    first = jnp.maximum(0, WINDOW - tokens * index).astype(jnp.int32).reshape(1)
    attended = attend(first, rows(attn_query), key_value, near, far)
    attn_out = lax.all_to_all(attended, "head", split_axis=0, concat_axis=1, tiled=True)
    starts = simple_call(
        relay_body,
        jax.ShapeDtypeStruct((half * 4, HEAD // 4, HEAD), bf16),
        "relay",
        gathered,
    )
    returned = lax.all_to_all(starts, CHIPS, split_axis=0, concat_axis=0, tiled=True)
    both = simple_call(
        unpack_body,
        jax.ShapeDtypeStruct((2, half, HEAD, HEAD), f32),
        "unpack",
        returned.reshape(half, HEAD, HEAD),
        pair,
    )
    incoming = lax.all_to_all(both, "core", split_axis=0, concat_axis=0, tiled=True)
    delta = simple_call(
        finish_body,
        jax.ShapeDtypeStruct(reach.shape, bf16),
        "finish",
        reach,
        local_out,
        incoming.reshape(heads, HEAD, HEAD),
    )
    delta_out = lax.all_to_all(delta, "head", split_axis=0, concat_axis=1, tiled=True)
    return (attn_out, delta_out)


def solution(mesh):
    fine = Mesh(mesh.devices.reshape(4, 4, 2, 4), ("y", "x", "core", "head"))
    cut = P(CTX, "head", None)
    gate = P("head", CTX)
    out = P((*CTX, "head"), None)
    return jax.shard_map(
        local,
        mesh=fine,
        in_specs=(cut,) * 6 + (gate, gate),
        out_specs=(out, out),
        check_vma=False,
    )
```

time: 742 us -> 150 us (0.20)
  the two profiles are of different devices: /device:TPU:16 before, /device:TPU:0 now
where the time goes in v1:
time: 150 us; the launch traced here: 149 us
  Pallas kernels  51.8 us (35%)
  waiting for transfers between devices  39 us (26%)
  starting transfers between devices  28.3 us (19%)
  local copies, waits for them, and re-layouts  14.7 us (10%)
  blocking collectives  11.7 us (8%)
  other arithmetic  2.3 us (2%)
    pallas_call x1, Pallas kernels, delta_local(): pl.pallas_call(delta_body, grid=(steps,), in_specs=[rows, rows, rows, gat...  23.5 us
    pallas_call x1, Pallas kernels, attend(): pl.pallas_call(attend_body, grid_spec=pltpu.PrefetchScalarGridSpec(num_sc...  16.5 us
    all_to_all x1, waiting for transfers between devices, local(): lax.all_to_all(delta, 'head', split_axis=0, concat_axis=1, tiled=True)  13.4 us
    all_to_all x1, waiting for transfers between devices, local(): lax.all_to_all(attended, 'head', split_axis=0, concat_axis=1, tiled=True)  12 us
    pallas_call x4, Pallas kernels, simple_call(): return pl.pallas_call(body, out_shape=shape, name=name)(*operands)  11.8 us
    all_to_all x1, blocking collectives, local(): lax.all_to_all(both, 'core', split_axis=0, concat_axis=0, tiled=True)  11.7 us
    all_to_all x1, waiting for transfers between devices, local(): lax.all_to_all(message, CHIPS, split_axis=0, concat_axis=0, tiled=True)  11.1 us
    all_to_all x1, starting transfers between devices, local(): lax.all_to_all(message, CHIPS, split_axis=0, concat_axis=0, tiled=True)  7.14 us
  transfers between devices with their start and end apart: 8, of which 6 were waited for; matrix products, arithmetic and copies ran while one was open for 7% of the time, Pallas kernels for 32%

profile of v1, /device:TPU:0, one launch (start us, length us, event | category | flops | bytes accessed | tf_op | source)
XLA Modules:
  0.0 148.7 jit_solution(10677702700347346120)
XLA Ops:
  0.6 0.0 copy-start.11
  0.6 0.0 copy-start.5
  0.7 0.0 copy-start.4
  0.7 1.0 reduce_sum.9
  1.7 0.1 exp.11
  1.7 0.7 broadcast_in_dim.2
  2.4 3.2 %all-to-all-start.2 = ((f32[2,4,128]{2,1,0:T(4,128)}), f32[2,4,128]{2,1,0:T(4,128)S(1)}, u32[]{:S(2)}, u32[]{:S(2)}) async-start(f32[2,4,128]{2,1,0:T(4,128)} %broadcast_in_dim.2), calls=%async_computation.2 | async-start | bytes 8192 | tf_op jit(solution)/shard_map/all_to_all | solution.py:338
  5.6 1.3 reshape.56.log_ref
  7.0 2.5 %copy.23 = bf16[64,8,8,128]{3,1,2,0:T(8,128)(2,1)} copy(bf16[64,8,8,128]{3,2,1,0:T(8,128)(2,1)} %bitcast.34) | data formatting | bytes 2097152
  9.4 0.0 copy-done.11
  9.4 0.6 reshape.57.beta_ref
  10.0 0.0 copy-done.5
  10.0 0.0 copy-done.4
  10.0 1.9 %copy_bitcast_fusion = (bf16[512,1024]{1,0:T(8,128)(2,1)}, bf16[512,1024]{1,0:T(8,128)(2,1)}) fusion(bf16[64,8,8,128]{3,2,1,0:T(8,128)(2,1)S(1)} %bitcast.39, bf16[64,8,8,128]{3,2,1,0:T(8,128)(2,1)S(1)} %bitcast.40), kind=kLoop, calls=%fused_computation | loop fusion | bytes 4194304 | tf_op jit(solution)/shard_map/reshape | solution.py:326
  11.9 23.5 %delta_local.1 = (f32[512,1024]{1,0:T(8,128)}, bf16[512,1024]{1,0:T(8,128)(2,1)}, f32[8,256,128]{2,1,0:T(8,128)}) custom-call(bf16[512,1024]{1,0:T(8,128)(2,1)} %bitcast.28, bf16[512,1024]{1,0:T(8,128)(2,1)} %get-tuple-element.9.k_ref, bf16[512,1024]{1,0:T(8,128)(2,1)} %get-tuple-element.8.v_ref, f32[4,2,512]{2,1,0:T(2,128)} %reshape.56.log_ref, ...), custom_call_target="tpu_custom_call" | custom-call | tf_op jit(solution)/shard_map/delta_local/pallas_call | solution.py:155
  35.4 0.0 all-to-all-done.2
  35.4 3.6 %all-to-all-start.1 = ((f32[2,4,256,128]{3,2,1,0:T(8,128)}), f32[2,4,256,128]{3,2,1,0:T(8,128)S(1)}, u32[]{:S(2)}, u32[]{:S(2)}) async-start(f32[2,4,256,128]{3,2,1,0:T(8,128)} %bitcast.36), calls=%async_computation.1 | async-start | bytes 2097152 | tf_op jit(solution)/shard_map/all_to_all | solution.py:334
  39.0 0.0 copy-start.9
  39.0 0.0 copy-start.10
  39.0 0.6 slice_multiply_fusion.whole_ref
  39.6 1.5 %all-to-all-done.1.pair_ref = f32[2,4,256,128]{3,2,1,0:T(8,128)S(1)} async-done(((f32[2,4,256,128]{3,2,1,0:T(8,128)}), f32[2,4,256,128]{3,2,1,0:T(8,128)S(1)}, u32[]{:S(2)}, u32[]{:S(2)}) %all-to-all-start.1) | async-done | bytes 1048608 | tf_op jit(solution)/shard_map/all_to_all | solution.py:334
  41.1 0.0 copy-start
  41.1 1.0 copy-done
  42.1 2.4 %pack.1 = bf16[16,176,128]{2,1,0:T(8,128)(2,1)} custom-call(f32[2,4,256,128]{3,2,1,0:T(8,128)} %copy-done, f32[1,4,128]{2,1,0:T(4,128)} %slice_multiply_fusion.whole_ref), custom_call_target="tpu_custom_call" | custom-call | tf_op jit(solution)/shard_map/pack/pallas_call | solution.py:303
  44.5 7.1 %all-to-all-start.3 = ((bf16[16,176,128]{2,1,0:T(8,128)(2,1)}), bf16[16,176,128]{2,1,0:T(8,128)(2,1)S(1)}, u32[]{:S(2)}, u32[]{:S(2)}) async-start(bf16[16,176,128]{2,1,0:T(8,128)(2,1)} %pack.1), calls=%async_computation.3 | async-start | bytes 1441792 | tf_op jit(solution)/shard_map/all_to_all | solution.py:352
  51.7 0.0 copy-done.9
  51.7 0.0 copy-done.10
  51.7 0.0 copy-start.3
  51.7 0.7 pad_maximum_fusion
  52.5 0.8 copy.10
  53.3 0.2 reshape.52.own_ref
  53.5 0.0 copy-start.2
  53.5 0.1 collective-permute-start
  53.6 2.0 %collective-permute-start.1 = (bf16[512,512]{1,0:T(8,128)(2,1)S(1)}, bf16[512,512]{1,0:T(8,128)(2,1)S(1)}, u32[]{:S(2)}, u32[]{:S(2)}) collective-permute-start(bf16[512,512]{1,0:T(8,128)(2,1)S(1)} %reshape.52.own_ref), channel_id=1, source_target_pairs={{0,8},{4,12},{8,16},{12,20},{16,24},{20,28},{24,32},{28,36},{32,40... | collective-permute-start | bytes 1572872 | tf_op jit(solution)/shard_map/ppermute | solution.py:307
  55.6 11.1 %all-to-all-done.3.message_ref = bf16[16,176,128]{2,1,0:T(8,128)(2,1)S(1)} async-done(((bf16[16,176,128]{2,1,0:T(8,128)(2,1)}), bf16[16,176,128]{2,1,0:T(8,128)(2,1)S(1)}, u32[]{:S(2)}, u32[]{:S(2)}) %all-to-all-start.3) | async-done | bytes 720928 | tf_op jit(solution)/shard_map/all_to_all | solution.py:352
  66.7 0.0 copy-start.1
  66.7 0.9 copy-done.1
  67.5 3.6 %relay.1 = bf16[16,32,128]{2,1,0:T(8,128)(2,1)} custom-call(bf16[16,176,128]{2,1,0:T(8,128)(2,1)} %copy-done.1), custom_call_target="tpu_custom_call" | custom-call | tf_op jit(solution)/shard_map/relay/pallas_call | solution.py:303
  71.2 3.5 %all-to-all-start.4 = ((bf16[16,32,128]{2,1,0:T(8,128)(2,1)}), bf16[16,32,128]{2,1,0:T(8,128)(2,1)S(1)}, u32[]{:S(2)}, u32[]{:S(2)}) async-start(bf16[16,32,128]{2,1,0:T(8,128)(2,1)} %relay.1), calls=%async_computation.4 | async-start | bytes 262144 | tf_op jit(solution)/shard_map/all_to_all | solution.py:362
  74.7 0.0 copy-done.3
  74.7 1.2 copy.24
  75.9 0.2 collective-permute-done.near_ref
  76.1 0.0 copy-start.6
  76.1 0.8 collective-permute-done.1.far_ref
  76.9 0.0 copy-start.7
  76.9 0.0 copy-done.2
  76.9 0.0 copy-done.6
  76.9 0.8 copy-done.7
  77.7 16.5 %attend.1 = bf16[512,1024]{1,0:T(8,128)(2,1)} custom-call(s32[1]{0:T(128)} %bitcast.first_ref, bf16[512,1024]{1,0:T(8,128)(2,1)} %bitcast.31, bf16[512,512]{1,0:T(8,128)(2,1)} %copy-done.2, bf16[512,512]{1,0:T(8,128)(2,1)} %copy-done.6, bf16[512,512]{1,0:T(8,128)(2,1)} %copy-done.7), custom_call_target="tpu_custom_call" | custom-call | tf_op jit(solution)/shard_map/attend/pallas_call | solution.py:287
  94.2 0.0 all-to-all-done.4
  94.2 0.0 copy-start.8
  94.2 0.7 copy-done.8
  94.9 2.4 %unpack.1 = f32[2,4,128,128]{3,2,1,0:T(8,128)} custom-call(bf16[4,128,128]{2,1,0:T(8,128)(2,1)} %bitcast.41, f32[2,4,256,128]{3,2,1,0:T(8,128)} %copy-done), custom_call_target="tpu_custom_call" | custom-call | tf_op jit(solution)/shard_map/unpack/pallas_call | solution.py:303
  97.2 11.7 %all_to_all.63 = f32[2,4,128,128]{3,2,1,0:T(8,128)} all-to-all(f32[2,4,128,128]{3,2,1,0:T(8,128)} %unpack.1), channel_id=1, replica_groups=mesh['y'=4,'x'=4,'core'=2,'head'=4] {'core'}, dimensions={0} | all-to-all | bytes 1048576 | tf_op jit(solution)/shard_map/all_to_all | solution.py:370
  108.9 5.3 %all-to-all-start = ((bf16[4,128,1024]{2,1,0:T(8,128)(2,1)}), bf16[4,128,1024]{2,1,0:T(8,128)(2,1)S(1)}, u32[]{:S(2)}, u32[]{:S(2)}) async-start(bf16[4,128,1024]{2,1,0:T(8,128)(2,1)} %bitcast.3), calls=%async_computation | async-start | bytes 2097152 | tf_op jit(solution)/shard_map/all_to_all | solution.py:355
  114.2 3.4 %finish.1 = bf16[512,1024]{1,0:T(8,128)(2,1)} custom-call(bf16[512,1024]{1,0:T(8,128)(2,1)} %get-tuple-element.5.reach_ref, f32[512,1024]{1,0:T(8,128)} %get-tuple-element.6.local_ref, f32[8,128,128]{2,1,0:T(8,128)} %bitcast.33), custom_call_target="tpu_custom_call" | custom-call | tf_op jit(solution)/shard_map/finish/pallas_call | solution.py:303
  117.6 12.0 %all-to-all-done = bf16[4,128,1024]{2,1,0:T(8,128)(2,1)S(1)} async-done(((bf16[4,128,1024]{2,1,0:T(8,128)(2,1)}), bf16[4,128,1024]{2,1,0:T(8,128)(2,1)S(1)}, u32[]{:S(2)}, u32[]{:S(2)}) %all-to-all-start) | async-done | bytes 1048608 | tf_op jit(solution)/shard_map/all_to_all | solution.py:355
  129.6 3.5 %all-to-all-start.6 = ((bf16[4,128,1024]{2,1,0:T(8,128)(2,1)}), bf16[4,128,1024]{2,1,0:T(8,128)(2,1)S(1)}, u32[]{:S(2)}, u32[]{:S(2)}) async-start(bf16[4,128,1024]{2,1,0:T(8,128)(2,1)} %bitcast.32), calls=%async_computation.6 | async-start | bytes 2097152 | tf_op jit(solution)/shard_map/all_to_all | solution.py:379
  133.1 1.1 copy.13
  134.2 13.4 %all-to-all-done.6 = bf16[4,128,1024]{2,1,0:T(8,128)(2,1)S(1)} async-done(((bf16[4,128,1024]{2,1,0:T(8,128)(2,1)}), bf16[4,128,1024]{2,1,0:T(8,128)(2,1)S(1)}, u32[]{:S(2)}, u32[]{:S(2)}) %all-to-all-start.6) | async-done | bytes 1048608 | tf_op jit(solution)/shard_map/all_to_all | solution.py:379
  147.6 1.1 copy.14
  (1 shorter events, 0.0 us)
Async XLA Ops:
  0.6 8.8 %copy-start.11 = (f32[8,512]{1,0:T(8,128)S(1)}, f32[8,512]{1,0:T(8,128)}, u32[]{:S(2)}) copy-start(f32[8,512]{1,0:T(8,128)} %param.15) | copy-start | bytes 49156
  0.6 9.4 %copy-start.5 = (bf16[512,8,128]{2,1,0:T(8,128)(2,1)S(1)}, bf16[512,8,128]{2,1,0:T(8,128)(2,1)}, u32[]{:S(2)}) copy-start(bf16[512,8,128]{2,1,0:T(8,128)(2,1)} %param.12) | copy-start | bytes 3145732
  0.7 9.4 %copy-start.4 = (bf16[512,8,128]{2,1,0:T(8,128)(2,1)S(1)}, bf16[512,8,128]{2,1,0:T(8,128)(2,1)}, u32[]{:S(2)}) copy-start(bf16[512,8,128]{2,1,0:T(8,128)(2,1)} %param.13) | copy-start | bytes 3145732
  2.4 33.0 %all-to-all-start.2 = ((f32[2,4,128]{2,1,0:T(4,128)}), f32[2,4,128]{2,1,0:T(4,128)S(1)}, u32[]{:S(2)}, u32[]{:S(2)}) async-start(f32[2,4,128]{2,1,0:T(4,128)} %broadcast_in_dim.2), calls=%async_computation.2 | async-start | bytes 8192 | tf_op jit(solution)/shard_map/all_to_all | solution.py:338
  35.4 5.7 %all-to-all-start.1 = ((f32[2,4,256,128]{3,2,1,0:T(8,128)}), f32[2,4,256,128]{3,2,1,0:T(8,128)S(1)}, u32[]{:S(2)}, u32[]{:S(2)}) async-start(f32[2,4,256,128]{3,2,1,0:T(8,128)} %bitcast.36), calls=%async_computation.1 | async-start | bytes 2097152 | tf_op jit(solution)/shard_map/all_to_all | solution.py:334
  39.0 12.7 %copy-start.9 = (bf16[512,2,128]{2,1,0:T(2,128)(2,1)S(1)}, bf16[512,2,128]{2,1,0:T(2,128)(2,1)}, u32[]{:S(2)}) copy-start(bf16[512,2,128]{2,1,0:T(2,128)(2,1)} %param.10) | copy-start | bytes 786436
  39.0 12.7 %copy-start.10 = (bf16[512,2,128]{2,1,0:T(2,128)(2,1)S(1)}, bf16[512,2,128]{2,1,0:T(2,128)(2,1)}, u32[]{:S(2)}) copy-start(bf16[512,2,128]{2,1,0:T(2,128)(2,1)} %param.9) | copy-start | bytes 786436
  41.1 1.0 copy-start
  44.5 22.2 %all-to-all-start.3 = ((bf16[16,176,128]{2,1,0:T(8,128)(2,1)}), bf16[16,176,128]{2,1,0:T(8,128)(2,1)S(1)}, u32[]{:S(2)}, u32[]{:S(2)}) async-start(bf16[16,176,128]{2,1,0:T(8,128)(2,1)} %pack.1), calls=%async_computation.3 | async-start | bytes 1441792 | tf_op jit(solution)/shard_map/all_to_all | solution.py:352
  51.7 23.0 %copy-start.3 = (bf16[512,8,128]{2,1,0:T(8,128)(2,1)S(1)}, bf16[512,8,128]{2,1,0:T(8,128)(2,1)}, u32[]{:S(2)}) copy-start(bf16[512,8,128]{2,1,0:T(8,128)(2,1)} %param.8) | copy-start | bytes 3145732
  53.5 23.4 %copy-start.2 = (bf16[512,512]{1,0:T(8,128)(2,1)}, bf16[512,512]{1,0:T(8,128)(2,1)S(1)}, u32[]{:S(2)}) copy-start(bf16[512,512]{1,0:T(8,128)(2,1)S(1)} %reshape.52.own_ref) | copy-start | bytes 1572868
  53.5 22.6 %collective-permute-start = (bf16[512,512]{1,0:T(8,128)(2,1)S(1)}, bf16[512,512]{1,0:T(8,128)(2,1)S(1)}, u32[]{:S(2)}, u32[]{:S(2)}) collective-permute-start(bf16[512,512]{1,0:T(8,128)(2,1)S(1)} %reshape.52.own_ref), channel_id=1, source_target_pairs={{0,4},{4,8},{8,12},{12,16},{16,20},{20,24},{24,28},{28,32},{32,36}... | collective-permute-start | bytes 1572872 | tf_op jit(solution)/shard_map/ppermute | solution.py:307
  53.6 23.3 %collective-permute-start.1 = (bf16[512,512]{1,0:T(8,128)(2,1)S(1)}, bf16[512,512]{1,0:T(8,128)(2,1)S(1)}, u32[]{:S(2)}, u32[]{:S(2)}) collective-permute-start(bf16[512,512]{1,0:T(8,128)(2,1)S(1)} %reshape.52.own_ref), channel_id=1, source_target_pairs={{0,8},{4,12},{8,16},{12,20},{16,24},{20,28},{24,32},{28,36},{32,40... | collective-permute-start | bytes 1572872 | tf_op jit(solution)/shard_map/ppermute | solution.py:307
  66.7 0.9 copy-start.1
  71.2 23.1 %all-to-all-start.4 = ((bf16[16,32,128]{2,1,0:T(8,128)(2,1)}), bf16[16,32,128]{2,1,0:T(8,128)(2,1)S(1)}, u32[]{:S(2)}, u32[]{:S(2)}) async-start(bf16[16,32,128]{2,1,0:T(8,128)(2,1)} %relay.1), calls=%async_computation.4 | async-start | bytes 262144 | tf_op jit(solution)/shard_map/all_to_all | solution.py:362
  76.1 0.8 copy-start.6
  76.9 0.8 copy-start.7
  94.2 0.7 copy-start.8
  108.9 20.7 %all-to-all-start = ((bf16[4,128,1024]{2,1,0:T(8,128)(2,1)}), bf16[4,128,1024]{2,1,0:T(8,128)(2,1)S(1)}, u32[]{:S(2)}, u32[]{:S(2)}) async-start(bf16[4,128,1024]{2,1,0:T(8,128)(2,1)} %bitcast.3), calls=%async_computation | async-start | bytes 2097152 | tf_op jit(solution)/shard_map/all_to_all | solution.py:355
  129.6 18.0 %all-to-all-start.6 = ((bf16[4,128,1024]{2,1,0:T(8,128)(2,1)}), bf16[4,128,1024]{2,1,0:T(8,128)(2,1)S(1)}, u32[]{:S(2)}, u32[]{:S(2)}) async-start(bf16[4,128,1024]{2,1,0:T(8,128)(2,1)} %bitcast.32), calls=%async_computation.6 | async-start | bytes 2097152 | tf_op jit(solution)/shard_map/all_to_all | solution.py:379

commit v2 on v1

v2 whole, which is shorter than its diff:
```python
import math

import jax
import jax.numpy as jnp
from jax import lax
from jax.experimental import pallas as pl
from jax.experimental.pallas import tpu as pltpu
from jax.sharding import Mesh, PartitionSpec as P


WINDOW = 1024
CHUNK = 128
HEAD = 128
EPSILON = 1e-06
MASKED = -1e30
STATE = 2 * HEAD + 8
ONCHIP = pl.BlockSpec(memory_space=pltpu.VMEM)
SCALAR = pl.BlockSpec(memory_space=pltpu.SMEM)

f32 = jnp.float32
bf16 = jnp.bfloat16


def dot(left, right):
    return lax.dot_general(left, right, (((1,), (0,)), ((), ())), preferred_element_type=f32)


def dot_t(left, right):
    return lax.dot_general(left, right, (((1,), (1,)), ((), ())), preferred_element_type=f32)


def split(value):
    high = value.astype(bf16)
    return high, (value - high.astype(f32)).astype(bf16)


def wide_left(value):
    return jnp.concatenate(split(value), axis=1)


def full_product(left, right):
    size = right.shape[1]
    pair = jnp.concatenate(split(right), axis=1)
    both = dot(wide_left(left), jnp.concatenate((pair, pair), axis=0))
    return both[:, :size] + both[:, size:]


def exact_right(left, right):
    return dot(wide_left(left), jnp.concatenate((right, right), axis=0))


def invert_unit(stricts, row, col):
    size = stricts[0].shape[0]
    eye = jnp.where(row == col, 1.0, 0.0).astype(f32)
    block = 8
    same = (row // block) == (col // block)
    power = [jnp.where(same, a, 0.0) for a in stricts]
    inverse = [eye - a for a in power]
    for _ in range(2):
        power = [full_product(a, a) for a in power]
        inverse = [x + full_product(x, a) for x, a in zip(inverse, power)]
    while block < size:
        below = ((row // block) % 2 == 1) & ((col // block) == (row // block) - 1)
        joint = [full_product(jnp.where(below, a, 0.0), x) for a, x in zip(stricts, inverse)]
        inverse = [x - full_product(x, j) for x, j in zip(inverse, joint)]
        block *= 2
    return inverse


def delta_body(base_ref, q_ref, k_ref, v_ref, log_ref, beta_ref, local_ref, reach_ref, state_ref):
    tokens = q_ref.shape[0]
    heads = q_ref.shape[1] // HEAD
    begin = (base_ref[0] + pl.program_id(0)) * heads
    head_index = lax.broadcasted_iota(jnp.int32, log_ref.shape, 0)
    log_rows = [
        jnp.sum(jnp.where(head_index == begin + h, log_ref[...], 0.0), axis=0, keepdims=True)
        for h in range(heads)
    ]
    beta_rows = [
        jnp.sum(jnp.where(head_index == begin + h, beta_ref[...], 0.0), axis=0, keepdims=True)
        for h in range(heads)
    ]
    chunks = tokens // CHUNK
    row = lax.broadcasted_iota(jnp.int32, (CHUNK, CHUNK), 0)
    col = lax.broadcasted_iota(jnp.int32, (CHUNK, CHUNK), 1)
    parts = []
    for h in range(heads):
        for c in range(chunks):
            span = slice(c * CHUNK, (c + 1) * CHUNK)
            lanes = slice(h * HEAD, (h + 1) * HEAD)
            key = k_ref[span, lanes]
            query = q_ref[span, lanes]
            log_row = log_rows[h][:, span]
            beta_row = beta_rows[h][:, span]
            cum_col = jnp.sum(jnp.where(col <= row, log_row, 0.0), axis=1, keepdims=True)
            log_col = jnp.sum(jnp.where(col == row, log_row, 0.0), axis=1, keepdims=True)
            beta_col = jnp.sum(jnp.where(col == row, beta_row, 0.0), axis=1, keepdims=True)
            cum_row = jnp.sum(jnp.where(row <= col, log_col, 0.0), axis=0, keepdims=True)
            inner = dot_t(key, key)
            cross = dot_t(query, key)
            diag = jnp.where(row == col, inner, 0.0)
            key_col = lax.rsqrt(jnp.sum(diag, axis=1, keepdims=True) + EPSILON)
            key_row = lax.rsqrt(jnp.sum(diag, axis=0, keepdims=True) + EPSILON)
            wide_query = query.astype(f32)
            query_col = lax.rsqrt(
                jnp.sum(wide_query * wide_query, axis=1, keepdims=True) + EPSILON
            ) * (1.0 / math.sqrt(HEAD))
            decay = jnp.exp(jnp.where(row >= col, cum_col - cum_row, MASKED)) * key_row
            strict = jnp.where(row > col, decay * inner * (beta_col * key_col), 0.0)
            causal = decay * cross * query_col
            lead_col = jnp.exp(cum_col)
            last = cum_col[CHUNK - 1 : CHUNK, :]
            parts.append(
                dict(
                    key=key,
                    query=query,
                    strict=strict,
                    causal=causal,
                    u_row=beta_row,
                    y_row=beta_row * jnp.exp(cum_row) * key_row,
                    out_col=lead_col * query_col,
                    trail_col=jnp.exp(last - cum_col) * key_col,
                    whole=jnp.exp(last),
                    value=v_ref[span, lanes],
                )
            )
    inverses = invert_unit([p["strict"] for p in parts], row, col)
    for p, inverse in zip(parts, inverses):
        p["u"] = exact_right(inverse * p["u_row"], p["value"])
        p["y"] = exact_right(inverse * p["y_row"], p["key"])
    eye = jnp.where(row == col, 1.0, 0.0).astype(f32)
    states = [jnp.concatenate((jnp.zeros((HEAD, HEAD), f32), eye), axis=1)] * heads
    zero = jnp.zeros((CHUNK, HEAD), f32)
    for c in range(chunks):
        for h in range(heads):
            p = parts[h * chunks + c]
            span = slice(c * CHUNK, (c + 1) * CHUNK)
            lanes = slice(h * HEAD, (h + 1) * HEAD)
            state = states[h]
            high, low = split(state)
            wide = jnp.concatenate((high, low), axis=0)
            y_wide = wide_left(p["y"])
            moved = dot(y_wide, jnp.concatenate((high, high), axis=0)) + dot(
                y_wide[:, :HEAD], low
            )
            weighted = jnp.concatenate((p["u"], zero), axis=1) - moved
            seen = dot(jnp.concatenate((p["query"], p["query"]), axis=1), wide)
            near, rest = split(weighted)
            causal = wide_left(p["causal"])
            result = (
                p["out_col"] * seen
                + dot(causal, jnp.concatenate((near, near), axis=0))
                + dot(causal[:, :HEAD], rest)
            )
            local_ref[span, lanes] = result[:, :HEAD]
            reach_ref[span, lanes] = result[:, HEAD:].astype(bf16)
            key_t = p["key"].T
            kept = jnp.concatenate(split(weighted * p["trail_col"]), axis=0)
            states[h] = p["whole"] * state + dot(jnp.concatenate((key_t, key_t), axis=1), kept)
    for h in range(heads):
        place = pl.program_id(0) * heads + h
        state_ref[place, :HEAD, :] = states[h][:, :HEAD].T
        state_ref[place, HEAD : 2 * HEAD, :] = states[h][:, HEAD:].T
        whole = jnp.exp(jnp.sum(log_rows[h], axis=1, keepdims=True))
        state_ref[place, 2 * HEAD :, :] = jnp.broadcast_to(whole, (8, HEAD))


def delta_local(base, query, key, value, log_decay, beta_gate, heads, heads_step=2):
    tokens = query.shape[0]
    steps = heads // heads_step
    lanes = heads_step * HEAD
    gates = pl.BlockSpec(log_decay.shape, lambda i, s: (0, 0))
    rows = pl.BlockSpec((tokens, lanes), lambda i, s: (0, s[0] + i))
    outs = pl.BlockSpec((tokens, lanes), lambda i, s: (0, i))
    return pl.pallas_call(
        delta_body,
        grid_spec=pltpu.PrefetchScalarGridSpec(
            num_scalar_prefetch=1,
            grid=(steps,),
            in_specs=[rows, rows, rows, gates, gates],
            out_specs=[
                outs,
                outs,
                ONCHIP,
            ],
        ),
        out_shape=[
            jax.ShapeDtypeStruct((tokens, heads * HEAD), f32),
            jax.ShapeDtypeStruct((tokens, heads * HEAD), bf16),
            jax.ShapeDtypeStruct((heads, STATE, HEAD), f32),
        ],
        name="delta_local",
        compiler_params=pltpu.CompilerParams(dimension_semantics=("arbitrary",)),
    )(base, query, key, value, log_decay, beta_gate)


def row_product(left, right):
    high, low = split(right)
    wide = wide_left(left)
    return dot(wide, jnp.concatenate((high, high), axis=0)) + dot(wide[:, :HEAD], low)


def pack_body(core_ref, own_ref, other_ref, out_ref, early_ref):
    heads = own_ref.shape[0]
    quarter = HEAD // 4
    row = lax.broadcasted_iota(jnp.int32, (HEAD, HEAD), 0)
    col = lax.broadcasted_iota(jnp.int32, (HEAD, HEAD), 1)
    leads = core_ref[0] == 0
    for h in range(heads):
        own = own_ref[h]
        other = other_ref[h]
        early = jnp.where(leads, own, other)
        late = jnp.where(leads, other, own)
        early_ref[h] = early
        joined = row_product(early[: 2 * HEAD], late[HEAD : 2 * HEAD])
        source = (joined[:HEAD] + late[:HEAD]).astype(bf16)
        scale = (early[2 * HEAD :] * late[2 * HEAD :])[:1].astype(bf16)
        transit = joined[HEAD:] - jnp.where(row == col, scale.astype(f32), 0.0)
        transit = transit.astype(bf16)
        for piece in range(4):
            index = h * 4 + piece
            out_ref[index, :HEAD, :] = transit
            out_ref[index, HEAD : HEAD + quarter, :] = source[
                piece * quarter : (piece + 1) * quarter
            ]
            out_ref[index, HEAD + quarter :, :] = jnp.broadcast_to(scale, (16, HEAD))


def relay_body(message_ref, out_ref):
    quarter = HEAD // 4
    carried = jnp.zeros((quarter, HEAD), f32)
    members = message_ref.shape[0]
    for m in range(members):
        out_ref[m] = carried.astype(bf16)
        if m + 1 < members:
            transit = message_ref[m, :HEAD, :]
            source = message_ref[m, HEAD : HEAD + quarter, :].astype(f32)
            scale = message_ref[m, HEAD + quarter : HEAD + quarter + 1, :].astype(f32)
            carried = exact_right(carried, transit) + carried * scale + source


def unpack_body(core_ref, start_ref, early_ref, keep_ref, send_ref):
    leads = core_ref[0] == 0
    for h in range(start_ref.shape[0]):
        start = start_ref[h]
        first = start.astype(f32)
        early = early_ref[h]
        second = row_product(first, early[HEAD : 2 * HEAD]) + early[:HEAD]
        keep_ref[h] = jnp.where(leads, first, second).astype(bf16)
        send_ref[h] = jnp.where(leads, second, first).astype(bf16)


def finish_body(reach_ref, local_ref, state_ref, out_ref):
    for h in range(state_ref.shape[0]):
        lanes = slice(h * HEAD, (h + 1) * HEAD)
        out_ref[:, lanes] = (
            local_ref[:, lanes] + dot_t(reach_ref[:, lanes], state_ref[h])
        ).astype(bf16)


def attend_body(first_ref, turn_ref, query_ref, own_ref, near_ref, far_ref, *rest):
    *out_refs, kv_ref = rest
    tokens = own_ref.shape[0]
    block = query_ref.shape[0]
    group = query_ref.shape[1] // HEAD
    reach = WINDOW + block
    step = pl.program_id(0)
    part = pl.program_id(1)

    @pl.when((step == 0) & (part == 0))
    def _():
        for kv in range(kv_ref.shape[0]):
            lanes = slice(kv * HEAD, (kv + 1) * HEAD)
            kv_ref[kv, :tokens, :] = far_ref[:, lanes]
            kv_ref[kv, tokens : 2 * tokens, :] = near_ref[:, lanes]
            kv_ref[kv, 2 * tokens :, :] = own_ref[:, lanes]

    begin = pl.multiple_of(((step + turn_ref[0]) % (tokens // block)) * block, block)
    row = lax.broadcasted_iota(jnp.int32, (block, block), 0)
    col = lax.broadcasted_iota(jnp.int32, (block, block), 1)
    scale = math.log2(math.e) / math.sqrt(HEAD)

    def run(bounded):
        keys = kv_ref[2 * part, pl.ds(begin, reach), :]
        values = kv_ref[2 * part + 1, pl.ds(begin, reach), :]
        queries = jnp.concatenate(
            [query_ref[:, r * HEAD : (r + 1) * HEAD] for r in range(group)], axis=0
        )
        everything = dot_t(queries, keys)
        position = lax.broadcasted_iota(jnp.int32, (1, reach), 1) + begin
        bias = jnp.where(position >= first_ref[0], 0.0, MASKED)
        weights = []
        totals = []
        for r in range(group):
            scores = everything[r * block : (r + 1) * block]
            if bounded:
                scores = scores + bias
            pieces = (
                jnp.where(col > row, scores[:, :block], MASKED),
                scores[:, block:WINDOW],
                jnp.where(col <= row, scores[:, WINDOW:], MASKED),
            )
            tops = [jnp.max(piece, axis=1, keepdims=True) for piece in pieces]
            top = jnp.maximum(jnp.maximum(tops[0], tops[1]), tops[2])
            powers = [jnp.exp2((piece - top) * scale) for piece in pieces]
            sums = [jnp.sum(power, axis=1, keepdims=True) for power in powers]
            totals.append(sums[0] + sums[1] + sums[2])
            weights.append(jnp.concatenate([power.astype(bf16) for power in powers], axis=1))
        mixed = dot(jnp.concatenate(weights, axis=0), values)
        result = jnp.concatenate(
            [
                (mixed[r * block : (r + 1) * block] / totals[r]).astype(bf16)
                for r in range(group)
            ],
            axis=1,
        )
        for d, out_ref in enumerate(out_refs):

            @pl.when(step == d)
            def _(out_ref=out_ref):
                for g in range(kv_ref.shape[0] // 2):

                    @pl.when(part == g)
                    def _(g=g):
                        out_ref[:, g * group * HEAD : (g + 1) * group * HEAD] = result

    @pl.when(first_ref[0] > begin)
    def _():
        run(True)

    @pl.when(first_ref[0] <= begin)
    def _():
        run(False)


def attend(first, turn, count, query, own, near, far):
    tokens, width = query.shape
    block = tokens // count
    groups = own.shape[1] // (2 * HEAD)
    lanes = width // groups
    return pl.pallas_call(
        attend_body,
        grid_spec=pltpu.PrefetchScalarGridSpec(
            num_scalar_prefetch=2,
            grid=(count, groups),
            in_specs=[
                pl.BlockSpec((block, lanes), lambda i, g, _, t: ((i + t[0]) % count, g)),
                ONCHIP,
                ONCHIP,
                ONCHIP,
            ],
            out_specs=[ONCHIP] * count,
            scratch_shapes=[pltpu.VMEM((2 * groups, WINDOW + tokens, HEAD), bf16)],
        ),
        out_shape=[jax.ShapeDtypeStruct((block, width), bf16)] * count,
        name="attend",
        compiler_params=pltpu.CompilerParams(dimension_semantics=("arbitrary", "arbitrary")),
    )(first, turn, query, own, near, far)


def join_turns_body(place_ref, *refs):
    *in_refs, out_ref, done = refs
    width = in_refs[0].shape[1]
    copies = []
    for d, in_ref in enumerate(in_refs):
        lanes = pl.ds(pl.multiple_of(place_ref[d] * width, width), width)
        copies.append(pltpu.make_async_copy(in_ref, out_ref.at[:, lanes], done.at[d]))
    for copy in copies:
        copy.start()
    for copy in copies:
        copy.wait()


def join_halves_body(place_ref, left_ref, right_ref, out_ref, done):
    count, _, width = left_ref.shape
    copies = []
    for k, in_ref in enumerate((left_ref, right_ref)):
        for d in range(count):
            lanes = pl.ds(pl.multiple_of((2 * d + place_ref[k]) * width, width), width)
            copies.append(
                pltpu.make_async_copy(in_ref.at[d], out_ref.at[:, lanes], done.at[k * count + d])
            )
    for copy in copies:
        copy.start()
    for copy in copies:
        copy.wait()


def join_call(body, copies, rows, width, place, *operands):
    return pl.pallas_call(
        body,
        in_specs=[SCALAR] + [ONCHIP] * len(operands),
        out_specs=pl.BlockSpec(memory_space=pltpu.HBM),
        out_shape=jax.ShapeDtypeStruct((rows, width), bf16),
        scratch_shapes=[pltpu.SemaphoreType.DMA((copies,))],
    )(place, *operands)


def onchip_call(body, shapes, scalars, *operands):
    return pl.pallas_call(
        body,
        in_specs=[SCALAR] * len(scalars) + [ONCHIP] * len(operands),
        out_specs=[ONCHIP] * len(shapes),
        out_shape=shapes,
    )(*scalars, *operands)


def ring(block, axes, distance, size):
    return lax.ppermute(block, axes, [(i, (i + distance) % size) for i in range(size)])


CTX = ("y", "x", "core")
CHIPS = ("y", "x")
SWAP = [(0, 1), (1, 0)]


def exchange(block, axes):
    return lax.all_to_all(block, axes, split_axis=0, concat_axis=0, tiled=True)


def local(
    attn_query, attn_key, attention_value, delta_query, delta_key, delta_value, log_decay, beta_gate
):
    tokens = attn_query.shape[0]
    size = lax.axis_size(CTX)
    index = lax.axis_index(CTX)
    core = lax.axis_index("core").astype(jnp.int32).reshape(1)
    key_value = jnp.stack((attn_key, attention_value), axis=2).reshape(tokens, -1)
    far = ring(key_value, CTX, 2, size)
    near = ring(key_value, CTX, 1, size)

    def rows(tensor):
        return tensor.reshape(tokens, -1)

    half = delta_query.shape[1] // 2
    delta_args = (rows(delta_query), rows(delta_key), rows(delta_value), log_decay, beta_gate)
    local_b, reach_b, state_b = delta_local((1 - core) * (half // 2), *delta_args, half)
    other = lax.ppermute(state_b, "core", SWAP)
    local_a, reach_a, state_a = delta_local(core * (half // 2), *delta_args, half)
    state_a, near, far = lax.optimization_barrier((state_a, near, far))
    shape = jax.ShapeDtypeStruct
    message, early = onchip_call(
        pack_body,
        [
            shape((half * 4, HEAD + HEAD // 4 + 16, HEAD), bf16),
            shape((half, STATE, HEAD), f32),
        ],
        [core],
        state_a,
        other,
    )
    gathered = exchange(message, CHIPS)
    first = jnp.maximum(0, WINDOW - tokens * index).astype(jnp.int32).reshape(1)
    count = lax.axis_size("head")
    rank = lax.axis_index("head").astype(jnp.int32).reshape(1)
    turn = tokens // count
    attended = attend(first, rank, count, rows(attn_query), key_value, near, far)
    attn = [attended[0]]
    for d in range(1, count):
        attn.append(ring(attended[d], "head", d, count))
    (starts,) = onchip_call(relay_body, [shape((half * 4, HEAD // 4, HEAD), bf16)], [], gathered)
    returned = exchange(starts, CHIPS)
    keep, send = onchip_call(
        unpack_body,
        [shape((half, HEAD, HEAD), bf16)] * 2,
        [core],
        returned.reshape(half, HEAD, HEAD),
        early,
    )
    received = lax.ppermute(send, "core", SWAP)
    halves = [shape((tokens, half * HEAD), bf16)]
    (delta_a,) = onchip_call(finish_body, halves, [], reach_a, local_a, keep)
    delta_a = exchange(delta_a.reshape(count, turn, -1), "head")
    (delta_b,) = onchip_call(finish_body, halves, [], reach_b, local_b, received)
    delta_b = exchange(delta_b.reshape(count, turn, -1), "head")
    wide = count * delta_query.shape[1] * HEAD
    places = (rank - jnp.arange(count, dtype=jnp.int32)) % count
    attn_out = join_call(join_turns_body, count, turn, wide, places, *attn)
    sides = jnp.concatenate((core, 1 - core))
    delta_out = join_call(join_halves_body, 2 * count, turn, wide, sides, delta_a, delta_b)
    return (attn_out, delta_out)


def solution(mesh):
    fine = Mesh(mesh.devices.reshape(4, 4, 2, 4), ("y", "x", "core", "head"))
    cut = P(CTX, "head", None)
    gate = P("head", CTX)
    out = P((*CTX, "head"), None)
    return jax.shard_map(
        local,
        mesh=fine,
        in_specs=(cut,) * 6 + (gate, gate),
        out_specs=(out, out),
        check_vma=False,
    )
```

time: 150 us -> 139 us (0.927)
  the two profiles are of different devices: /device:TPU:0 before, /device:TPU:1 now
where the time goes in v2:
time: 139 us
  Pallas kernels  59.1 us (43%)
  blocking collectives  25.4 us (18%)
  waiting for transfers between devices  22.8 us (16%)
  starting transfers between devices  17.7 us (13%)
  local copies, waits for them, and re-layouts  10.6 us (8%)
  other arithmetic  1.94 us (1%)
    pallas_call x2, Pallas kernels, delta_local(): pl.pallas_call(delta_body, grid_spec=pltpu.PrefetchScalarGridSpec(num_sca...  26.1 us
    all_to_all x2, blocking collectives, exchange(): return lax.all_to_all(block, axes, split_axis=0, concat_axis=0, tiled=True)  25.4 us
    ppermute x5, waiting for transfers between devices, ring(): lax.ppermute(block, axes, [(i, (i + distance) % size) for i in range(size)])  16.9 us
    pallas_call x1, Pallas kernels, attend(): pl.pallas_call(attend_body, grid_spec=pltpu.PrefetchScalarGridSpec(num_sc...  15.4 us
    pallas_call x5, Pallas kernels, onchip_call(): pl.pallas_call(body, in_specs=[SCALAR] * len(scalars) + [ONCHIP] * len(op...  13.2 us
    all_to_all x2, starting transfers between devices, exchange(): return lax.all_to_all(block, axes, split_axis=0, concat_axis=0, tiled=True)  8.76 us
    unnamed x34, local copies, waits for them, and re-layouts  7.76 us
    ppermute x5, starting transfers between devices, ring(): lax.ppermute(block, axes, [(i, (i + distance) % size) for i in range(size)])  7.51 us
  transfers between devices with their start and end apart: 9, of which 5 were waited for; matrix products, arithmetic and copies ran while one was open for 3% of the time, Pallas kernels for 24%

profile of v2, /device:TPU:1, one launch (start us, length us, event | category | flops | bytes accessed | tf_op | source)
XLA Modules:
  0.0 138.5 jit_solution(11661868293616682614)
XLA Ops:
  0.6 0.0 copy-start.4
  0.6 0.0 copy-start.5
  0.7 2.6 %copy.19 = bf16[64,8,8,128]{3,1,2,0:T(8,128)(2,1)} copy(bf16[64,8,8,128]{3,2,1,0:T(8,128)(2,1)} %bitcast.27) | data formatting | bytes 2097152
  3.3 0.0 copy-done.4
  3.3 0.0 copy-done.5
  3.3 1.8 %copy_bitcast_fusion = (bf16[512,1024]{1,0:T(8,128)(2,1)}, bf16[512,1024]{1,0:T(8,128)(2,1)}) fusion(bf16[64,8,8,128]{3,2,1,0:T(8,128)(2,1)S(1)} %bitcast.29, bf16[64,8,8,128]{3,2,1,0:T(8,128)(2,1)S(1)} %bitcast.30), kind=kLoop, calls=%fused_computation | loop fusion | bytes 4194304 | tf_op jit(solution)/shard_map/reshape | solution.py:433
  5.1 0.0 copy-start.12
  5.1 0.0 copy-start.13
  5.1 13.0 %delta_local.3 = (f32[512,512]{1,0:T(8,128)}, bf16[512,512]{1,0:T(8,128)(2,1)}, f32[4,264,128]{2,1,0:T(8,128)}) custom-call(s32[1]{0:T(128)S(6)} %mul.15.base_ref, bf16[512,1024]{1,0:T(8,128)(2,1)} %bitcast.22, bf16[512,1024]{1,0:T(8,128)(2,1)} %get-tuple-element.37.k_ref, bf16[512,1024]{1,0:T(8,128)(2,1)} %get-tuple-element.36.v_ref, f32[8,512]{1,0:T(8,128)} %log_ref.3, ...), custom_call_target="tpu_custom_call" | custom-call | tf_op jit(solution)/shard_map/delta_local/pallas_call | solution.py:175
  18.2 1.5 %collective-permute-start.5 = (f32[4,264,128]{2,1,0:T(8,128)}, f32[4,264,128]{2,1,0:T(8,128)S(1)}, u32[]{:S(2)}, u32[]{:S(2)}) collective-permute-start(f32[4,264,128]{2,1,0:T(8,128)} %get-tuple-element.29), channel_id=1, source_target_pairs={{0,4},{4,0},{1,5},{5,1},{2,6},{6,2},{3,7},{7,3},{8,12},{12,8},{9,1... | collective-permute-start | bytes 1622024 | tf_op jit(solution)/shard_map/ppermute | solution.py:438
  19.6 0.0 copy-done.12
  19.6 0.0 copy-done.13
  19.6 0.7 pad_maximum_fusion
  20.4 0.8 copy.10
  21.2 0.2 reshape.41.own_ref
  21.4 0.0 copy-start
  21.4 1.3 collective-permute-start
  22.7 1.2 collective-permute-start.1
  23.9 13.1 %delta_local.2 = (f32[512,512]{1,0:T(8,128)}, bf16[512,512]{1,0:T(8,128)(2,1)}, f32[4,264,128]{2,1,0:T(8,128)}) custom-call(s32[1]{0:T(128)S(6)} %mul.14.base_ref, bf16[512,1024]{1,0:T(8,128)(2,1)} %bitcast.23, bf16[512,1024]{1,0:T(8,128)(2,1)} %get-tuple-element.37.k_ref, bf16[512,1024]{1,0:T(8,128)(2,1)} %get-tuple-element.36.v_ref, f32[8,512]{1,0:T(8,128)} %log_ref.3, ...), custom_call_target="tpu_custom_call" | custom-call | tf_op jit(solution)/shard_map/delta_local/pallas_call | solution.py:175
  37.0 0.0 copy-done
  37.0 0.0 collective-permute-done.near_ref
  37.0 0.0 copy-start.7
  37.0 7.3 %collective-permute-done.1.far_ref = bf16[512,512]{1,0:T(8,128)(2,1)S(1)} collective-permute-done((bf16[512,512]{1,0:T(8,128)(2,1)S(1)}, bf16[512,512]{1,0:T(8,128)(2,1)S(1)}, u32[]{:S(2)}, u32[]{:S(2)}) %collective-permute-start.1) | collective-permute-done | bytes 524320 | tf_op jit(solution)/shard_map/ppermute | solution.py:409
  44.3 0.0 copy-start.8
  44.3 0.0 collective-permute-done.5.other_ref
  44.3 0.0 copy-start.6
  44.3 0.8 copy-done.6
  45.1 2.5 %shard_map.96 = (bf16[16,176,128]{2,1,0:T(8,128)(2,1)}, f32[4,264,128]{2,1,0:T(8,128)}) custom-call(s32[1]{0:T(128)} %bitcast.4.core_ref, f32[4,264,128]{2,1,0:T(8,128)} %get-tuple-element.28.own_ref, f32[4,264,128]{2,1,0:T(8,128)} %copy-done.6), custom_call_target="tpu_custom_call" | custom-call | tf_op jit(solution)/shard_map/pallas_call | solution.py:400
  47.7 14.4 %all_to_all.20.message_ref = bf16[16,176,128]{2,1,0:T(8,128)(2,1)} all-to-all(bf16[16,176,128]{2,1,0:T(8,128)(2,1)} %get-tuple-element.30), channel_id=1, replica_groups=mesh['y'=4,'x'=4,'core'=2,'head'=4] {'y','x'}, dimensions={0} | all-to-all | bytes 1441792 | tf_op jit(solution)/shard_map/all_to_all | solution.py:418
  62.1 3.6 %shard_map.97 = bf16[16,32,128]{2,1,0:T(8,128)(2,1)} custom-call(bf16[16,176,128]{2,1,0:T(8,128)(2,1)} %all_to_all.20.message_ref), custom_call_target="tpu_custom_call" | custom-call | tf_op jit(solution)/shard_map/pallas_call | solution.py:400
  65.7 0.0 copy-done.7
  65.7 0.0 copy-done.8
  65.7 11.0 %all_to_all.21 = bf16[16,32,128]{2,1,0:T(8,128)(2,1)} all-to-all(bf16[16,32,128]{2,1,0:T(8,128)(2,1)} %shard_map.97), channel_id=1, replica_groups=mesh['y'=4,'x'=4,'core'=2,'head'=4] {'y','x'}, dimensions={0} | all-to-all | bytes 262144 | tf_op jit(solution)/shard_map/all_to_all | solution.py:418
  76.7 2.1 %shard_map.98 = (bf16[4,128,128]{2,1,0:T(8,128)(2,1)}, bf16[4,128,128]{2,1,0:T(8,128)(2,1)}) custom-call(s32[1]{0:T(128)} %bitcast.4.core_ref, bf16[4,128,128]{2,1,0:T(8,128)(2,1)} %bitcast.31, f32[4,264,128]{2,1,0:T(8,128)} %get-tuple-element.31.early_ref), custom_call_target="tpu_custom_call" | custom-call | tf_op jit(solution)/shard_map/pallas_call | solution.py:400
  78.8 2.5 %shard_map.99 = bf16[512,512]{1,0:T(8,128)(2,1)} custom-call(bf16[512,512]{1,0:T(8,128)(2,1)} %get-tuple-element.26.reach_ref, f32[512,512]{1,0:T(8,128)} %get-tuple-element.27.local_ref, bf16[4,128,128]{2,1,0:T(8,128)(2,1)} %get-tuple-element.32.state_ref), custom_call_target="tpu_custom_call" | custom-call | tf_op jit(solution)/shard_map/pallas_call | solution.py:400
  81.3 0.0 copy-start.15
  81.3 5.3 %all-to-all-start.2 = ((bf16[4,128,512]{2,1,0:T(8,128)(2,1)}), bf16[4,128,512]{2,1,0:T(8,128)(2,1)S(1)}, u32[]{:S(2)}, u32[]{:S(2)}) async-start(bf16[4,128,512]{2,1,0:T(8,128)(2,1)} %bitcast.26), calls=%async_computation.2 | async-start | bytes 1048576 | tf_op jit(solution)/shard_map/all_to_all | solution.py:418
  86.6 0.0 copy-done.15
  86.6 0.0 collective-permute-start.6
  86.6 1.3 collective-permute-done.6.state_ref
  88.0 0.7 copy-done.14
  88.6 2.5 %shard_map.100 = bf16[512,512]{1,0:T(8,128)(2,1)} custom-call(bf16[512,512]{1,0:T(8,128)(2,1)} %get-tuple-element.33.reach_ref, f32[512,512]{1,0:T(8,128)} %get-tuple-element.34.local_ref, bf16[4,128,128]{2,1,0:T(8,128)(2,1)} %copy-done.14), custom_call_target="tpu_custom_call" | custom-call | tf_op jit(solution)/shard_map/pallas_call | solution.py:400
  91.1 4.5 %all-to-all-done.2.left_ref = bf16[4,128,512]{2,1,0:T(8,128)(2,1)S(1)} async-done(((bf16[4,128,512]{2,1,0:T(8,128)(2,1)}), bf16[4,128,512]{2,1,0:T(8,128)(2,1)S(1)}, u32[]{:S(2)}, u32[]{:S(2)}) %all-to-all-start.2) | async-done | bytes 524320 | tf_op jit(solution)/shard_map/all_to_all | solution.py:418
  95.6 0.8 copy-done.1
  96.4 3.5 %all-to-all-start.3 = ((bf16[4,128,512]{2,1,0:T(8,128)(2,1)}), bf16[4,128,512]{2,1,0:T(8,128)(2,1)S(1)}, u32[]{:S(2)}, u32[]{:S(2)}) async-start(bf16[4,128,512]{2,1,0:T(8,128)(2,1)} %bitcast.25), calls=%async_computation.3 | async-start | bytes 1048576 | tf_op jit(solution)/shard_map/all_to_all | solution.py:418
  99.9 0.0 copy-done.3
  99.9 1.2 copy.20
  101.1 15.4 %attend.1 = (bf16[128,1024]{1,0:T(8,128)(2,1)}, bf16[128,1024]{1,0:T(8,128)(2,1)}, bf16[128,1024]{1,0:T(8,128)(2,1)}, bf16[128,1024]{1,0:T(8,128)(2,1)}) custom-call(s32[1]{0:T(128)} %bitcast.first_ref, s32[1]{0:T(128)} %bitcast.1.turn_ref, bf16[512,1024]{1,0:T(8,128)(2,1)} %bitcast.24, bf16[512,512]{1,0:T(8,128)(2,1)} %copy-done, ...), custom_call_target="tpu_custom_call" | custom-call | tf_op jit(solution)/shard_map/attend/pallas_call | solution.py:341
  116.5 1.4 %collective-permute-start.2 = (bf16[128,1024]{1,0:T(8,128)(2,1)}, bf16[128,1024]{1,0:T(8,128)(2,1)S(1)}, u32[]{:S(2)}, u32[]{:S(2)}) collective-permute-start(bf16[128,1024]{1,0:T(8,128)(2,1)} %get-tuple-element.23), channel_id=1, source_target_pairs={{0,1},{1,2},{2,3},{3,0},{4,5},{5,6},{6,7},{7,4},{8,9},{9,10},{10,1... | collective-permute-start | bytes 786440 | tf_op jit(solution)/shard_map/ppermute | solution.py:409
  117.9 2.4 %collective-permute-start.3 = (bf16[128,1024]{1,0:T(8,128)(2,1)}, bf16[128,1024]{1,0:T(8,128)(2,1)S(1)}, u32[]{:S(2)}, u32[]{:S(2)}) collective-permute-start(bf16[128,1024]{1,0:T(8,128)(2,1)} %get-tuple-element.24), channel_id=1, source_target_pairs={{0,2},{1,3},{2,0},{3,1},{4,6},{5,7},{6,4},{7,5},{8,10},{9,11},{10,... | collective-permute-start | bytes 786440 | tf_op jit(solution)/shard_map/ppermute | solution.py:409
  120.3 1.2 collective-permute-start.4
  121.5 0.6 and_select_fusion.place_ref
  122.0 0.7 pad_add_fusion.place_ref
  122.7 3.2 %collective-permute-done.2.refs_1_ = bf16[128,1024]{1,0:T(8,128)(2,1)S(1)} collective-permute-done((bf16[128,1024]{1,0:T(8,128)(2,1)}, bf16[128,1024]{1,0:T(8,128)(2,1)S(1)}, u32[]{:S(2)}, u32[]{:S(2)}) %collective-permute-start.2) | collective-permute-done | bytes 262176 | tf_op jit(solution)/shard_map/ppermute | solution.py:409
  125.9 6.5 %collective-permute-done.3.refs_2_ = bf16[128,1024]{1,0:T(8,128)(2,1)S(1)} collective-permute-done((bf16[128,1024]{1,0:T(8,128)(2,1)}, bf16[128,1024]{1,0:T(8,128)(2,1)S(1)}, u32[]{:S(2)}, u32[]{:S(2)}) %collective-permute-start.3) | collective-permute-done | bytes 262176 | tf_op jit(solution)/shard_map/ppermute | solution.py:409
  132.3 0.0 collective-permute-done.4.refs_3_
  132.3 0.0 copy-done.9
  132.3 0.7 copy-done.10
  133.0 0.1 copy-done.11
  133.1 2.2 %shard_map.95 = bf16[128,4096]{1,0:T(8,128)(2,1)} custom-call(s32[4]{0:T(128)} %and_select_fusion.place_ref, bf16[128,1024]{1,0:T(8,128)(2,1)} %get-tuple-element.22.refs_0_, bf16[128,1024]{1,0:T(8,128)(2,1)} %copy-done.9, bf16[128,1024]{1,0:T(8,128)(2,1)} %copy-done.10, bf16[128,1024]{1,0:T(8,128)(2,1)} %copy-done.11), custom_call_target="tpu_custom_call" | custom-call | tf_op jit(solution)/shard_map/pallas_call | solution.py:390
  135.3 0.0 all-to-all-done.3.right_ref
  135.3 0.0 copy-start.2
  135.4 0.8 copy-done.2
  136.1 2.2 %shard_map.101 = bf16[128,4096]{1,0:T(8,128)(2,1)} custom-call(s32[2]{0:T(128)} %pad_add_fusion.place_ref, bf16[4,128,512]{2,1,0:T(8,128)(2,1)} %copy-done.1, bf16[4,128,512]{2,1,0:T(8,128)(2,1)} %copy-done.2), custom_call_target="tpu_custom_call" | custom-call | tf_op jit(solution)/shard_map/pallas_call | solution.py:390
  (6 shorter events, 0.0 us)
Async XLA Ops:
  0.6 2.6 %copy-start.4 = (bf16[512,8,128]{2,1,0:T(8,128)(2,1)S(1)}, bf16[512,8,128]{2,1,0:T(8,128)(2,1)}, u32[]{:S(2)}) copy-start(bf16[512,8,128]{2,1,0:T(8,128)(2,1)} %param.13) | copy-start | bytes 3145732
  0.6 2.6 %copy-start.5 = (bf16[512,8,128]{2,1,0:T(8,128)(2,1)S(1)}, bf16[512,8,128]{2,1,0:T(8,128)(2,1)}, u32[]{:S(2)}) copy-start(bf16[512,8,128]{2,1,0:T(8,128)(2,1)} %param.12) | copy-start | bytes 3145732
  5.1 14.5 %copy-start.12 = (bf16[512,2,128]{2,1,0:T(2,128)(2,1)S(1)}, bf16[512,2,128]{2,1,0:T(2,128)(2,1)}, u32[]{:S(2)}) copy-start(bf16[512,2,128]{2,1,0:T(2,128)(2,1)} %param.10) | copy-start | bytes 786436
  5.1 14.5 %copy-start.13 = (bf16[512,2,128]{2,1,0:T(2,128)(2,1)S(1)}, bf16[512,2,128]{2,1,0:T(2,128)(2,1)}, u32[]{:S(2)}) copy-start(bf16[512,2,128]{2,1,0:T(2,128)(2,1)} %param.9) | copy-start | bytes 786436
  18.2 26.2 %collective-permute-start.5 = (f32[4,264,128]{2,1,0:T(8,128)}, f32[4,264,128]{2,1,0:T(8,128)S(1)}, u32[]{:S(2)}, u32[]{:S(2)}) collective-permute-start(f32[4,264,128]{2,1,0:T(8,128)} %get-tuple-element.29), channel_id=1, source_target_pairs={{0,4},{4,0},{1,5},{5,1},{2,6},{6,2},{3,7},{7,3},{8,12},{12,8},{9,1... | collective-permute-start | bytes 1622024 | tf_op jit(solution)/shard_map/ppermute | solution.py:438
  21.4 15.6 %copy-start = (bf16[512,512]{1,0:T(8,128)(2,1)}, bf16[512,512]{1,0:T(8,128)(2,1)S(1)}, u32[]{:S(2)}) copy-start(bf16[512,512]{1,0:T(8,128)(2,1)S(1)} %reshape.41.own_ref) | copy-start | bytes 1572868
  21.4 15.6 %collective-permute-start = (bf16[512,512]{1,0:T(8,128)(2,1)S(1)}, bf16[512,512]{1,0:T(8,128)(2,1)S(1)}, u32[]{:S(2)}, u32[]{:S(2)}) collective-permute-start(bf16[512,512]{1,0:T(8,128)(2,1)S(1)} %reshape.41.own_ref), channel_id=1, source_target_pairs={{0,4},{4,8},{8,12},{12,16},{16,20},{20,24},{24,28},{28,32},{32,36}... | collective-permute-start | bytes 1572872 | tf_op jit(solution)/shard_map/ppermute | solution.py:409
  22.7 21.6 %collective-permute-start.1 = (bf16[512,512]{1,0:T(8,128)(2,1)S(1)}, bf16[512,512]{1,0:T(8,128)(2,1)S(1)}, u32[]{:S(2)}, u32[]{:S(2)}) collective-permute-start(bf16[512,512]{1,0:T(8,128)(2,1)S(1)} %reshape.41.own_ref), channel_id=1, source_target_pairs={{0,8},{4,12},{8,16},{12,20},{16,24},{20,28},{24,32},{28,36},{32,40... | collective-permute-start | bytes 1572872 | tf_op jit(solution)/shard_map/ppermute | solution.py:409
  37.0 28.7 %copy-start.7 = (bf16[512,512]{1,0:T(8,128)(2,1)}, bf16[512,512]{1,0:T(8,128)(2,1)S(1)}, u32[]{:S(2)}) copy-start(bf16[512,512]{1,0:T(8,128)(2,1)S(1)} %collective-permute-done.near_ref) | copy-start | bytes 1572868
  44.3 21.4 %copy-start.8 = (bf16[512,512]{1,0:T(8,128)(2,1)}, bf16[512,512]{1,0:T(8,128)(2,1)S(1)}, u32[]{:S(2)}) copy-start(bf16[512,512]{1,0:T(8,128)(2,1)S(1)} %collective-permute-done.1.far_ref) | copy-start | bytes 1572868
  44.3 0.8 copy-start.6
  81.3 5.3 %copy-start.15 = (bf16[4,128,128]{2,1,0:T(8,128)(2,1)S(1)}, bf16[4,128,128]{2,1,0:T(8,128)(2,1)}, u32[]{:S(2)}) copy-start(bf16[4,128,128]{2,1,0:T(8,128)(2,1)} %get-tuple-element.35) | copy-start | bytes 393220
  81.3 14.3 %all-to-all-start.2 = ((bf16[4,128,512]{2,1,0:T(8,128)(2,1)}), bf16[4,128,512]{2,1,0:T(8,128)(2,1)S(1)}, u32[]{:S(2)}, u32[]{:S(2)}) async-start(bf16[4,128,512]{2,1,0:T(8,128)(2,1)} %bitcast.26), calls=%async_computation.2 | async-start | bytes 1048576 | tf_op jit(solution)/shard_map/all_to_all | solution.py:418
  86.6 1.3 collective-permute-start.6
  88.0 0.7 copy-start.14
  91.1 8.8 %copy-start.3 = (bf16[512,8,128]{2,1,0:T(8,128)(2,1)S(1)}, bf16[512,8,128]{2,1,0:T(8,128)(2,1)}, u32[]{:S(2)}) copy-start(bf16[512,8,128]{2,1,0:T(8,128)(2,1)} %param.8) | copy-start | bytes 3145732
  95.6 0.8 copy-start.1
  96.4 39.0 %all-to-all-start.3 = ((bf16[4,128,512]{2,1,0:T(8,128)(2,1)}), bf16[4,128,512]{2,1,0:T(8,128)(2,1)S(1)}, u32[]{:S(2)}, u32[]{:S(2)}) async-start(bf16[4,128,512]{2,1,0:T(8,128)(2,1)} %bitcast.25), calls=%async_computation.3 | async-start | bytes 1048576 | tf_op jit(solution)/shard_map/all_to_all | solution.py:418
  116.5 9.4 %collective-permute-start.2 = (bf16[128,1024]{1,0:T(8,128)(2,1)}, bf16[128,1024]{1,0:T(8,128)(2,1)S(1)}, u32[]{:S(2)}, u32[]{:S(2)}) collective-permute-start(bf16[128,1024]{1,0:T(8,128)(2,1)} %get-tuple-element.23), channel_id=1, source_target_pairs={{0,1},{1,2},{2,3},{3,0},{4,5},{5,6},{6,7},{7,4},{8,9},{9,10},{10,1... | collective-permute-start | bytes 786440 | tf_op jit(solution)/shard_map/ppermute | solution.py:409
  117.9 14.4 %collective-permute-start.3 = (bf16[128,1024]{1,0:T(8,128)(2,1)}, bf16[128,1024]{1,0:T(8,128)(2,1)S(1)}, u32[]{:S(2)}, u32[]{:S(2)}) collective-permute-start(bf16[128,1024]{1,0:T(8,128)(2,1)} %get-tuple-element.24), channel_id=1, source_target_pairs={{0,2},{1,3},{2,0},{3,1},{4,6},{5,7},{6,4},{7,5},{8,10},{9,11},{10,... | collective-permute-start | bytes 786440 | tf_op jit(solution)/shard_map/ppermute | solution.py:409
  120.3 12.0 %collective-permute-start.4 = (bf16[128,1024]{1,0:T(8,128)(2,1)}, bf16[128,1024]{1,0:T(8,128)(2,1)S(1)}, u32[]{:S(2)}, u32[]{:S(2)}) collective-permute-start(bf16[128,1024]{1,0:T(8,128)(2,1)} %get-tuple-element.25), channel_id=1, source_target_pairs={{0,3},{1,0},{2,1},{3,2},{4,7},{5,4},{6,5},{7,6},{8,11},{9,8},{10,9... | collective-permute-start | bytes 786440 | tf_op jit(solution)/shard_map/ppermute | solution.py:409
  125.9 6.5 %copy-start.9 = (bf16[128,1024]{1,0:T(8,128)(2,1)}, bf16[128,1024]{1,0:T(8,128)(2,1)S(1)}, u32[]{:S(2)}) copy-start(bf16[128,1024]{1,0:T(8,128)(2,1)S(1)} %collective-permute-done.2.refs_1_) | copy-start | bytes 786436
  132.3 0.7 copy-start.10
  132.3 0.8 copy-start.11
  135.3 0.8 copy-start.2

commit v3 on v2

--- a/solution.py
+++ b/solution.py
@@ -38,134 +38,171 @@
     return jnp.concatenate(split(value), axis=1)
 
 
-def full_product(left, right):
-    size = right.shape[1]
-    pair = jnp.concatenate(split(right), axis=1)
-    both = dot(wide_left(left), jnp.concatenate((pair, pair), axis=0))
-    return both[:, :size] + both[:, size:]
-
-
 def exact_right(left, right):
     return dot(wide_left(left), jnp.concatenate((right, right), axis=0))
 
 
 def invert_unit(stricts, row, col):
     size = stricts[0].shape[0]
-    eye = jnp.where(row == col, 1.0, 0.0).astype(f32)
-    block = 8
-    same = (row // block) == (col // block)
-    power = [jnp.where(same, a, 0.0) for a in stricts]
-    inverse = [eye - a for a in power]
-    for _ in range(2):
-        power = [full_product(a, a) for a in power]
-        inverse = [x + full_product(x, a) for x, a in zip(inverse, power)]
+    base = 8
+    blocks = size // base
+    sub = lax.broadcasted_iota(jnp.int32, (base, size), 0)
+    lane = lax.broadcasted_iota(jnp.int32, (base, size), 1)
+    owner = lane // base
+    inside = lane % base
+    inverse = []
+    for a in stricts:
+        small = jnp.where(owner == 0, a[:base], 0.0)
+        for k in range(1, blocks):
+            small = jnp.where(owner == k, a[k * base : (k + 1) * base], small)
+        x = jnp.where(inside == sub, 1.0, 0.0).astype(f32)
+        for r in range(base - 1):
+            factor = jnp.take_along_axis(small, owner * base + r, axis=1)
+            x = x - factor * x[r : r + 1, :]
+        inverse.append(
+            jnp.concatenate([jnp.where(owner == k, x, 0.0) for k in range(blocks)], axis=0)
+        )
+    near = [a.astype(bf16) for a in stricts]
+    block = base
     while block < size:
         below = ((row // block) % 2 == 1) & ((col // block) == (row // block) - 1)
-        joint = [full_product(jnp.where(below, a, 0.0), x) for a, x in zip(stricts, inverse)]
-        inverse = [x - full_product(x, j) for x, j in zip(inverse, joint)]
+        mask = jnp.where(below, 1.0, 0.0).astype(bf16)
+        rounded = [x.astype(bf16) for x in inverse]
+        joint = [dot(a * mask, x).astype(bf16) for a, x in zip(near, rounded)]
+        inverse = [x - dot(y, j) for x, y, j in zip(inverse, rounded, joint)]
         block *= 2
-    return inverse
+    eye = jnp.where(row == col, 1.0, 0.0).astype(f32)
+    rounded = [x.astype(bf16) for x in inverse]
+    residual = [eye - x.astype(f32) - exact_right(a, x) for a, x in zip(stricts, rounded)]
+    return [x.astype(f32) + dot(x, e.astype(bf16)) for x, e in zip(rounded, residual)]
+
+
+def running_sum(rows):
+    lane = lax.broadcasted_iota(jnp.int32, rows.shape, 1)
+    step = 1
+    while step < rows.shape[1]:
+        rows = rows + jnp.where(lane >= step, pltpu.roll(rows, step, 1), 0.0)
+        step *= 2
+    return rows
 
 
 def delta_body(base_ref, q_ref, k_ref, v_ref, log_ref, beta_ref, local_ref, reach_ref, state_ref):
     tokens = q_ref.shape[0]
     heads = q_ref.shape[1] // HEAD
-    begin = (base_ref[0] + pl.program_id(0)) * heads
-    head_index = lax.broadcasted_iota(jnp.int32, log_ref.shape, 0)
-    log_rows = [
-        jnp.sum(jnp.where(head_index == begin + h, log_ref[...], 0.0), axis=0, keepdims=True)
-        for h in range(heads)
-    ]
-    beta_rows = [
-        jnp.sum(jnp.where(head_index == begin + h, beta_ref[...], 0.0), axis=0, keepdims=True)
-        for h in range(heads)
-    ]
     chunks = tokens // CHUNK
     row = lax.broadcasted_iota(jnp.int32, (CHUNK, CHUNK), 0)
     col = lax.broadcasted_iota(jnp.int32, (CHUNK, CHUNK), 1)
-    parts = []
-    for h in range(heads):
-        for c in range(chunks):
-            span = slice(c * CHUNK, (c + 1) * CHUNK)
-            lanes = slice(h * HEAD, (h + 1) * HEAD)
-            key = k_ref[span, lanes]
-            query = q_ref[span, lanes]
-            log_row = log_rows[h][:, span]
-            beta_row = beta_rows[h][:, span]
-            cum_col = jnp.sum(jnp.where(col <= row, log_row, 0.0), axis=1, keepdims=True)
-            log_col = jnp.sum(jnp.where(col == row, log_row, 0.0), axis=1, keepdims=True)
-            beta_col = jnp.sum(jnp.where(col == row, beta_row, 0.0), axis=1, keepdims=True)
-            cum_row = jnp.sum(jnp.where(row <= col, log_col, 0.0), axis=0, keepdims=True)
-            inner = dot_t(key, key)
-            cross = dot_t(query, key)
-            diag = jnp.where(row == col, inner, 0.0)
-            key_col = lax.rsqrt(jnp.sum(diag, axis=1, keepdims=True) + EPSILON)
-            key_row = lax.rsqrt(jnp.sum(diag, axis=0, keepdims=True) + EPSILON)
-            wide_query = query.astype(f32)
-            query_col = lax.rsqrt(
-                jnp.sum(wide_query * wide_query, axis=1, keepdims=True) + EPSILON
-            ) * (1.0 / math.sqrt(HEAD))
-            decay = jnp.exp(jnp.where(row >= col, cum_col - cum_row, MASKED)) * key_row
-            strict = jnp.where(row > col, decay * inner * (beta_col * key_col), 0.0)
-            causal = decay * cross * query_col
-            lead_col = jnp.exp(cum_col)
-            last = cum_col[CHUNK - 1 : CHUNK, :]
-            parts.append(
-                dict(
-                    key=key,
-                    query=query,
-                    strict=strict,
-                    causal=causal,
-                    u_row=beta_row,
-                    y_row=beta_row * jnp.exp(cum_row) * key_row,
-                    out_col=lead_col * query_col,
-                    trail_col=jnp.exp(last - cum_col) * key_col,
-                    whole=jnp.exp(last),
-                    value=v_ref[span, lanes],
-                )
+    begin = (base_ref[0] + pl.program_id(0)) * heads
+    pairs = [(h, c) for c in range(chunks) for h in range(heads)]
+    parts = {}
+
+    def own_heads(ref):
+        picked = ref[:heads]
+        for k in range(1, ref.shape[0] // heads):
+            picked = jnp.where(begin == k * heads, ref[k * heads : (k + 1) * heads], picked)
+        return picked
+
+    def stack(rows):
+        return jnp.concatenate(rows, axis=0)
+
+    logs = own_heads(log_ref)
+    betas = own_heads(beta_ref)
+    spans = [slice(c * CHUNK, (c + 1) * CHUNK) for c in range(chunks)]
+    cum = running_sum(stack([logs[:, span] for span in spans]))
+    beta = stack([betas[:, span] for span in spans])
+    key_rows = []
+    for h, c in pairs:
+        lanes = slice(h * HEAD, (h + 1) * HEAD)
+        key = k_ref[spans[c], lanes]
+        query = q_ref[spans[c], lanes]
+        inner = dot_t(jnp.concatenate((key, query), axis=0), key)
+        wide_query = query.astype(f32)
+        square = jnp.sum(wide_query * wide_query, axis=1, keepdims=True)
+        key_rows.append(
+            jnp.sum(jnp.where(row == col, inner[:CHUNK], 0.0), axis=0, keepdims=True)
+        )
+        parts[h, c] = dict(
+            key=key,
+            query=query,
+            value=v_ref[spans[c], lanes],
+            inner=inner[:CHUNK],
+            cross=inner[CHUNK:],
+            query_col=lax.rsqrt(square + EPSILON) * (1.0 / math.sqrt(HEAD)),
+        )
+    key_unit = lax.rsqrt(stack(key_rows) + EPSILON)
+    last = cum[:, CHUNK - 1 :]
+    y_rows = beta * jnp.exp(cum) * key_unit
+    cum_cols = cum.T
+    lead_cols = jnp.exp(cum_cols)
+    strict_cols = (beta * key_unit).T
+    trail_cols = (jnp.exp(last - cum) * key_unit).T
+    whole = jnp.exp(last)
+    for n, pair in enumerate(pairs):
+        p = parts[pair]
+        at = slice(n, n + 1)
+        decay = jnp.exp(jnp.where(row >= col, cum_cols[:, at] - cum[at], MASKED)) * key_unit[at]
+        p["strict"] = jnp.where(row > col, decay * p["inner"] * strict_cols[:, at], 0.0)
+        p["causal"] = wide_left(decay * p["cross"] * p["query_col"])
+    inverses = invert_unit([parts[pair]["strict"] for pair in pairs], row, col)
+    eye = row == col
+    numbered = [(slice(n, n + 1), parts[pair]) for n, pair in enumerate(pairs)]
+    u_wide = [wide_left(x * beta[at]) for x, (at, p) in zip(inverses, numbered)]
+    y_wide = [wide_left(x * y_rows[at]) for x, (at, p) in zip(inverses, numbered)]
+    twice = [jnp.concatenate((p["value"], p["value"]), axis=0) for at, p in numbered]
+    u_part = [dot(x, y) for x, y in zip(u_wide, twice)]
+    twice = [jnp.concatenate((p["key"], p["key"]), axis=0) for at, p in numbered]
+    y_part = [dot(x, y) for x, y in zip(y_wide, twice)]
+    solved = [jnp.concatenate(both, axis=1) for both in zip(u_part, y_part)]
+    terms = [
+        jnp.concatenate(split(x * trail_cols[:, at]), axis=0)
+        for x, (at, p) in zip(solved, numbered)
+    ]
+    key_t = [p["key"].T for at, p in numbered]
+    kept = [dot(jnp.concatenate((k, k), axis=1), x) for k, x in zip(key_t, terms)]
+    halves = [split(x) for x in solved]
+    near = [
+        dot(p["causal"], jnp.concatenate((x[0], x[0]), axis=0))
+        for x, (at, p) in zip(halves, numbered)
+    ]
+    rest = [dot(p["causal"][:, :HEAD], x[1]) for x, (at, p) in zip(halves, numbered)]
+    near = [x + y for x, y in zip(near, rest)]
+    for n, (at, p) in enumerate(numbered):
+        reach = p["query"].astype(f32) * (lead_cols[:, at] * p["query_col"]) - near[n][:, HEAD:]
+        p["near"] = near[n][:, :HEAD]
+        p["source"] = kept[n][:, :HEAD]
+        transit = jnp.where(eye, whole[at], 0.0) - kept[n][:, HEAD:]
+        if pairs[n][1] == 0:
+            p["reach"] = reach
+            p["transit"] = transit
+        else:
+            p["step"] = wide_left(jnp.concatenate((transit, reach), axis=0))
+    states = [None] * heads
+    for h, c in pairs:
+        p = parts[h, c]
+        lanes = slice(h * HEAD, (h + 1) * HEAD)
+        if c == 0:
+            local_ref[spans[c], lanes] = p["near"]
+            reach_ref[spans[c], lanes] = p["reach"].astype(bf16)
+            states[h] = jnp.concatenate((p["source"], p["transit"]), axis=1)
+        else:
+            high, low = split(states[h])
+            moved = dot(p["step"], jnp.concatenate((high, high), axis=0)) + dot(
+                p["step"][:, :HEAD], low
             )
-    inverses = invert_unit([p["strict"] for p in parts], row, col)
-    for p, inverse in zip(parts, inverses):
-        p["u"] = exact_right(inverse * p["u_row"], p["value"])
-        p["y"] = exact_right(inverse * p["y_row"], p["key"])
-    eye = jnp.where(row == col, 1.0, 0.0).astype(f32)
-    states = [jnp.concatenate((jnp.zeros((HEAD, HEAD), f32), eye), axis=1)] * heads
-    zero = jnp.zeros((CHUNK, HEAD), f32)
-    for c in range(chunks):
-        for h in range(heads):
-            p = parts[h * chunks + c]
-            span = slice(c * CHUNK, (c + 1) * CHUNK)
-            lanes = slice(h * HEAD, (h + 1) * HEAD)
-            state = states[h]
-            high, low = split(state)
-            wide = jnp.concatenate((high, low), axis=0)
-            y_wide = wide_left(p["y"])
-            moved = dot(y_wide, jnp.concatenate((high, high), axis=0)) + dot(
-                y_wide[:, :HEAD], low
+            local_ref[spans[c], lanes] = p["near"] + moved[HEAD:, :HEAD]
+            reach_ref[spans[c], lanes] = moved[HEAD:, HEAD:].astype(bf16)
+            states[h] = jnp.concatenate(
+                (p["source"] + moved[:HEAD, :HEAD], moved[:HEAD, HEAD:]), axis=1
             )
-            weighted = jnp.concatenate((p["u"], zero), axis=1) - moved
-            seen = dot(jnp.concatenate((p["query"], p["query"]), axis=1), wide)
-            near, rest = split(weighted)
-            causal = wide_left(p["causal"])
-            result = (
-                p["out_col"] * seen
-                + dot(causal, jnp.concatenate((near, near), axis=0))
-                + dot(causal[:, :HEAD], rest)
-            )
-            local_ref[span, lanes] = result[:, :HEAD]
-            reach_ref[span, lanes] = result[:, HEAD:].astype(bf16)
-            key_t = p["key"].T
-            kept = jnp.concatenate(split(weighted * p["trail_col"]), axis=0)
-            states[h] = p["whole"] * state + dot(jnp.concatenate((key_t, key_t), axis=1), kept)
+    total = jnp.exp(jnp.sum(logs, axis=1, keepdims=True))
     for h in range(heads):
         place = pl.program_id(0) * heads + h
         state_ref[place, :HEAD, :] = states[h][:, :HEAD].T
         state_ref[place, HEAD : 2 * HEAD, :] = states[h][:, HEAD:].T
-        whole = jnp.exp(jnp.sum(log_rows[h], axis=1, keepdims=True))
-        state_ref[place, 2 * HEAD :, :] = jnp.broadcast_to(whole, (8, HEAD))
-
-
-def delta_local(base, query, key, value, log_decay, beta_gate, heads, heads_step=2):
+        state_ref[place, 2 * HEAD :, :] = jnp.broadcast_to(total[h : h + 1], (8, HEAD))
+
+
+def delta_local(base, query, key, value, log_decay, beta_gate, heads, heads_step=4):
     tokens = query.shape[0]
     steps = heads // heads_step
     lanes = heads_step * HEAD
@@ -283,37 +320,40 @@
     def run(bounded):
         keys = kv_ref[2 * part, pl.ds(begin, reach), :]
         values = kv_ref[2 * part + 1, pl.ds(begin, reach), :]
-        queries = jnp.concatenate(
-            [query_ref[:, r * HEAD : (r + 1) * HEAD] for r in range(group)], axis=0
-        )
-        everything = dot_t(queries, keys)
         position = lax.broadcasted_iota(jnp.int32, (1, reach), 1) + begin
         bias = jnp.where(position >= first_ref[0], 0.0, MASKED)
-        weights = []
-        totals = []
-        for r in range(group):
-            scores = everything[r * block : (r + 1) * block]
-            if bounded:
-                scores = scores + bias
-            pieces = (
-                jnp.where(col > row, scores[:, :block], MASKED),
-                scores[:, block:WINDOW],
-                jnp.where(col <= row, scores[:, WINDOW:], MASKED),
+        at_once = 2
+        scored = []
+        for r in range(0, group, at_once):
+            queries = jnp.concatenate(
+                [query_ref[:, q * HEAD : (q + 1) * HEAD] for q in range(r, r + at_once)], axis=0
             )
-            tops = [jnp.max(piece, axis=1, keepdims=True) for piece in pieces]
-            top = jnp.maximum(jnp.maximum(tops[0], tops[1]), tops[2])
-            powers = [jnp.exp2((piece - top) * scale) for piece in pieces]
-            sums = [jnp.sum(power, axis=1, keepdims=True) for power in powers]
-            totals.append(sums[0] + sums[1] + sums[2])
-            weights.append(jnp.concatenate([power.astype(bf16) for power in powers], axis=1))
-        mixed = dot(jnp.concatenate(weights, axis=0), values)
-        result = jnp.concatenate(
-            [
-                (mixed[r * block : (r + 1) * block] / totals[r]).astype(bf16)
-                for r in range(group)
-            ],
-            axis=1,
-        )
+            scored.append(dot_t(queries, keys))
+        results = []
+        for everything in scored:
+            weights = []
+            totals = []
+            for r in range(at_once):
+                scores = everything[r * block : (r + 1) * block]
+                if bounded:
+                    scores = scores + bias
+                pieces = (
+                    jnp.where(col > row, scores[:, :block], MASKED),
+                    scores[:, block:WINDOW],
+                    jnp.where(col <= row, scores[:, WINDOW:], MASKED),
+                )
+                tops = [jnp.max(piece, axis=1, keepdims=True) for piece in pieces]
+                top = jnp.maximum(jnp.maximum(tops[0], tops[1]), tops[2])
+                powers = [jnp.exp2((piece - top) * scale) for piece in pieces]
+                sums = [jnp.sum(power, axis=1, keepdims=True) for power in powers]
+                totals.append(sums[0] + sums[1] + sums[2])
+                weights.append(
+                    jnp.concatenate([power.astype(bf16) for power in powers], axis=1)
+                )
+            mixed = dot(jnp.concatenate(weights, axis=0), values)
+            for r in range(at_once):
+                results.append((mixed[r * block : (r + 1) * block] / totals[r]).astype(bf16))
+        result = jnp.concatenate(results, axis=1)
         for d, out_ref in enumerate(out_refs):
 
             @pl.when(step == d)
@@ -434,9 +474,9 @@
 
     half = delta_query.shape[1] // 2
     delta_args = (rows(delta_query), rows(delta_key), rows(delta_value), log_decay, beta_gate)
-    local_b, reach_b, state_b = delta_local((1 - core) * (half // 2), *delta_args, half)
+    local_b, reach_b, state_b = delta_local(1 - core, *delta_args, half)
     other = lax.ppermute(state_b, "core", SWAP)
-    local_a, reach_a, state_a = delta_local(core * (half // 2), *delta_args, half)
+    local_a, reach_a, state_a = delta_local(core, *delta_args, half)
     state_a, near, far = lax.optimization_barrier((state_a, near, far))
     shape = jax.ShapeDtypeStruct
     message, early = onchip_call(

time: 139 us -> 132 us (0.950)
  Pallas kernels: 59.1 us -> 47.7 us
  waiting for transfers between devices: 22.8 us -> 26.9 us
    pallas_call x2, Pallas kernels: 26.1 us -> 17.9 us  [delta_local(): pl.pallas_call(delta_body, grid_spec=pltpu.PrefetchScalarGridSpec(num_sca...]
    ppermute x5, waiting for transfers between devices: 16.9 us -> 21.1 us  [ring(): lax.ppermute(block, axes, [(i, (i + distance) % size) for i in range(size)])]
    pallas_call x1, Pallas kernels: 15.4 us -> 12.1 us  [attend(): pl.pallas_call(attend_body, grid_spec=pltpu.PrefetchScalarGridSpec(num_sc...]
  transfers between devices with their start and end apart: 9 -> 9, of which waited for: 5 -> 6; matrix products, arithmetic and copies ran while one was open for 3% -> 3% of each run, Pallas kernels for 24% -> 20%
where the time goes in v3:
time: 132 us; the launch traced here: 131 us
  Pallas kernels  47.7 us (36%)
  waiting for transfers between devices  26.9 us (20%)
  blocking collectives  25.4 us (19%)
  starting transfers between devices  17.6 us (13%)
  local copies, waits for them, and re-layouts  10.6 us (8%)
  other arithmetic  1.94 us (1%)
    all_to_all x2, blocking collectives, exchange(): return lax.all_to_all(block, axes, split_axis=0, concat_axis=0, tiled=True)  25.4 us
    ppermute x5, waiting for transfers between devices, ring(): lax.ppermute(block, axes, [(i, (i + distance) % size) for i in range(size)])  21.1 us
    pallas_call x2, Pallas kernels, delta_local(): pl.pallas_call(delta_body, grid_spec=pltpu.PrefetchScalarGridSpec(num_sca...  17.9 us
    pallas_call x5, Pallas kernels, onchip_call(): pl.pallas_call(body, in_specs=[SCALAR] * len(scalars) + [ONCHIP] * len(op...  13.2 us
    pallas_call x1, Pallas kernels, attend(): pl.pallas_call(attend_body, grid_spec=pltpu.PrefetchScalarGridSpec(num_sc...  12.1 us
    all_to_all x2, starting transfers between devices, exchange(): return lax.all_to_all(block, axes, split_axis=0, concat_axis=0, tiled=True)  8.74 us
    unnamed x34, local copies, waits for them, and re-layouts  7.76 us
    ppermute x5, starting transfers between devices, ring(): lax.ppermute(block, axes, [(i, (i + distance) % size) for i in range(size)])  7.49 us
  transfers between devices with their start and end apart: 9, of which 6 were waited for; matrix products, arithmetic and copies ran while one was open for 3% of the time, Pallas kernels for 20%

profile of v3, /device:TPU:1, one launch (start us, length us, event | category | flops | bytes accessed | tf_op | source)
XLA Modules:
  0.0 131.1 jit_solution(15723351503841221978)
XLA Ops:
  0.6 0.0 copy-start.4
  0.6 0.0 copy-start.5
  0.7 2.6 %copy.19 = bf16[64,8,8,128]{3,1,2,0:T(8,128)(2,1)} copy(bf16[64,8,8,128]{3,2,1,0:T(8,128)(2,1)} %bitcast.27) | data formatting | bytes 2097152
  3.3 0.0 copy-done.4
  3.3 0.0 copy-done.5
  3.3 1.8 %copy_bitcast_fusion = (bf16[512,1024]{1,0:T(8,128)(2,1)}, bf16[512,1024]{1,0:T(8,128)(2,1)}) fusion(bf16[64,8,8,128]{3,2,1,0:T(8,128)(2,1)S(1)} %bitcast.29, bf16[64,8,8,128]{3,2,1,0:T(8,128)(2,1)S(1)} %bitcast.30), kind=kLoop, calls=%fused_computation | loop fusion | bytes 4194304 | tf_op jit(solution)/shard_map/reshape | solution.py:473
  5.1 0.0 copy-start.12
  5.1 0.0 copy-start.13
  5.1 9.0 %delta_local.3 = (f32[512,512]{1,0:T(8,128)}, bf16[512,512]{1,0:T(8,128)(2,1)}, f32[4,264,128]{2,1,0:T(8,128)}) custom-call(s32[1]{0:T(128)S(6)} %sub.18.base_ref, bf16[512,1024]{1,0:T(8,128)(2,1)} %bitcast.22, bf16[512,1024]{1,0:T(8,128)(2,1)} %get-tuple-element.37.k_ref, bf16[512,1024]{1,0:T(8,128)(2,1)} %get-tuple-element.36.v_ref, f32[8,512]{1,0:T(8,128)} %log_ref.3, ...), custom_call_target="tpu_custom_call" | custom-call | tf_op jit(solution)/shard_map/delta_local/pallas_call | solution.py:212
  14.1 1.4 %collective-permute-start.5 = (f32[4,264,128]{2,1,0:T(8,128)}, f32[4,264,128]{2,1,0:T(8,128)S(1)}, u32[]{:S(2)}, u32[]{:S(2)}) collective-permute-start(f32[4,264,128]{2,1,0:T(8,128)} %get-tuple-element.29), channel_id=1, source_target_pairs={{0,4},{4,0},{1,5},{5,1},{2,6},{6,2},{3,7},{7,3},{8,12},{12,8},{9,1... | collective-permute-start | bytes 1622024 | tf_op jit(solution)/shard_map/ppermute | solution.py:478
  15.5 0.0 copy-done.12
  15.5 0.0 copy-done.13
  15.5 0.7 pad_maximum_fusion
  16.2 0.8 copy.10
  17.1 0.2 reshape.41.own_ref
  17.3 0.0 copy-start
  17.3 1.3 collective-permute-start
  18.6 1.2 collective-permute-start.1
  19.8 8.9 %delta_local.2 = (f32[512,512]{1,0:T(8,128)}, bf16[512,512]{1,0:T(8,128)(2,1)}, f32[4,264,128]{2,1,0:T(8,128)}) custom-call(s32[1]{0:T(128)} %bitcast.4.base_ref.core_ref, bf16[512,1024]{1,0:T(8,128)(2,1)} %bitcast.23, bf16[512,1024]{1,0:T(8,128)(2,1)} %get-tuple-element.37.k_ref, bf16[512,1024]{1,0:T(8,128)(2,1)} %get-tuple-element.36.v_ref, ...), custom_call_target="tpu_custom_call" | custom-call | tf_op jit(solution)/shard_map/delta_local/pallas_call | solution.py:212
  28.7 0.0 copy-done
  28.7 0.5 collective-permute-done.near_ref
  29.2 0.0 copy-start.7
  29.2 11.0 %collective-permute-done.1.far_ref = bf16[512,512]{1,0:T(8,128)(2,1)S(1)} collective-permute-done((bf16[512,512]{1,0:T(8,128)(2,1)S(1)}, bf16[512,512]{1,0:T(8,128)(2,1)S(1)}, u32[]{:S(2)}, u32[]{:S(2)}) %collective-permute-start.1) | collective-permute-done | bytes 524320 | tf_op jit(solution)/shard_map/ppermute | solution.py:449
  40.2 0.0 copy-start.8
  40.2 0.0 collective-permute-done.5.other_ref
  40.2 0.0 copy-start.6
  40.2 0.8 copy-done.6
  41.0 2.5 %shard_map.96 = (bf16[16,176,128]{2,1,0:T(8,128)(2,1)}, f32[4,264,128]{2,1,0:T(8,128)}) custom-call(s32[1]{0:T(128)} %bitcast.4.base_ref.core_ref, f32[4,264,128]{2,1,0:T(8,128)} %get-tuple-element.28.own_ref, f32[4,264,128]{2,1,0:T(8,128)} %copy-done.6), custom_call_target="tpu_custom_call" | custom-call | tf_op jit(solution)/shard_map/pallas_call | solution.py:440
  43.6 14.4 %all_to_all.20.message_ref = bf16[16,176,128]{2,1,0:T(8,128)(2,1)} all-to-all(bf16[16,176,128]{2,1,0:T(8,128)(2,1)} %get-tuple-element.30), channel_id=1, replica_groups=mesh['y'=4,'x'=4,'core'=2,'head'=4] {'y','x'}, dimensions={0} | all-to-all | bytes 1441792 | tf_op jit(solution)/shard_map/all_to_all | solution.py:458
  58.0 3.6 %shard_map.97 = bf16[16,32,128]{2,1,0:T(8,128)(2,1)} custom-call(bf16[16,176,128]{2,1,0:T(8,128)(2,1)} %all_to_all.20.message_ref), custom_call_target="tpu_custom_call" | custom-call | tf_op jit(solution)/shard_map/pallas_call | solution.py:440
  61.6 0.0 copy-done.7
  61.6 0.0 copy-done.8
  61.6 11.0 %all_to_all.21 = bf16[16,32,128]{2,1,0:T(8,128)(2,1)} all-to-all(bf16[16,32,128]{2,1,0:T(8,128)(2,1)} %shard_map.97), channel_id=1, replica_groups=mesh['y'=4,'x'=4,'core'=2,'head'=4] {'y','x'}, dimensions={0} | all-to-all | bytes 262144 | tf_op jit(solution)/shard_map/all_to_all | solution.py:458
  72.6 2.1 %shard_map.98 = (bf16[4,128,128]{2,1,0:T(8,128)(2,1)}, bf16[4,128,128]{2,1,0:T(8,128)(2,1)}) custom-call(s32[1]{0:T(128)} %bitcast.4.base_ref.core_ref, bf16[4,128,128]{2,1,0:T(8,128)(2,1)} %bitcast.31, f32[4,264,128]{2,1,0:T(8,128)} %get-tuple-element.31.early_ref), custom_call_target="tpu_custom_call" | custom-call | tf_op jit(solution)/shard_map/pallas_call | solution.py:440
  74.7 2.5 %shard_map.99 = bf16[512,512]{1,0:T(8,128)(2,1)} custom-call(bf16[512,512]{1,0:T(8,128)(2,1)} %get-tuple-element.26.reach_ref, f32[512,512]{1,0:T(8,128)} %get-tuple-element.27.local_ref, bf16[4,128,128]{2,1,0:T(8,128)(2,1)} %get-tuple-element.32.state_ref), custom_call_target="tpu_custom_call" | custom-call | tf_op jit(solution)/shard_map/pallas_call | solution.py:440
  77.2 0.0 copy-start.15
  77.2 5.3 %all-to-all-start.2 = ((bf16[4,128,512]{2,1,0:T(8,128)(2,1)}), bf16[4,128,512]{2,1,0:T(8,128)(2,1)S(1)}, u32[]{:S(2)}, u32[]{:S(2)}) async-start(bf16[4,128,512]{2,1,0:T(8,128)(2,1)} %bitcast.26), calls=%async_computation.2 | async-start | bytes 1048576 | tf_op jit(solution)/shard_map/all_to_all | solution.py:458
  82.5 0.0 copy-done.15
  82.5 0.0 collective-permute-start.6
  82.5 1.3 %collective-permute-done.6.state_ref = bf16[4,128,128]{2,1,0:T(8,128)(2,1)S(1)} collective-permute-done((bf16[4,128,128]{2,1,0:T(8,128)(2,1)S(1)}, bf16[4,128,128]{2,1,0:T(8,128)(2,1)S(1)}, u32[]{:S(2)}, u32[]{:S(2)}) %collective-permute-start.6) | collective-permute-done | bytes 131104 | tf_op jit(solution)/shard_map/ppermute | solution.py:510
  83.8 0.7 copy-done.14
  84.5 2.5 %shard_map.100 = bf16[512,512]{1,0:T(8,128)(2,1)} custom-call(bf16[512,512]{1,0:T(8,128)(2,1)} %get-tuple-element.33.reach_ref, f32[512,512]{1,0:T(8,128)} %get-tuple-element.34.local_ref, bf16[4,128,128]{2,1,0:T(8,128)(2,1)} %copy-done.14), custom_call_target="tpu_custom_call" | custom-call | tf_op jit(solution)/shard_map/pallas_call | solution.py:440
  87.0 4.5 %all-to-all-done.2.left_ref = bf16[4,128,512]{2,1,0:T(8,128)(2,1)S(1)} async-done(((bf16[4,128,512]{2,1,0:T(8,128)(2,1)}), bf16[4,128,512]{2,1,0:T(8,128)(2,1)S(1)}, u32[]{:S(2)}, u32[]{:S(2)}) %all-to-all-start.2) | async-done | bytes 524320 | tf_op jit(solution)/shard_map/all_to_all | solution.py:458
  91.4 0.8 copy-done.1
  92.2 3.5 %all-to-all-start.3 = ((bf16[4,128,512]{2,1,0:T(8,128)(2,1)}), bf16[4,128,512]{2,1,0:T(8,128)(2,1)S(1)}, u32[]{:S(2)}, u32[]{:S(2)}) async-start(bf16[4,128,512]{2,1,0:T(8,128)(2,1)} %bitcast.25), calls=%async_computation.3 | async-start | bytes 1048576 | tf_op jit(solution)/shard_map/all_to_all | solution.py:458
  95.7 0.0 copy-done.3
  95.7 1.2 copy.20
  97.0 12.1 %attend.1 = (bf16[128,1024]{1,0:T(8,128)(2,1)}, bf16[128,1024]{1,0:T(8,128)(2,1)}, bf16[128,1024]{1,0:T(8,128)(2,1)}, bf16[128,1024]{1,0:T(8,128)(2,1)}) custom-call(s32[1]{0:T(128)} %bitcast.first_ref, s32[1]{0:T(128)} %bitcast.1.turn_ref, bf16[512,1024]{1,0:T(8,128)(2,1)} %bitcast.24, bf16[512,512]{1,0:T(8,128)(2,1)} %copy-done, ...), custom_call_target="tpu_custom_call" | custom-call | tf_op jit(solution)/shard_map/attend/pallas_call | solution.py:381
  109.1 1.4 %collective-permute-start.2 = (bf16[128,1024]{1,0:T(8,128)(2,1)}, bf16[128,1024]{1,0:T(8,128)(2,1)S(1)}, u32[]{:S(2)}, u32[]{:S(2)}) collective-permute-start(bf16[128,1024]{1,0:T(8,128)(2,1)} %get-tuple-element.23), channel_id=1, source_target_pairs={{0,1},{1,2},{2,3},{3,0},{4,5},{5,6},{6,7},{7,4},{8,9},{9,10},{10,1... | collective-permute-start | bytes 786440 | tf_op jit(solution)/shard_map/ppermute | solution.py:449
  110.5 2.4 %collective-permute-start.3 = (bf16[128,1024]{1,0:T(8,128)(2,1)}, bf16[128,1024]{1,0:T(8,128)(2,1)S(1)}, u32[]{:S(2)}, u32[]{:S(2)}) collective-permute-start(bf16[128,1024]{1,0:T(8,128)(2,1)} %get-tuple-element.24), channel_id=1, source_target_pairs={{0,2},{1,3},{2,0},{3,1},{4,6},{5,7},{6,4},{7,5},{8,10},{9,11},{10,... | collective-permute-start | bytes 786440 | tf_op jit(solution)/shard_map/ppermute | solution.py:449
  112.9 1.2 collective-permute-start.4
  114.0 0.6 and_select_fusion.place_ref
  114.6 0.7 pad_add_fusion.place_ref
  115.2 3.2 %collective-permute-done.2.refs_1_ = bf16[128,1024]{1,0:T(8,128)(2,1)S(1)} collective-permute-done((bf16[128,1024]{1,0:T(8,128)(2,1)}, bf16[128,1024]{1,0:T(8,128)(2,1)S(1)}, u32[]{:S(2)}, u32[]{:S(2)}) %collective-permute-start.2) | collective-permute-done | bytes 262176 | tf_op jit(solution)/shard_map/ppermute | solution.py:449
  118.4 6.5 %collective-permute-done.3.refs_2_ = bf16[128,1024]{1,0:T(8,128)(2,1)S(1)} collective-permute-done((bf16[128,1024]{1,0:T(8,128)(2,1)}, bf16[128,1024]{1,0:T(8,128)(2,1)S(1)}, u32[]{:S(2)}, u32[]{:S(2)}) %collective-permute-start.3) | collective-permute-done | bytes 262176 | tf_op jit(solution)/shard_map/ppermute | solution.py:449
  124.9 0.0 collective-permute-done.4.refs_3_
  124.9 0.0 copy-done.9
  124.9 0.7 copy-done.10
  125.6 0.1 copy-done.11
  125.7 2.2 %shard_map.95 = bf16[128,4096]{1,0:T(8,128)(2,1)} custom-call(s32[4]{0:T(128)} %and_select_fusion.place_ref, bf16[128,1024]{1,0:T(8,128)(2,1)} %get-tuple-element.22.refs_0_, bf16[128,1024]{1,0:T(8,128)(2,1)} %copy-done.9, bf16[128,1024]{1,0:T(8,128)(2,1)} %copy-done.10, bf16[128,1024]{1,0:T(8,128)(2,1)} %copy-done.11), custom_call_target="tpu_custom_call" | custom-call | tf_op jit(solution)/shard_map/pallas_call | solution.py:430
  127.9 0.0 all-to-all-done.3.right_ref
  127.9 0.0 copy-start.2
  127.9 0.8 copy-done.2
  128.7 2.2 %shard_map.101 = bf16[128,4096]{1,0:T(8,128)(2,1)} custom-call(s32[2]{0:T(128)} %pad_add_fusion.place_ref, bf16[4,128,512]{2,1,0:T(8,128)(2,1)} %copy-done.1, bf16[4,128,512]{2,1,0:T(8,128)(2,1)} %copy-done.2), custom_call_target="tpu_custom_call" | custom-call | tf_op jit(solution)/shard_map/pallas_call | solution.py:430
  (6 shorter events, 0.0 us)
Async XLA Ops:
  0.6 2.6 %copy-start.4 = (bf16[512,8,128]{2,1,0:T(8,128)(2,1)S(1)}, bf16[512,8,128]{2,1,0:T(8,128)(2,1)}, u32[]{:S(2)}) copy-start(bf16[512,8,128]{2,1,0:T(8,128)(2,1)} %param.13) | copy-start | bytes 3145732
  0.6 2.6 %copy-start.5 = (bf16[512,8,128]{2,1,0:T(8,128)(2,1)S(1)}, bf16[512,8,128]{2,1,0:T(8,128)(2,1)}, u32[]{:S(2)}) copy-start(bf16[512,8,128]{2,1,0:T(8,128)(2,1)} %param.12) | copy-start | bytes 3145732
  5.1 10.4 %copy-start.12 = (bf16[512,2,128]{2,1,0:T(2,128)(2,1)S(1)}, bf16[512,2,128]{2,1,0:T(2,128)(2,1)}, u32[]{:S(2)}) copy-start(bf16[512,2,128]{2,1,0:T(2,128)(2,1)} %param.10) | copy-start | bytes 786436
  5.1 10.4 %copy-start.13 = (bf16[512,2,128]{2,1,0:T(2,128)(2,1)S(1)}, bf16[512,2,128]{2,1,0:T(2,128)(2,1)}, u32[]{:S(2)}) copy-start(bf16[512,2,128]{2,1,0:T(2,128)(2,1)} %param.9) | copy-start | bytes 786436
  14.1 26.1 %collective-permute-start.5 = (f32[4,264,128]{2,1,0:T(8,128)}, f32[4,264,128]{2,1,0:T(8,128)S(1)}, u32[]{:S(2)}, u32[]{:S(2)}) collective-permute-start(f32[4,264,128]{2,1,0:T(8,128)} %get-tuple-element.29), channel_id=1, source_target_pairs={{0,4},{4,0},{1,5},{5,1},{2,6},{6,2},{3,7},{7,3},{8,12},{12,8},{9,1... | collective-permute-start | bytes 1622024 | tf_op jit(solution)/shard_map/ppermute | solution.py:478
  17.3 11.5 %copy-start = (bf16[512,512]{1,0:T(8,128)(2,1)}, bf16[512,512]{1,0:T(8,128)(2,1)S(1)}, u32[]{:S(2)}) copy-start(bf16[512,512]{1,0:T(8,128)(2,1)S(1)} %reshape.41.own_ref) | copy-start | bytes 1572868
  17.3 12.0 %collective-permute-start = (bf16[512,512]{1,0:T(8,128)(2,1)S(1)}, bf16[512,512]{1,0:T(8,128)(2,1)S(1)}, u32[]{:S(2)}, u32[]{:S(2)}) collective-permute-start(bf16[512,512]{1,0:T(8,128)(2,1)S(1)} %reshape.41.own_ref), channel_id=1, source_target_pairs={{0,4},{4,8},{8,12},{12,16},{16,20},{20,24},{24,28},{28,32},{32,36}... | collective-permute-start | bytes 1572872 | tf_op jit(solution)/shard_map/ppermute | solution.py:449
  18.6 21.6 %collective-permute-start.1 = (bf16[512,512]{1,0:T(8,128)(2,1)S(1)}, bf16[512,512]{1,0:T(8,128)(2,1)S(1)}, u32[]{:S(2)}, u32[]{:S(2)}) collective-permute-start(bf16[512,512]{1,0:T(8,128)(2,1)S(1)} %reshape.41.own_ref), channel_id=1, source_target_pairs={{0,8},{4,12},{8,16},{12,20},{16,24},{20,28},{24,32},{28,36},{32,40... | collective-permute-start | bytes 1572872 | tf_op jit(solution)/shard_map/ppermute | solution.py:449
  29.2 32.4 %copy-start.7 = (bf16[512,512]{1,0:T(8,128)(2,1)}, bf16[512,512]{1,0:T(8,128)(2,1)S(1)}, u32[]{:S(2)}) copy-start(bf16[512,512]{1,0:T(8,128)(2,1)S(1)} %collective-permute-done.near_ref) | copy-start | bytes 1572868
  40.2 21.4 %copy-start.8 = (bf16[512,512]{1,0:T(8,128)(2,1)}, bf16[512,512]{1,0:T(8,128)(2,1)S(1)}, u32[]{:S(2)}) copy-start(bf16[512,512]{1,0:T(8,128)(2,1)S(1)} %collective-permute-done.1.far_ref) | copy-start | bytes 1572868
  40.2 0.8 copy-start.6
  77.2 5.3 %copy-start.15 = (bf16[4,128,128]{2,1,0:T(8,128)(2,1)S(1)}, bf16[4,128,128]{2,1,0:T(8,128)(2,1)}, u32[]{:S(2)}) copy-start(bf16[4,128,128]{2,1,0:T(8,128)(2,1)} %get-tuple-element.35) | copy-start | bytes 393220
  77.2 14.2 %all-to-all-start.2 = ((bf16[4,128,512]{2,1,0:T(8,128)(2,1)}), bf16[4,128,512]{2,1,0:T(8,128)(2,1)S(1)}, u32[]{:S(2)}, u32[]{:S(2)}) async-start(bf16[4,128,512]{2,1,0:T(8,128)(2,1)} %bitcast.26), calls=%async_computation.2 | async-start | bytes 1048576 | tf_op jit(solution)/shard_map/all_to_all | solution.py:458
  82.5 1.3 %collective-permute-start.6 = (bf16[4,128,128]{2,1,0:T(8,128)(2,1)S(1)}, bf16[4,128,128]{2,1,0:T(8,128)(2,1)S(1)}, u32[]{:S(2)}, u32[]{:S(2)}) collective-permute-start(bf16[4,128,128]{2,1,0:T(8,128)(2,1)S(1)} %copy-done.15), channel_id=1, source_target_pairs={{0,4},{4,0},{1,5},{5,1},{2,6},{6,2},{3,7},{7,3},{8,12},{12,8},{9,1... | collective-permute-start | bytes 393224 | tf_op jit(solution)/shard_map/ppermute | solution.py:510
  83.8 0.7 copy-start.14
  87.0 8.8 %copy-start.3 = (bf16[512,8,128]{2,1,0:T(8,128)(2,1)S(1)}, bf16[512,8,128]{2,1,0:T(8,128)(2,1)}, u32[]{:S(2)}) copy-start(bf16[512,8,128]{2,1,0:T(8,128)(2,1)} %param.8) | copy-start | bytes 3145732
  91.4 0.8 copy-start.1
  92.2 35.7 %all-to-all-start.3 = ((bf16[4,128,512]{2,1,0:T(8,128)(2,1)}), bf16[4,128,512]{2,1,0:T(8,128)(2,1)S(1)}, u32[]{:S(2)}, u32[]{:S(2)}) async-start(bf16[4,128,512]{2,1,0:T(8,128)(2,1)} %bitcast.25), calls=%async_computation.3 | async-start | bytes 1048576 | tf_op jit(solution)/shard_map/all_to_all | solution.py:458
  109.1 9.4 %collective-permute-start.2 = (bf16[128,1024]{1,0:T(8,128)(2,1)}, bf16[128,1024]{1,0:T(8,128)(2,1)S(1)}, u32[]{:S(2)}, u32[]{:S(2)}) collective-permute-start(bf16[128,1024]{1,0:T(8,128)(2,1)} %get-tuple-element.23), channel_id=1, source_target_pairs={{0,1},{1,2},{2,3},{3,0},{4,5},{5,6},{6,7},{7,4},{8,9},{9,10},{10,1... | collective-permute-start | bytes 786440 | tf_op jit(solution)/shard_map/ppermute | solution.py:449
  110.5 14.4 %collective-permute-start.3 = (bf16[128,1024]{1,0:T(8,128)(2,1)}, bf16[128,1024]{1,0:T(8,128)(2,1)S(1)}, u32[]{:S(2)}, u32[]{:S(2)}) collective-permute-start(bf16[128,1024]{1,0:T(8,128)(2,1)} %get-tuple-element.24), channel_id=1, source_target_pairs={{0,2},{1,3},{2,0},{3,1},{4,6},{5,7},{6,4},{7,5},{8,10},{9,11},{10,... | collective-permute-start | bytes 786440 | tf_op jit(solution)/shard_map/ppermute | solution.py:449
  112.9 12.0 %collective-permute-start.4 = (bf16[128,1024]{1,0:T(8,128)(2,1)}, bf16[128,1024]{1,0:T(8,128)(2,1)S(1)}, u32[]{:S(2)}, u32[]{:S(2)}) collective-permute-start(bf16[128,1024]{1,0:T(8,128)(2,1)} %get-tuple-element.25), channel_id=1, source_target_pairs={{0,3},{1,0},{2,1},{3,2},{4,7},{5,4},{6,5},{7,6},{8,11},{9,8},{10,9... | collective-permute-start | bytes 786440 | tf_op jit(solution)/shard_map/ppermute | solution.py:449
  118.4 6.5 %copy-start.9 = (bf16[128,1024]{1,0:T(8,128)(2,1)}, bf16[128,1024]{1,0:T(8,128)(2,1)S(1)}, u32[]{:S(2)}) copy-start(bf16[128,1024]{1,0:T(8,128)(2,1)S(1)} %collective-permute-done.2.refs_1_) | copy-start | bytes 786436
  124.9 0.7 copy-start.10
  124.9 0.8 copy-start.11
  127.9 0.8 copy-start.2

commit v4 on v3

--- a/solution.py
+++ b/solution.py
@@ -398,12 +398,13 @@
     )(first, turn, query, own, near, far)
 
 
-def join_turns_body(place_ref, *refs):
+def join_turns_body(rank_ref, *refs):
     *in_refs, out_ref, done = refs
     width = in_refs[0].shape[1]
+    count = len(in_refs)
     copies = []
     for d, in_ref in enumerate(in_refs):
-        lanes = pl.ds(pl.multiple_of(place_ref[d] * width, width), width)
+        lanes = pl.ds(pl.multiple_of((rank_ref[0] + count - d) % count * width, width), width)
         copies.append(pltpu.make_async_copy(in_ref, out_ref.at[:, lanes], done.at[d]))
     for copy in copies:
         copy.start()
@@ -411,12 +412,13 @@
         copy.wait()
 
 
-def join_halves_body(place_ref, left_ref, right_ref, out_ref, done):
+def join_halves_body(core_ref, left_ref, right_ref, out_ref, done):
     count, _, width = left_ref.shape
     copies = []
     for k, in_ref in enumerate((left_ref, right_ref)):
         for d in range(count):
-            lanes = pl.ds(pl.multiple_of((2 * d + place_ref[k]) * width, width), width)
+            side = core_ref[0] if k == 0 else 1 - core_ref[0]
+            lanes = pl.ds(pl.multiple_of((2 * d + side) * width, width), width)
             copies.append(
                 pltpu.make_async_copy(in_ref.at[d], out_ref.at[:, lanes], done.at[k * count + d])
             )
@@ -433,7 +435,11 @@
         out_specs=pl.BlockSpec(memory_space=pltpu.HBM),
         out_shape=jax.ShapeDtypeStruct((rows, width), bf16),
         scratch_shapes=[pltpu.SemaphoreType.DMA((copies,))],
-    )(place, *operands)
+    )(place, *map(onchip, operands))
+
+
+def onchip(operand):
+    return pltpu.with_memory_space_constraint(operand, pltpu.VMEM)
 
 
 def onchip_call(body, shapes, scalars, *operands):
@@ -442,7 +448,7 @@
         in_specs=[SCALAR] * len(scalars) + [ONCHIP] * len(operands),
         out_specs=[ONCHIP] * len(shapes),
         out_shape=shapes,
-    )(*scalars, *operands)
+    )(*scalars, *map(onchip, operands))
 
 
 def ring(block, axes, distance, size):
@@ -514,10 +520,8 @@
     (delta_b,) = onchip_call(finish_body, halves, [], reach_b, local_b, received)
     delta_b = exchange(delta_b.reshape(count, turn, -1), "head")
     wide = count * delta_query.shape[1] * HEAD
-    places = (rank - jnp.arange(count, dtype=jnp.int32)) % count
-    attn_out = join_call(join_turns_body, count, turn, wide, places, *attn)
-    sides = jnp.concatenate((core, 1 - core))
-    delta_out = join_call(join_halves_body, 2 * count, turn, wide, sides, delta_a, delta_b)
+    attn_out = join_call(join_turns_body, count, turn, wide, rank, *attn)
+    delta_out = join_call(join_halves_body, 2 * count, turn, wide, core, delta_a, delta_b)
     return (attn_out, delta_out)
 
 

time: 132 us -> 124 us (0.939)
  Pallas kernels: 47.7 us -> 39 us
  waiting for transfers between devices: 26.9 us -> 30.2 us
    pallas_call x5, Pallas kernels: 13.2 us -> 6.98 us  [onchip_call(): pl.pallas_call(body, in_specs=[SCALAR] * len(scalars) + [ONCHIP] * len(op...]
    pallas_call x2, Pallas kernels: 4.43 us -> 2.02 us  [join_call(): pl.pallas_call(body, in_specs=[SCALAR] + [ONCHIP] * len(operands), out_sp...]
    all_to_all x2, waiting for transfers between devices: 4.47 us -> 6.69 us  [exchange(): return lax.all_to_all(block, axes, split_axis=0, concat_axis=0, tiled=True)]
    unnamed x34 -> x36, local copies, waits for them, and re-layouts: 7.76 us -> 7.61 us
  transfers between devices with their start and end apart: 9 -> 9, of which waited for: 6 -> 6; matrix products, arithmetic and copies ran while one was open for 3% -> 2% of each run, Pallas kernels for 20% -> 19%
where the time goes in v4:
time: 124 us; the launch traced here: 123 us
  Pallas kernels  39 us (31%)
  waiting for transfers between devices  30.2 us (24%)
  blocking collectives  24.5 us (20%)
  starting transfers between devices  17.5 us (14%)
  local copies, waits for them, and re-layouts  10.5 us (8%)
    all_to_all x2, blocking collectives, exchange(): return lax.all_to_all(block, axes, split_axis=0, concat_axis=0, tiled=True)  24.5 us
    ppermute x5, waiting for transfers between devices, ring(): lax.ppermute(block, axes, [(i, (i + distance) % size) for i in range(size)])  22.2 us
    pallas_call x2, Pallas kernels, delta_local(): pl.pallas_call(delta_body, grid_spec=pltpu.PrefetchScalarGridSpec(num_sca...  17.9 us
    pallas_call x1, Pallas kernels, attend(): pl.pallas_call(attend_body, grid_spec=pltpu.PrefetchScalarGridSpec(num_sc...  12.1 us
    all_to_all x2, starting transfers between devices, exchange(): return lax.all_to_all(block, axes, split_axis=0, concat_axis=0, tiled=True)  8.63 us
    unnamed x36, local copies, waits for them, and re-layouts  7.61 us
    ppermute x5, starting transfers between devices, ring(): lax.ppermute(block, axes, [(i, (i + distance) % size) for i in range(size)])  7.49 us
    pallas_call x5, Pallas kernels, onchip_call(): pl.pallas_call(body, in_specs=[SCALAR] * len(scalars) + [ONCHIP] * len(op...  6.98 us
  transfers between devices with their start and end apart: 9, of which 6 were waited for; matrix products, arithmetic and copies ran while one was open for 2% of the time, Pallas kernels for 19%

profile of v4, /device:TPU:1, one launch (start us, length us, event | category | flops | bytes accessed | tf_op | source)
XLA Modules:
  0.0 123.4 jit_solution(2150347159529729846)
XLA Ops:
  0.6 0.0 copy-start.10
  0.6 0.0 copy-start.11
  0.7 2.6 %copy.19 = bf16[64,8,8,128]{3,1,2,0:T(8,128)(2,1)} copy(bf16[64,8,8,128]{3,2,1,0:T(8,128)(2,1)} %bitcast.28) | data formatting | bytes 2097152
  3.3 0.0 copy-done.10
  3.3 0.0 copy-done.11
  3.3 1.8 %copy_bitcast_fusion = (bf16[512,1024]{1,0:T(8,128)(2,1)}, bf16[512,1024]{1,0:T(8,128)(2,1)}) fusion(bf16[64,8,8,128]{3,2,1,0:T(8,128)(2,1)S(1)} %bitcast.30, bf16[64,8,8,128]{3,2,1,0:T(8,128)(2,1)S(1)} %bitcast.31), kind=kLoop, calls=%fused_computation | loop fusion | bytes 4194304 | tf_op jit(solution)/shard_map/reshape | solution.py:479
  5.1 0.0 copy-start.14
  5.1 0.0 copy-start.15
  5.1 9.0 %delta_local.3 = (f32[512,512]{1,0:T(8,128)}, bf16[512,512]{1,0:T(8,128)(2,1)}, f32[4,264,128]{2,1,0:T(8,128)}) custom-call(s32[1]{0:T(128)S(6)} %sub.7.base_ref, bf16[512,1024]{1,0:T(8,128)(2,1)} %bitcast.23, bf16[512,1024]{1,0:T(8,128)(2,1)} %get-tuple-element.37.k_ref, bf16[512,1024]{1,0:T(8,128)(2,1)} %get-tuple-element.36.v_ref, f32[8,512]{1,0:T(8,128)} %log_ref.3, ...), custom_call_target="tpu_custom_call" | custom-call | tf_op jit(solution)/shard_map/delta_local/pallas_call | solution.py:212
  14.1 1.4 %collective-permute-start.5 = (f32[4,264,128]{2,1,0:T(8,128)}, f32[4,264,128]{2,1,0:T(8,128)S(1)}, u32[]{:S(2)}, u32[]{:S(2)}) collective-permute-start(f32[4,264,128]{2,1,0:T(8,128)} %get-tuple-element.29), channel_id=1, source_target_pairs={{0,4},{4,0},{1,5},{5,1},{2,6},{6,2},{3,7},{7,3},{8,12},{12,8},{9,1... | collective-permute-start | bytes 1622024 | tf_op jit(solution)/shard_map/ppermute | solution.py:484
  15.5 0.0 copy-done.14
  15.5 0.0 copy-done.15
  15.5 0.7 pad_maximum_fusion
  16.3 0.8 copy.10
  17.1 0.2 reshape.40.own_ref
  17.3 0.0 copy-start.8
  17.3 1.3 %collective-permute-start = (bf16[512,512]{1,0:T(8,128)(2,1)S(1)}, bf16[512,512]{1,0:T(8,128)(2,1)S(1)}, u32[]{:S(2)}, u32[]{:S(2)}) collective-permute-start(bf16[512,512]{1,0:T(8,128)(2,1)S(1)} %reshape.40.own_ref), channel_id=1, source_target_pairs={{0,4},{4,8},{8,12},{12,16},{16,20},{20,24},{24,28},{28,32},{32,36}... | collective-permute-start | bytes 1572872 | tf_op jit(solution)/shard_map/ppermute | solution.py:455
  18.6 1.2 collective-permute-start.1
  19.8 8.9 %delta_local.2 = (f32[512,512]{1,0:T(8,128)}, bf16[512,512]{1,0:T(8,128)(2,1)}, f32[4,264,128]{2,1,0:T(8,128)}) custom-call(s32[1]{0:T(128)} %bitcast.4.base_ref.core_ref, bf16[512,1024]{1,0:T(8,128)(2,1)} %bitcast.24, bf16[512,1024]{1,0:T(8,128)(2,1)} %get-tuple-element.37.k_ref, bf16[512,1024]{1,0:T(8,128)(2,1)} %get-tuple-element.36.v_ref, ...), custom_call_target="tpu_custom_call" | custom-call | tf_op jit(solution)/shard_map/delta_local/pallas_call | solution.py:212
  28.7 0.0 copy-done.8
  28.7 0.5 collective-permute-done.near_ref
  29.2 0.0 copy-start.12
  29.2 11.0 %collective-permute-done.1.far_ref = bf16[512,512]{1,0:T(8,128)(2,1)S(1)} collective-permute-done((bf16[512,512]{1,0:T(8,128)(2,1)S(1)}, bf16[512,512]{1,0:T(8,128)(2,1)S(1)}, u32[]{:S(2)}, u32[]{:S(2)}) %collective-permute-start.1) | collective-permute-done | bytes 524320 | tf_op jit(solution)/shard_map/ppermute | solution.py:455
  40.2 0.0 copy-start.13
  40.2 0.8 copy-done.13
  41.0 0.0 collective-permute-done.5.other_ref
  41.0 0.0 copy-start.3
  41.0 1.0 copy-done.3
  42.0 1.3 %shard_map.96 = (bf16[16,176,128]{2,1,0:T(8,128)(2,1)}, f32[4,264,128]{2,1,0:T(8,128)}) custom-call(s32[1]{0:T(128)} %bitcast.4.base_ref.core_ref, f32[4,264,128]{2,1,0:T(8,128)S(1)} %copy-done.3, f32[4,264,128]{2,1,0:T(8,128)S(1)} %collective-permute-done.5.other_ref), custom_call_target="tpu_custom_call" | custom-call | tf_op jit(solution)/shard_map/pallas_call | solution.py:446
  43.4 0.0 copy-done.12
  43.4 0.0 copy-start.2
  43.4 14.1 %all_to_all.20.message_ref = bf16[16,176,128]{2,1,0:T(8,128)(2,1)S(1)} all-to-all(bf16[16,176,128]{2,1,0:T(8,128)(2,1)} %get-tuple-element.30), channel_id=1, replica_groups=mesh['y'=4,'x'=4,'core'=2,'head'=4] {'y','x'}, dimensions={0} | all-to-all | bytes 1441792 | tf_op jit(solution)/shard_map/all_to_all | solution.py:464
  57.5 0.0 copy-start.1
  57.5 2.5 %shard_map.97 = bf16[16,32,128]{2,1,0:T(8,128)(2,1)} custom-call(bf16[16,176,128]{2,1,0:T(8,128)(2,1)S(1)} %all_to_all.20.message_ref), custom_call_target="tpu_custom_call" | custom-call | tf_op jit(solution)/shard_map/pallas_call | solution.py:446
  60.0 0.0 copy-start.5
  60.0 10.4 %all_to_all.21 = bf16[16,32,128]{2,1,0:T(8,128)(2,1)S(1)} all-to-all(bf16[16,32,128]{2,1,0:T(8,128)(2,1)} %shard_map.97), channel_id=1, replica_groups=mesh['y'=4,'x'=4,'core'=2,'head'=4] {'y','x'}, dimensions={0} | all-to-all | bytes 262144 | tf_op jit(solution)/shard_map/all_to_all | solution.py:464
  70.4 0.0 copy-done.2
  70.4 1.0 shard_map.98
  71.4 0.0 copy-done.1
  71.4 0.0 copy-done.5
  71.4 0.9 copy-done.7
  72.3 1.1 shard_map.99
  73.4 5.2 %all-to-all-start.2 = ((bf16[4,128,512]{2,1,0:T(8,128)(2,1)}), bf16[4,128,512]{2,1,0:T(8,128)(2,1)S(1)}, u32[]{:S(2)}, u32[]{:S(2)}) async-start(bf16[4,128,512]{2,1,0:T(8,128)(2,1)} %bitcast.27), calls=%async_computation.2 | async-start | bytes 1048576 | tf_op jit(solution)/shard_map/all_to_all | solution.py:464
  78.6 0.0 copy-done.16
  78.6 0.0 collective-permute-start.6
  78.6 1.3 %collective-permute-done.6.state_ref = bf16[4,128,128]{2,1,0:T(8,128)(2,1)S(1)} collective-permute-done((bf16[4,128,128]{2,1,0:T(8,128)(2,1)S(1)}, bf16[4,128,128]{2,1,0:T(8,128)(2,1)S(1)}, u32[]{:S(2)}, u32[]{:S(2)}) %collective-permute-start.6) | collective-permute-done | bytes 131104 | tf_op jit(solution)/shard_map/ppermute | solution.py:516
  79.9 0.0 copy-done.4
  79.9 0.0 copy-done
  79.9 1.1 shard_map.100
  81.0 6.7 %all-to-all-done.2.left_ref = bf16[4,128,512]{2,1,0:T(8,128)(2,1)S(1)} async-done(((bf16[4,128,512]{2,1,0:T(8,128)(2,1)}), bf16[4,128,512]{2,1,0:T(8,128)(2,1)S(1)}, u32[]{:S(2)}, u32[]{:S(2)}) %all-to-all-start.2) | async-done | bytes 524320 | tf_op jit(solution)/shard_map/all_to_all | solution.py:464
  87.7 3.5 %all-to-all-start.3 = ((bf16[4,128,512]{2,1,0:T(8,128)(2,1)}), bf16[4,128,512]{2,1,0:T(8,128)(2,1)S(1)}, u32[]{:S(2)}, u32[]{:S(2)}) async-start(bf16[4,128,512]{2,1,0:T(8,128)(2,1)} %bitcast.26), calls=%async_computation.3 | async-start | bytes 1048576 | tf_op jit(solution)/shard_map/all_to_all | solution.py:464
  91.2 0.0 copy-done.9
  91.2 1.2 %copy.20 = bf16[64,8,8,128]{3,1,2,0:T(8,128)(2,1)} copy(bf16[64,8,8,128]{3,2,1,0:T(8,128)(2,1)S(1)} %bitcast.29) | data formatting | bytes 2097152
  92.5 12.1 %attend.1 = (bf16[128,1024]{1,0:T(8,128)(2,1)}, bf16[128,1024]{1,0:T(8,128)(2,1)}, bf16[128,1024]{1,0:T(8,128)(2,1)}, bf16[128,1024]{1,0:T(8,128)(2,1)}) custom-call(s32[1]{0:T(128)} %bitcast.1.first_ref, s32[1]{0:T(128)} %bitcast.turn_ref.rank_ref, bf16[512,1024]{1,0:T(8,128)(2,1)} %bitcast.25, bf16[512,512]{1,0:T(8,128)(2,1)} %copy-done.8, ...), custom_call_target="tpu_custom_call" | custom-call | tf_op jit(solution)/shard_map/attend/pallas_call | solution.py:381
  104.5 1.4 %collective-permute-start.2 = (bf16[128,1024]{1,0:T(8,128)(2,1)}, bf16[128,1024]{1,0:T(8,128)(2,1)S(1)}, u32[]{:S(2)}, u32[]{:S(2)}) collective-permute-start(bf16[128,1024]{1,0:T(8,128)(2,1)} %get-tuple-element.23), channel_id=1, source_target_pairs={{0,1},{1,2},{2,3},{3,0},{4,5},{5,6},{6,7},{7,4},{8,9},{9,10},{10,1... | collective-permute-start | bytes 786440 | tf_op jit(solution)/shard_map/ppermute | solution.py:455
  105.9 2.4 %collective-permute-start.3 = (bf16[128,1024]{1,0:T(8,128)(2,1)}, bf16[128,1024]{1,0:T(8,128)(2,1)S(1)}, u32[]{:S(2)}, u32[]{:S(2)}) collective-permute-start(bf16[128,1024]{1,0:T(8,128)(2,1)} %get-tuple-element.24), channel_id=1, source_target_pairs={{0,2},{1,3},{2,0},{3,1},{4,6},{5,7},{6,4},{7,5},{8,10},{9,11},{10,... | collective-permute-start | bytes 786440 | tf_op jit(solution)/shard_map/ppermute | solution.py:455
  108.3 1.2 collective-permute-start.4
  109.5 4.2 %collective-permute-done.2.refs_1_ = bf16[128,1024]{1,0:T(8,128)(2,1)S(1)} collective-permute-done((bf16[128,1024]{1,0:T(8,128)(2,1)}, bf16[128,1024]{1,0:T(8,128)(2,1)S(1)}, u32[]{:S(2)}, u32[]{:S(2)}) %collective-permute-start.2) | collective-permute-done | bytes 262176 | tf_op jit(solution)/shard_map/ppermute | solution.py:455
  113.7 6.5 %collective-permute-done.3.refs_2_ = bf16[128,1024]{1,0:T(8,128)(2,1)S(1)} collective-permute-done((bf16[128,1024]{1,0:T(8,128)(2,1)}, bf16[128,1024]{1,0:T(8,128)(2,1)S(1)}, u32[]{:S(2)}, u32[]{:S(2)}) %collective-permute-start.3) | collective-permute-done | bytes 262176 | tf_op jit(solution)/shard_map/ppermute | solution.py:455
  120.2 0.0 collective-permute-done.4.refs_3_
  120.2 0.9 copy-done.6
  121.2 1.0 shard_map.95
  122.2 0.0 all-to-all-done.3.right_ref
  122.2 1.0 shard_map.101
  (6 shorter events, 0.0 us)
Async XLA Ops:
  0.6 2.6 %copy-start.10 = (bf16[512,8,128]{2,1,0:T(8,128)(2,1)S(1)}, bf16[512,8,128]{2,1,0:T(8,128)(2,1)}, u32[]{:S(2)}) copy-start(bf16[512,8,128]{2,1,0:T(8,128)(2,1)} %param.13) | copy-start | bytes 3145732
  0.6 2.6 %copy-start.11 = (bf16[512,8,128]{2,1,0:T(8,128)(2,1)S(1)}, bf16[512,8,128]{2,1,0:T(8,128)(2,1)}, u32[]{:S(2)}) copy-start(bf16[512,8,128]{2,1,0:T(8,128)(2,1)} %param.12) | copy-start | bytes 3145732
  5.1 10.4 %copy-start.14 = (bf16[512,2,128]{2,1,0:T(2,128)(2,1)S(1)}, bf16[512,2,128]{2,1,0:T(2,128)(2,1)}, u32[]{:S(2)}) copy-start(bf16[512,2,128]{2,1,0:T(2,128)(2,1)} %param.10) | copy-start | bytes 786436
  5.1 10.4 %copy-start.15 = (bf16[512,2,128]{2,1,0:T(2,128)(2,1)S(1)}, bf16[512,2,128]{2,1,0:T(2,128)(2,1)}, u32[]{:S(2)}) copy-start(bf16[512,2,128]{2,1,0:T(2,128)(2,1)} %param.9) | copy-start | bytes 786436
  14.1 26.9 %collective-permute-start.5 = (f32[4,264,128]{2,1,0:T(8,128)}, f32[4,264,128]{2,1,0:T(8,128)S(1)}, u32[]{:S(2)}, u32[]{:S(2)}) collective-permute-start(f32[4,264,128]{2,1,0:T(8,128)} %get-tuple-element.29), channel_id=1, source_target_pairs={{0,4},{4,0},{1,5},{5,1},{2,6},{6,2},{3,7},{7,3},{8,12},{12,8},{9,1... | collective-permute-start | bytes 1622024 | tf_op jit(solution)/shard_map/ppermute | solution.py:484
  17.3 11.5 %copy-start.8 = (bf16[512,512]{1,0:T(8,128)(2,1)}, bf16[512,512]{1,0:T(8,128)(2,1)S(1)}, u32[]{:S(2)}) copy-start(bf16[512,512]{1,0:T(8,128)(2,1)S(1)} %reshape.40.own_ref) | copy-start | bytes 1572868
  17.3 12.0 %collective-permute-start = (bf16[512,512]{1,0:T(8,128)(2,1)S(1)}, bf16[512,512]{1,0:T(8,128)(2,1)S(1)}, u32[]{:S(2)}, u32[]{:S(2)}) collective-permute-start(bf16[512,512]{1,0:T(8,128)(2,1)S(1)} %reshape.40.own_ref), channel_id=1, source_target_pairs={{0,4},{4,8},{8,12},{12,16},{16,20},{20,24},{24,28},{28,32},{32,36}... | collective-permute-start | bytes 1572872 | tf_op jit(solution)/shard_map/ppermute | solution.py:455
  18.6 21.6 %collective-permute-start.1 = (bf16[512,512]{1,0:T(8,128)(2,1)S(1)}, bf16[512,512]{1,0:T(8,128)(2,1)S(1)}, u32[]{:S(2)}, u32[]{:S(2)}) collective-permute-start(bf16[512,512]{1,0:T(8,128)(2,1)S(1)} %reshape.40.own_ref), channel_id=1, source_target_pairs={{0,8},{4,12},{8,16},{12,20},{16,24},{20,28},{24,32},{28,36},{32,40... | collective-permute-start | bytes 1572872 | tf_op jit(solution)/shard_map/ppermute | solution.py:455
  29.2 14.1 %copy-start.12 = (bf16[512,512]{1,0:T(8,128)(2,1)}, bf16[512,512]{1,0:T(8,128)(2,1)S(1)}, u32[]{:S(2)}) copy-start(bf16[512,512]{1,0:T(8,128)(2,1)S(1)} %collective-permute-done.near_ref) | copy-start | bytes 1572868
  40.2 0.8 copy-start.13
  41.0 1.0 copy-start.3
  43.4 27.1 %copy-start.2 = (f32[4,264,128]{2,1,0:T(8,128)S(1)}, f32[4,264,128]{2,1,0:T(8,128)}, u32[]{:S(2)}) copy-start(f32[4,264,128]{2,1,0:T(8,128)} %get-tuple-element.31.early_ref) | copy-start | bytes 1622020
  57.5 13.9 %copy-start.1 = (f32[512,512]{1,0:T(8,128)S(1)}, f32[512,512]{1,0:T(8,128)}, u32[]{:S(2)}) copy-start(f32[512,512]{1,0:T(8,128)} %get-tuple-element.27.local_ref) | copy-start | bytes 3145732
  60.0 11.4 %copy-start.5 = (bf16[512,512]{1,0:T(8,128)(2,1)S(1)}, bf16[512,512]{1,0:T(8,128)(2,1)}, u32[]{:S(2)}) copy-start(bf16[512,512]{1,0:T(8,128)(2,1)} %get-tuple-element.26.reach_ref) | copy-start | bytes 1572868
  71.4 0.9 copy-start.7
  72.3 6.3 %copy-start.16 = (bf16[4,128,128]{2,1,0:T(8,128)(2,1)S(1)}, bf16[4,128,128]{2,1,0:T(8,128)(2,1)}, u32[]{:S(2)}) copy-start(bf16[4,128,128]{2,1,0:T(8,128)(2,1)} %get-tuple-element.35) | copy-start | bytes 393220
  72.3 7.6 %copy-start.4 = (bf16[512,512]{1,0:T(8,128)(2,1)S(1)}, bf16[512,512]{1,0:T(8,128)(2,1)}, u32[]{:S(2)}) copy-start(bf16[512,512]{1,0:T(8,128)(2,1)} %get-tuple-element.33.reach_ref) | copy-start | bytes 1572868
  73.4 6.5 %copy-start = (f32[512,512]{1,0:T(8,128)S(1)}, f32[512,512]{1,0:T(8,128)}, u32[]{:S(2)}) copy-start(f32[512,512]{1,0:T(8,128)} %get-tuple-element.34.local_ref) | copy-start | bytes 3145732
  73.4 14.3 %all-to-all-start.2 = ((bf16[4,128,512]{2,1,0:T(8,128)(2,1)}), bf16[4,128,512]{2,1,0:T(8,128)(2,1)S(1)}, u32[]{:S(2)}, u32[]{:S(2)}) async-start(bf16[4,128,512]{2,1,0:T(8,128)(2,1)} %bitcast.27), calls=%async_computation.2 | async-start | bytes 1048576 | tf_op jit(solution)/shard_map/all_to_all | solution.py:464
  78.6 1.3 %collective-permute-start.6 = (bf16[4,128,128]{2,1,0:T(8,128)(2,1)S(1)}, bf16[4,128,128]{2,1,0:T(8,128)(2,1)S(1)}, u32[]{:S(2)}, u32[]{:S(2)}) collective-permute-start(bf16[4,128,128]{2,1,0:T(8,128)(2,1)S(1)} %copy-done.16), channel_id=1, source_target_pairs={{0,4},{4,0},{1,5},{5,1},{2,6},{6,2},{3,7},{7,3},{8,12},{12,8},{9,1... | collective-permute-start | bytes 393224 | tf_op jit(solution)/shard_map/ppermute | solution.py:516
  81.0 10.2 %copy-start.9 = (bf16[512,8,128]{2,1,0:T(8,128)(2,1)S(1)}, bf16[512,8,128]{2,1,0:T(8,128)(2,1)}, u32[]{:S(2)}) copy-start(bf16[512,8,128]{2,1,0:T(8,128)(2,1)} %param.8) | copy-start | bytes 3145732
  87.7 34.5 %all-to-all-start.3 = ((bf16[4,128,512]{2,1,0:T(8,128)(2,1)}), bf16[4,128,512]{2,1,0:T(8,128)(2,1)S(1)}, u32[]{:S(2)}, u32[]{:S(2)}) async-start(bf16[4,128,512]{2,1,0:T(8,128)(2,1)} %bitcast.26), calls=%async_computation.3 | async-start | bytes 1048576 | tf_op jit(solution)/shard_map/all_to_all | solution.py:464
  104.5 9.2 %collective-permute-start.2 = (bf16[128,1024]{1,0:T(8,128)(2,1)}, bf16[128,1024]{1,0:T(8,128)(2,1)S(1)}, u32[]{:S(2)}, u32[]{:S(2)}) collective-permute-start(bf16[128,1024]{1,0:T(8,128)(2,1)} %get-tuple-element.23), channel_id=1, source_target_pairs={{0,1},{1,2},{2,3},{3,0},{4,5},{5,6},{6,7},{7,4},{8,9},{9,10},{10,1... | collective-permute-start | bytes 786440 | tf_op jit(solution)/shard_map/ppermute | solution.py:455
  105.9 14.3 %collective-permute-start.3 = (bf16[128,1024]{1,0:T(8,128)(2,1)}, bf16[128,1024]{1,0:T(8,128)(2,1)S(1)}, u32[]{:S(2)}, u32[]{:S(2)}) collective-permute-start(bf16[128,1024]{1,0:T(8,128)(2,1)} %get-tuple-element.24), channel_id=1, source_target_pairs={{0,2},{1,3},{2,0},{3,1},{4,6},{5,7},{6,4},{7,5},{8,10},{9,11},{10,... | collective-permute-start | bytes 786440 | tf_op jit(solution)/shard_map/ppermute | solution.py:455
  108.3 11.9 %collective-permute-start.4 = (bf16[128,1024]{1,0:T(8,128)(2,1)}, bf16[128,1024]{1,0:T(8,128)(2,1)S(1)}, u32[]{:S(2)}, u32[]{:S(2)}) collective-permute-start(bf16[128,1024]{1,0:T(8,128)(2,1)} %get-tuple-element.25), channel_id=1, source_target_pairs={{0,3},{1,0},{2,1},{3,2},{4,7},{5,4},{6,5},{7,6},{8,11},{9,8},{10,9... | collective-permute-start | bytes 786440 | tf_op jit(solution)/shard_map/ppermute | solution.py:455
  120.2 1.0 copy-start.6

commit v5 on v4

--- a/solution.py
+++ b/solution.py
@@ -1,3 +1,4 @@
+import functools
 import math
 
 import jax
@@ -295,7 +296,7 @@
         ).astype(bf16)
 
 
-def attend_body(first_ref, turn_ref, query_ref, own_ref, near_ref, far_ref, *rest):
+def attend_body(turns, first_ref, rank_ref, query_ref, own_ref, near_ref, far_ref, *rest):
     *out_refs, kv_ref = rest
     tokens = own_ref.shape[0]
     block = query_ref.shape[0]
@@ -312,7 +313,8 @@
             kv_ref[kv, tokens : 2 * tokens, :] = near_ref[:, lanes]
             kv_ref[kv, 2 * tokens :, :] = own_ref[:, lanes]
 
-    begin = pl.multiple_of(((step + turn_ref[0]) % (tokens // block)) * block, block)
+    place = (pick(turns, step) + rank_ref[0]) % (tokens // block)
+    begin = pl.multiple_of(place * block, block)
     row = lax.broadcasted_iota(jnp.int32, (block, block), 0)
     col = lax.broadcasted_iota(jnp.int32, (block, block), 1)
     scale = math.log2(math.e) / math.sqrt(HEAD)
@@ -373,29 +375,38 @@
         run(False)
 
 
-def attend(first, turn, count, query, own, near, far):
+def pick(values, step):
+    chosen = values[0]
+    for n, value in enumerate(values[1:], 1):
+        chosen = jnp.where(step == n, value, chosen)
+    return chosen
+
+
+def attend(turns, first, rank, count, query, own, near, far):
     tokens, width = query.shape
     block = tokens // count
     groups = own.shape[1] // (2 * HEAD)
     lanes = width // groups
     return pl.pallas_call(
-        attend_body,
+        functools.partial(attend_body, turns),
         grid_spec=pltpu.PrefetchScalarGridSpec(
             num_scalar_prefetch=2,
-            grid=(count, groups),
+            grid=(len(turns), groups),
             in_specs=[
-                pl.BlockSpec((block, lanes), lambda i, g, _, t: ((i + t[0]) % count, g)),
+                pl.BlockSpec(
+                    (block, lanes), lambda i, g, _, t: ((pick(turns, i) + t[0]) % count, g)
+                ),
                 ONCHIP,
                 ONCHIP,
                 ONCHIP,
             ],
-            out_specs=[ONCHIP] * count,
+            out_specs=[ONCHIP] * len(turns),
             scratch_shapes=[pltpu.VMEM((2 * groups, WINDOW + tokens, HEAD), bf16)],
         ),
-        out_shape=[jax.ShapeDtypeStruct((block, width), bf16)] * count,
+        out_shape=[jax.ShapeDtypeStruct((block, width), bf16)] * len(turns),
         name="attend",
         compiler_params=pltpu.CompilerParams(dimension_semantics=("arbitrary", "arbitrary")),
-    )(first, turn, query, own, near, far)
+    )(first, rank, query, own, near, far)
 
 
 def join_turns_body(rank_ref, *refs):
@@ -500,10 +511,12 @@
     count = lax.axis_size("head")
     rank = lax.axis_index("head").astype(jnp.int32).reshape(1)
     turn = tokens // count
-    attended = attend(first, rank, count, rows(attn_query), key_value, near, far)
-    attn = [attended[0]]
-    for d in range(1, count):
-        attn.append(ring(attended[d], "head", d, count))
+    queries = rows(attn_query)
+    ahead = attend((2, 1, 3), first, rank, count, queries, key_value, near, far)
+    attn = [None] * count
+    for block, d in zip(ahead, (2, 1, 3)):
+        attn[d] = ring(block, "head", d, count)
+    (attn[0],) = attend((0,), first, rank, count, queries, key_value, near, far)
     (starts,) = onchip_call(relay_body, [shape((half * 4, HEAD // 4, HEAD), bf16)], [], gathered)
     returned = exchange(starts, CHIPS)
     keep, send = onchip_call(

time: 124 us -> 122 us (0.984)
  waiting for transfers between devices: 30.2 us -> 25.5 us
  Pallas kernels: 39 us -> 41.3 us
    ppermute x5, waiting for transfers between devices: 22.2 us -> 17.5 us  [ring(): lax.ppermute(block, axes, [(i, (i + distance) % size) for i in range(size)])]
    pallas_call x1 -> x2, Pallas kernels: 12.1 us -> 14.3 us  [attend(): pl.pallas_call(functools.partial(attend_body, turns), grid_spec=pltpu.Pre...]
  transfers between devices with their start and end apart: 9 -> 9, of which waited for: 6 -> 5; matrix products, arithmetic and copies ran while one was open for 2% -> 2% of each run, Pallas kernels for 19% -> 21%
where the time goes in v5:
time: 122 us; the launch traced here: 121 us
  Pallas kernels  41.3 us (34%)
  waiting for transfers between devices  25.5 us (21%)
  blocking collectives  24.5 us (20%)
  starting transfers between devices  17.5 us (14%)
  local copies, waits for them, and re-layouts  10.5 us (9%)
    all_to_all x2, blocking collectives, exchange(): return lax.all_to_all(block, axes, split_axis=0, concat_axis=0, tiled=True)  24.5 us
    pallas_call x2, Pallas kernels, delta_local(): pl.pallas_call(delta_body, grid_spec=pltpu.PrefetchScalarGridSpec(num_sca...  17.9 us
    ppermute x5, waiting for transfers between devices, ring(): lax.ppermute(block, axes, [(i, (i + distance) % size) for i in range(size)])  17.5 us
    pallas_call x2, Pallas kernels, attend(): pl.pallas_call(functools.partial(attend_body, turns), grid_spec=pltpu.Pre...  14.3 us
    all_to_all x2, starting transfers between devices, exchange(): return lax.all_to_all(block, axes, split_axis=0, concat_axis=0, tiled=True)  8.63 us
    unnamed x36, local copies, waits for them, and re-layouts  7.61 us
    ppermute x5, starting transfers between devices, ring(): lax.ppermute(block, axes, [(i, (i + distance) % size) for i in range(size)])  7.48 us
    pallas_call x5, Pallas kernels, onchip_call(): pl.pallas_call(body, in_specs=[SCALAR] * len(scalars) + [ONCHIP] * len(op...  6.98 us
  transfers between devices with their start and end apart: 9, of which 5 were waited for; matrix products, arithmetic and copies ran while one was open for 2% of the time, Pallas kernels for 21%

profile of v5, /device:TPU:1, one launch (start us, length us, event | category | flops | bytes accessed | tf_op | source)
XLA Modules:
  0.0 121.0 jit_solution(5067715054030760430)
XLA Ops:
  0.6 0.0 copy-start.12
  0.6 0.0 copy-start.13
  0.7 2.6 %copy.19 = bf16[64,8,8,128]{3,1,2,0:T(8,128)(2,1)} copy(bf16[64,8,8,128]{3,2,1,0:T(8,128)(2,1)} %bitcast.29) | data formatting | bytes 2097152
  3.3 0.0 copy-done.12
  3.3 0.0 copy-done.13
  3.3 1.8 %copy_bitcast_fusion = (bf16[512,1024]{1,0:T(8,128)(2,1)}, bf16[512,1024]{1,0:T(8,128)(2,1)}) fusion(bf16[64,8,8,128]{3,2,1,0:T(8,128)(2,1)S(1)} %bitcast.31, bf16[64,8,8,128]{3,2,1,0:T(8,128)(2,1)S(1)} %bitcast.32), kind=kLoop, calls=%fused_computation | loop fusion | bytes 4194304 | tf_op jit(solution)/shard_map/reshape | solution.py:490
  5.1 0.0 copy-start.14
  5.1 0.0 copy-start.15
  5.1 9.0 %delta_local.3 = (f32[512,512]{1,0:T(8,128)}, bf16[512,512]{1,0:T(8,128)(2,1)}, f32[4,264,128]{2,1,0:T(8,128)}) custom-call(s32[1]{0:T(128)S(6)} %sub.7.base_ref, bf16[512,1024]{1,0:T(8,128)(2,1)} %bitcast.25, bf16[512,1024]{1,0:T(8,128)(2,1)} %get-tuple-element.35.k_ref, bf16[512,1024]{1,0:T(8,128)(2,1)} %get-tuple-element.34.v_ref, f32[8,512]{1,0:T(8,128)} %log_ref.3, ...), custom_call_target="tpu_custom_call" | custom-call | tf_op jit(solution)/shard_map/delta_local/pallas_call | solution.py:213
  14.1 1.4 %collective-permute-start.5 = (f32[4,264,128]{2,1,0:T(8,128)}, f32[4,264,128]{2,1,0:T(8,128)S(1)}, u32[]{:S(2)}, u32[]{:S(2)}) collective-permute-start(f32[4,264,128]{2,1,0:T(8,128)} %get-tuple-element.27), channel_id=1, source_target_pairs={{0,4},{4,0},{1,5},{5,1},{2,6},{6,2},{3,7},{7,3},{8,12},{12,8},{9,1... | collective-permute-start | bytes 1622024 | tf_op jit(solution)/shard_map/ppermute | solution.py:495
  15.5 0.0 copy-done.14
  15.5 0.0 copy-done.15
  15.5 0.7 pad_maximum_fusion
  16.3 0.8 copy.10
  17.1 0.2 reshape.40.own_ref
  17.3 0.0 copy-start.8
  17.3 1.3 %collective-permute-start = (bf16[512,512]{1,0:T(8,128)(2,1)S(1)}, bf16[512,512]{1,0:T(8,128)(2,1)S(1)}, u32[]{:S(2)}, u32[]{:S(2)}) collective-permute-start(bf16[512,512]{1,0:T(8,128)(2,1)S(1)} %reshape.40.own_ref), channel_id=1, source_target_pairs={{0,4},{4,8},{8,12},{12,16},{16,20},{20,24},{24,28},{28,32},{32,36}... | collective-permute-start | bytes 1572872 | tf_op jit(solution)/shard_map/ppermute | solution.py:466
  18.6 1.2 %collective-permute-start.1 = (bf16[512,512]{1,0:T(8,128)(2,1)S(1)}, bf16[512,512]{1,0:T(8,128)(2,1)S(1)}, u32[]{:S(2)}, u32[]{:S(2)}) collective-permute-start(bf16[512,512]{1,0:T(8,128)(2,1)S(1)} %reshape.40.own_ref), channel_id=1, source_target_pairs={{0,8},{4,12},{8,16},{12,20},{16,24},{20,28},{24,32},{28,36},{32,40... | collective-permute-start | bytes 1572872 | tf_op jit(solution)/shard_map/ppermute | solution.py:466
  19.8 8.9 %delta_local.2 = (f32[512,512]{1,0:T(8,128)}, bf16[512,512]{1,0:T(8,128)(2,1)}, f32[4,264,128]{2,1,0:T(8,128)}) custom-call(s32[1]{0:T(128)} %bitcast.4.base_ref.core_ref, bf16[512,1024]{1,0:T(8,128)(2,1)} %bitcast.26, bf16[512,1024]{1,0:T(8,128)(2,1)} %get-tuple-element.35.k_ref, bf16[512,1024]{1,0:T(8,128)(2,1)} %get-tuple-element.34.v_ref, ...), custom_call_target="tpu_custom_call" | custom-call | tf_op jit(solution)/shard_map/delta_local/pallas_call | solution.py:213
  28.7 0.0 copy-done.8
  28.7 0.5 collective-permute-done.near_ref
  29.2 0.0 copy-start.9
  29.2 11.0 %collective-permute-done.1.far_ref = bf16[512,512]{1,0:T(8,128)(2,1)S(1)} collective-permute-done((bf16[512,512]{1,0:T(8,128)(2,1)S(1)}, bf16[512,512]{1,0:T(8,128)(2,1)S(1)}, u32[]{:S(2)}, u32[]{:S(2)}) %collective-permute-start.1) | collective-permute-done | bytes 524320 | tf_op jit(solution)/shard_map/ppermute | solution.py:466
  40.2 0.0 copy-start.10
  40.2 0.8 copy-done.10
  41.0 0.0 collective-permute-done.5.other_ref
  41.0 0.0 copy-start.4
  41.0 1.0 copy-done.4
  42.0 1.3 %shard_map.96 = (bf16[16,176,128]{2,1,0:T(8,128)(2,1)}, f32[4,264,128]{2,1,0:T(8,128)}) custom-call(s32[1]{0:T(128)} %bitcast.4.base_ref.core_ref, f32[4,264,128]{2,1,0:T(8,128)S(1)} %copy-done.4, f32[4,264,128]{2,1,0:T(8,128)S(1)} %collective-permute-done.5.other_ref), custom_call_target="tpu_custom_call" | custom-call | tf_op jit(solution)/shard_map/pallas_call | solution.py:457
  43.4 0.0 copy-done.9
  43.4 0.0 copy-start.3
  43.4 14.1 %all_to_all.20.message_ref = bf16[16,176,128]{2,1,0:T(8,128)(2,1)S(1)} all-to-all(bf16[16,176,128]{2,1,0:T(8,128)(2,1)} %get-tuple-element.28), channel_id=1, replica_groups=mesh['y'=4,'x'=4,'core'=2,'head'=4] {'y','x'}, dimensions={0} | all-to-all | bytes 1441792 | tf_op jit(solution)/shard_map/all_to_all | solution.py:475
  57.5 0.0 copy-start.1
  57.5 2.5 %shard_map.97 = bf16[16,32,128]{2,1,0:T(8,128)(2,1)} custom-call(bf16[16,176,128]{2,1,0:T(8,128)(2,1)S(1)} %all_to_all.20.message_ref), custom_call_target="tpu_custom_call" | custom-call | tf_op jit(solution)/shard_map/pallas_call | solution.py:457
  60.0 10.4 %all_to_all.21 = bf16[16,32,128]{2,1,0:T(8,128)(2,1)S(1)} all-to-all(bf16[16,32,128]{2,1,0:T(8,128)(2,1)} %shard_map.97), channel_id=1, replica_groups=mesh['y'=4,'x'=4,'core'=2,'head'=4] {'y','x'}, dimensions={0} | all-to-all | bytes 262144 | tf_op jit(solution)/shard_map/all_to_all | solution.py:475
  70.4 0.0 copy-done.3
  70.4 1.0 shard_map.98
  71.4 0.0 copy-done.1
  71.4 0.0 copy-done.6
  71.4 0.9 copy-done.7
  72.3 1.1 shard_map.99
  73.4 5.2 %all-to-all-start.2 = ((bf16[4,128,512]{2,1,0:T(8,128)(2,1)}), bf16[4,128,512]{2,1,0:T(8,128)(2,1)S(1)}, u32[]{:S(2)}, u32[]{:S(2)}) async-start(bf16[4,128,512]{2,1,0:T(8,128)(2,1)} %bitcast.28), calls=%async_computation.2 | async-start | bytes 1048576 | tf_op jit(solution)/shard_map/all_to_all | solution.py:475
  78.6 0.0 copy-done.16
  78.6 0.0 collective-permute-start.6
  78.6 1.3 %collective-permute-done.6.state_ref = bf16[4,128,128]{2,1,0:T(8,128)(2,1)S(1)} collective-permute-done((bf16[4,128,128]{2,1,0:T(8,128)(2,1)S(1)}, bf16[4,128,128]{2,1,0:T(8,128)(2,1)S(1)}, u32[]{:S(2)}, u32[]{:S(2)}) %collective-permute-start.6) | collective-permute-done | bytes 131104 | tf_op jit(solution)/shard_map/ppermute | solution.py:529
  79.9 0.0 copy-done.5
  79.9 0.0 copy-done
  79.9 1.1 shard_map.100
  81.0 6.7 %all-to-all-done.2.left_ref = bf16[4,128,512]{2,1,0:T(8,128)(2,1)S(1)} async-done(((bf16[4,128,512]{2,1,0:T(8,128)(2,1)}), bf16[4,128,512]{2,1,0:T(8,128)(2,1)S(1)}, u32[]{:S(2)}, u32[]{:S(2)}) %all-to-all-start.2) | async-done | bytes 524320 | tf_op jit(solution)/shard_map/all_to_all | solution.py:475
  87.7 3.5 %all-to-all-start.3 = ((bf16[4,128,512]{2,1,0:T(8,128)(2,1)}), bf16[4,128,512]{2,1,0:T(8,128)(2,1)S(1)}, u32[]{:S(2)}, u32[]{:S(2)}) async-start(bf16[4,128,512]{2,1,0:T(8,128)(2,1)} %bitcast.27), calls=%async_computation.3 | async-start | bytes 1048576 | tf_op jit(solution)/shard_map/all_to_all | solution.py:475
  91.2 0.0 copy-done.11
  91.2 1.2 %copy.20 = bf16[64,8,8,128]{3,1,2,0:T(8,128)(2,1)} copy(bf16[64,8,8,128]{3,2,1,0:T(8,128)(2,1)S(1)} %bitcast.30) | data formatting | bytes 2097152
  92.5 9.7 %attend.3 = (bf16[128,1024]{1,0:T(8,128)(2,1)}, bf16[128,1024]{1,0:T(8,128)(2,1)}, bf16[128,1024]{1,0:T(8,128)(2,1)}) custom-call(s32[1]{0:T(128)} %bitcast.1.first_ref, s32[1]{0:T(128)} %bitcast.rank_ref, bf16[512,1024]{1,0:T(8,128)(2,1)} %bitcast.23, bf16[512,512]{1,0:T(8,128)(2,1)} %copy-done.8, bf16[512,512]{1,0:T(8,128)(2,1)} %copy-done.9, ...), custom_call_target="tpu_custom_call" | custom-call | tf_op jit(solution)/shard_map/attend/pallas_call | solution.py:390
  102.1 1.4 %collective-permute-start.2 = (bf16[128,1024]{1,0:T(8,128)(2,1)}, bf16[128,1024]{1,0:T(8,128)(2,1)S(1)}, u32[]{:S(2)}, u32[]{:S(2)}) collective-permute-start(bf16[128,1024]{1,0:T(8,128)(2,1)} %get-tuple-element.21), channel_id=1, source_target_pairs={{0,1},{1,2},{2,3},{3,0},{4,5},{5,6},{6,7},{7,4},{8,9},{9,10},{10,1... | collective-permute-start | bytes 786440 | tf_op jit(solution)/shard_map/ppermute | solution.py:466
  103.5 2.4 %collective-permute-start.3 = (bf16[128,1024]{1,0:T(8,128)(2,1)}, bf16[128,1024]{1,0:T(8,128)(2,1)S(1)}, u32[]{:S(2)}, u32[]{:S(2)}) collective-permute-start(bf16[128,1024]{1,0:T(8,128)(2,1)} %get-tuple-element.22), channel_id=1, source_target_pairs={{0,2},{1,3},{2,0},{3,1},{4,6},{5,7},{6,4},{7,5},{8,10},{9,11},{10,... | collective-permute-start | bytes 786440 | tf_op jit(solution)/shard_map/ppermute | solution.py:466
  105.9 1.2 collective-permute-start.4
  107.1 4.7 %attend.2.refs_0_ = bf16[128,1024]{1,0:T(8,128)(2,1)} custom-call(s32[1]{0:T(128)} %bitcast.1.first_ref, s32[1]{0:T(128)} %bitcast.rank_ref, bf16[512,1024]{1,0:T(8,128)(2,1)} %bitcast.24, bf16[512,512]{1,0:T(8,128)(2,1)} %copy-done.8, bf16[512,512]{1,0:T(8,128)(2,1)} %copy-done.9, bf16[512,512]{1,0:T(8,128)(2,1)} %copy-done.10), custom_call_target="tpu_custom_call" | custom-call | tf_op jit(solution)/shard_map/attend/pallas_call | solution.py:390
  111.8 0.0 collective-permute-done.2.refs_1_
  111.8 6.0 %collective-permute-done.3.refs_2_ = bf16[128,1024]{1,0:T(8,128)(2,1)S(1)} collective-permute-done((bf16[128,1024]{1,0:T(8,128)(2,1)}, bf16[128,1024]{1,0:T(8,128)(2,1)S(1)}, u32[]{:S(2)}, u32[]{:S(2)}) %collective-permute-start.3) | collective-permute-done | bytes 262176 | tf_op jit(solution)/shard_map/ppermute | solution.py:466
  117.8 0.0 collective-permute-done.4.refs_3_
  117.8 0.9 copy-done.2
  118.7 1.0 shard_map.95
  119.7 0.0 all-to-all-done.3.right_ref
  119.7 1.0 shard_map.101
  (7 shorter events, 0.0 us)
Async XLA Ops:
  0.6 2.6 %copy-start.12 = (bf16[512,8,128]{2,1,0:T(8,128)(2,1)S(1)}, bf16[512,8,128]{2,1,0:T(8,128)(2,1)}, u32[]{:S(2)}) copy-start(bf16[512,8,128]{2,1,0:T(8,128)(2,1)} %param.13) | copy-start | bytes 3145732
  0.6 2.6 %copy-start.13 = (bf16[512,8,128]{2,1,0:T(8,128)(2,1)S(1)}, bf16[512,8,128]{2,1,0:T(8,128)(2,1)}, u32[]{:S(2)}) copy-start(bf16[512,8,128]{2,1,0:T(8,128)(2,1)} %param.12) | copy-start | bytes 3145732
  5.1 10.4 %copy-start.14 = (bf16[512,2,128]{2,1,0:T(2,128)(2,1)S(1)}, bf16[512,2,128]{2,1,0:T(2,128)(2,1)}, u32[]{:S(2)}) copy-start(bf16[512,2,128]{2,1,0:T(2,128)(2,1)} %param.10) | copy-start | bytes 786436
  5.1 10.4 %copy-start.15 = (bf16[512,2,128]{2,1,0:T(2,128)(2,1)S(1)}, bf16[512,2,128]{2,1,0:T(2,128)(2,1)}, u32[]{:S(2)}) copy-start(bf16[512,2,128]{2,1,0:T(2,128)(2,1)} %param.9) | copy-start | bytes 786436
  14.1 26.9 %collective-permute-start.5 = (f32[4,264,128]{2,1,0:T(8,128)}, f32[4,264,128]{2,1,0:T(8,128)S(1)}, u32[]{:S(2)}, u32[]{:S(2)}) collective-permute-start(f32[4,264,128]{2,1,0:T(8,128)} %get-tuple-element.27), channel_id=1, source_target_pairs={{0,4},{4,0},{1,5},{5,1},{2,6},{6,2},{3,7},{7,3},{8,12},{12,8},{9,1... | collective-permute-start | bytes 1622024 | tf_op jit(solution)/shard_map/ppermute | solution.py:495
  17.3 11.5 %copy-start.8 = (bf16[512,512]{1,0:T(8,128)(2,1)}, bf16[512,512]{1,0:T(8,128)(2,1)S(1)}, u32[]{:S(2)}) copy-start(bf16[512,512]{1,0:T(8,128)(2,1)S(1)} %reshape.40.own_ref) | copy-start | bytes 1572868
  17.3 12.0 %collective-permute-start = (bf16[512,512]{1,0:T(8,128)(2,1)S(1)}, bf16[512,512]{1,0:T(8,128)(2,1)S(1)}, u32[]{:S(2)}, u32[]{:S(2)}) collective-permute-start(bf16[512,512]{1,0:T(8,128)(2,1)S(1)} %reshape.40.own_ref), channel_id=1, source_target_pairs={{0,4},{4,8},{8,12},{12,16},{16,20},{20,24},{24,28},{28,32},{32,36}... | collective-permute-start | bytes 1572872 | tf_op jit(solution)/shard_map/ppermute | solution.py:466
  18.6 21.6 %collective-permute-start.1 = (bf16[512,512]{1,0:T(8,128)(2,1)S(1)}, bf16[512,512]{1,0:T(8,128)(2,1)S(1)}, u32[]{:S(2)}, u32[]{:S(2)}) collective-permute-start(bf16[512,512]{1,0:T(8,128)(2,1)S(1)} %reshape.40.own_ref), channel_id=1, source_target_pairs={{0,8},{4,12},{8,16},{12,20},{16,24},{20,28},{24,32},{28,36},{32,40... | collective-permute-start | bytes 1572872 | tf_op jit(solution)/shard_map/ppermute | solution.py:466
  29.2 14.1 %copy-start.9 = (bf16[512,512]{1,0:T(8,128)(2,1)}, bf16[512,512]{1,0:T(8,128)(2,1)S(1)}, u32[]{:S(2)}) copy-start(bf16[512,512]{1,0:T(8,128)(2,1)S(1)} %collective-permute-done.near_ref) | copy-start | bytes 1572868
  40.2 0.8 copy-start.10
  41.0 1.0 copy-start.4
  43.4 27.1 %copy-start.3 = (f32[4,264,128]{2,1,0:T(8,128)S(1)}, f32[4,264,128]{2,1,0:T(8,128)}, u32[]{:S(2)}) copy-start(f32[4,264,128]{2,1,0:T(8,128)} %get-tuple-element.29.early_ref) | copy-start | bytes 1622020
  57.5 13.9 %copy-start.1 = (f32[512,512]{1,0:T(8,128)S(1)}, f32[512,512]{1,0:T(8,128)}, u32[]{:S(2)}) copy-start(f32[512,512]{1,0:T(8,128)} %get-tuple-element.25.local_ref) | copy-start | bytes 3145732
  60.0 11.4 %copy-start.6 = (bf16[512,512]{1,0:T(8,128)(2,1)S(1)}, bf16[512,512]{1,0:T(8,128)(2,1)}, u32[]{:S(2)}) copy-start(bf16[512,512]{1,0:T(8,128)(2,1)} %get-tuple-element.24.reach_ref) | copy-start | bytes 1572868
  71.4 0.9 copy-start.7
  72.3 6.3 %copy-start.16 = (bf16[4,128,128]{2,1,0:T(8,128)(2,1)S(1)}, bf16[4,128,128]{2,1,0:T(8,128)(2,1)}, u32[]{:S(2)}) copy-start(bf16[4,128,128]{2,1,0:T(8,128)(2,1)} %get-tuple-element.33) | copy-start | bytes 393220
  72.3 7.6 %copy-start.5 = (bf16[512,512]{1,0:T(8,128)(2,1)S(1)}, bf16[512,512]{1,0:T(8,128)(2,1)}, u32[]{:S(2)}) copy-start(bf16[512,512]{1,0:T(8,128)(2,1)} %get-tuple-element.31.reach_ref) | copy-start | bytes 1572868
  73.4 6.5 %copy-start = (f32[512,512]{1,0:T(8,128)S(1)}, f32[512,512]{1,0:T(8,128)}, u32[]{:S(2)}) copy-start(f32[512,512]{1,0:T(8,128)} %get-tuple-element.32.local_ref) | copy-start | bytes 3145732
  73.4 14.3 %all-to-all-start.2 = ((bf16[4,128,512]{2,1,0:T(8,128)(2,1)}), bf16[4,128,512]{2,1,0:T(8,128)(2,1)S(1)}, u32[]{:S(2)}, u32[]{:S(2)}) async-start(bf16[4,128,512]{2,1,0:T(8,128)(2,1)} %bitcast.28), calls=%async_computation.2 | async-start | bytes 1048576 | tf_op jit(solution)/shard_map/all_to_all | solution.py:475
  78.6 1.3 %collective-permute-start.6 = (bf16[4,128,128]{2,1,0:T(8,128)(2,1)S(1)}, bf16[4,128,128]{2,1,0:T(8,128)(2,1)S(1)}, u32[]{:S(2)}, u32[]{:S(2)}) collective-permute-start(bf16[4,128,128]{2,1,0:T(8,128)(2,1)S(1)} %copy-done.16), channel_id=1, source_target_pairs={{0,4},{4,0},{1,5},{5,1},{2,6},{6,2},{3,7},{7,3},{8,12},{12,8},{9,1... | collective-permute-start | bytes 393224 | tf_op jit(solution)/shard_map/ppermute | solution.py:529
  81.0 10.2 %copy-start.11 = (bf16[512,8,128]{2,1,0:T(8,128)(2,1)S(1)}, bf16[512,8,128]{2,1,0:T(8,128)(2,1)}, u32[]{:S(2)}) copy-start(bf16[512,8,128]{2,1,0:T(8,128)(2,1)} %param.8) | copy-start | bytes 3145732
  87.7 32.0 %all-to-all-start.3 = ((bf16[4,128,512]{2,1,0:T(8,128)(2,1)}), bf16[4,128,512]{2,1,0:T(8,128)(2,1)S(1)}, u32[]{:S(2)}, u32[]{:S(2)}) async-start(bf16[4,128,512]{2,1,0:T(8,128)(2,1)} %bitcast.27), calls=%async_computation.3 | async-start | bytes 1048576 | tf_op jit(solution)/shard_map/all_to_all | solution.py:475
  102.1 9.7 %collective-permute-start.2 = (bf16[128,1024]{1,0:T(8,128)(2,1)}, bf16[128,1024]{1,0:T(8,128)(2,1)S(1)}, u32[]{:S(2)}, u32[]{:S(2)}) collective-permute-start(bf16[128,1024]{1,0:T(8,128)(2,1)} %get-tuple-element.21), channel_id=1, source_target_pairs={{0,1},{1,2},{2,3},{3,0},{4,5},{5,6},{6,7},{7,4},{8,9},{9,10},{10,1... | collective-permute-start | bytes 786440 | tf_op jit(solution)/shard_map/ppermute | solution.py:466
  103.5 14.3 %collective-permute-start.3 = (bf16[128,1024]{1,0:T(8,128)(2,1)}, bf16[128,1024]{1,0:T(8,128)(2,1)S(1)}, u32[]{:S(2)}, u32[]{:S(2)}) collective-permute-start(bf16[128,1024]{1,0:T(8,128)(2,1)} %get-tuple-element.22), channel_id=1, source_target_pairs={{0,2},{1,3},{2,0},{3,1},{4,6},{5,7},{6,4},{7,5},{8,10},{9,11},{10,... | collective-permute-start | bytes 786440 | tf_op jit(solution)/shard_map/ppermute | solution.py:466
  105.9 11.9 %collective-permute-start.4 = (bf16[128,1024]{1,0:T(8,128)(2,1)}, bf16[128,1024]{1,0:T(8,128)(2,1)S(1)}, u32[]{:S(2)}, u32[]{:S(2)}) collective-permute-start(bf16[128,1024]{1,0:T(8,128)(2,1)} %get-tuple-element.23), channel_id=1, source_target_pairs={{0,3},{1,0},{2,1},{3,2},{4,7},{5,4},{6,5},{7,6},{8,11},{9,8},{10,9... | collective-permute-start | bytes 786440 | tf_op jit(solution)/shard_map/ppermute | solution.py:466
  117.8 1.0 copy-start.2
